TPU v7x, 32 devices: a whole 2x2x4 slice. The times are simulated.
32 devices in a mesh: space: 8 (over z, y), orb: 4 (over x, core).
Axes of the slice: x: 2, y: 2, z: 4, core: 2. Of those that a mesh axis runs over, the one named last changes fastest.
Arguments:
- orbitals: float32 [8, 8192, 256], P('orb', 'space'), may hold values from -6 to 6
- near_source: int32 [8192, 27], P('space'), may hold values from 0 to 8191, as said below
- far_leaf: int32 [8192, 108], P('space'), may hold values from 0 to 8191, as said below
- far_mid: int32 [1024, 108], P('space'), may hold values from 0 to 1023, as said below
- far_top: int32 [128, 108], P('space'), may hold values from 0 to 127, as said below
- leaf_basis: bfloat16 [64, 256], replicated, may hold values from -0.375 to 0.375
- near_table: bfloat16 [27, 256, 256], replicated, may hold values from -0.078125 to 0.078125
- transfer: bfloat16 [8, 64, 64], replicated, may hold values from -0.75 to 0.75
- coupling: bfloat16 [108, 64, 64], replicated, may hold values from -0.078125 to 0.078125
- pair_transfer: bfloat16 [2, 64, 64], replicated, may hold values from -0.75 to 0.75
- coarse_coupling: bfloat16 [4, 64, 64], replicated, may hold values from -0.4375 to 0.4375
Outputs:
- relaxed: float32 [8, 8192, 256], P('orb', 'space')
Inputs may be any that keep to these rules, and one draw needn't show every extreme that they name: `near_source`: with layer(t) = t // 64: every entry of leaf t lies in a layer at most 1 from layer(t); entry 13 is t itself; entry 0 is the leaf at t's transverse position one layer away. `far_leaf`: with layer(t) = t // 64: every entry of box t lies in a layer 2 or 3 away from layer(t); entry 0 is exactly 3 layers away. `far_mid`: with layer(t) = t // 16: every entry of box t lies in a layer 2 or 3 away from layer(t); entry 0 is exactly 3 layers away. `far_top`: with layer(t) = t // 4: every entry of box t lies in a layer 2 or 3 away from layer(t); entry 0 is exactly 3 layers away.
All inputs are finite; a program needn't handle non-finite values.
Results may differ from a plain program's by a relative error of at most 0.012.
Values may be sent and summed in bfloat16 or wider, within the bound.
No kernel may reach another device: no remote copies, remote signals or barrier semaphores. Data moves between devices by JAX's collectives and lax.ppermute only.
A program may use at most 192 MiB of HBM per device.

v0:
```python
import jax
import jax.numpy as jnp
from jax import lax
from jax.sharding import PartitionSpec as P

SIDE = 8


relax_step = 0.1


def padded(cells, sides, width):
    for axis, dim in sides:
        count = lax.axis_size(axis)
        ends = count - 1
        head = lax.slice_in_dim(cells, 0, width, axis=dim)
        tail = lax.slice_in_dim(cells, cells.shape[dim] - width, cells.shape[dim], axis=dim)
        cells = jnp.concatenate(
            [
                lax.ppermute(tail, axis, [(i, (i + 1) % count) for i in range(ends)]),
                cells,
                lax.ppermute(head, axis, [((i + 1) % count, i) for i in range(ends)]),
            ],
            axis=dim,
        )
    return cells


def leaf_project(density, leaf_basis):
    return jnp.einsum(
        "olp,rp->lor", density, leaf_basis, preferred_element_type=jnp.float32
    ).astype(jnp.bfloat16)


def octant_up(moments, side_boxes, transfer):
    node_count, orbits, rank_width = moments.shape
    layers = node_count // (side_boxes * side_boxes)
    half_side = side_boxes // 2
    shaped = moments.reshape(layers // 2, 2, half_side, 2, half_side, 2, orbits, rank_width)
    octant_grid = transfer.reshape(2, 2, 2, rank_width, rank_width)
    parents = jnp.einsum(
        "apbqcuos,pqusr->abcor", shaped, octant_grid, preferred_element_type=jnp.float32
    )
    return parents.reshape(-1, orbits, rank_width).astype(jnp.bfloat16)


def octant_down(coeffs, side_boxes, transfer):
    node_count, orbits, rank_width = coeffs.shape
    layers = node_count // (side_boxes * side_boxes)
    shaped = coeffs.reshape(layers, side_boxes, side_boxes, orbits, rank_width)
    octant_grid = transfer.reshape(2, 2, 2, rank_width, rank_width)
    children = jnp.einsum(
        "abcor,pqusr->apbqcuos", shaped, octant_grid, preferred_element_type=jnp.float32
    )
    return children.reshape(-1, orbits, rank_width)


def couple_rows(moments, sources, coupling, scale):
    node_count, orbits, rank_width = moments.shape
    flattened = moments.reshape(node_count, orbits * rank_width)
    identity = jnp.eye(orbits, dtype=coupling.dtype)
    running = None
    for column_start in range(0, sources.shape[1], 27):
        block_coupling = coupling[column_start : column_start + 27]
        widened = jnp.einsum("ab,krs->kasbr", identity, block_coupling).reshape(
            block_coupling.shape[0], orbits * rank_width, orbits * rank_width
        )
        picked = jnp.take(flattened, sources[:, column_start : column_start + 27], axis=0)
        piece_sum = jnp.einsum("lkx,kxy->ly", picked, widened, preferred_element_type=jnp.float32)
        running = piece_sum if running is None else running + piece_sum
    return scale * running.reshape(-1, orbits, rank_width)


def near_sum(density, sources, near_table):
    running = None
    for column_start in range(0, sources.shape[1], 9):
        picked = jnp.take(density, sources[:, column_start : column_start + 9], axis=1)
        piece_sum = jnp.einsum(
            "olkq,kpq->olp",
            picked,
            near_table[column_start : column_start + 9],
            preferred_element_type=jnp.float32,
        )
        running = piece_sum if running is None else running + piece_sum
    return running


def shifted(values, offset):
    node_count = values.shape[0]
    if abs(offset) >= node_count:
        return jnp.zeros_like(values)
    empty = jnp.zeros((abs(offset), values.shape[1], values.shape[2]), values.dtype)
    if offset > 0:
        return jnp.concatenate([values[offset:], empty], axis=0)
    return jnp.concatenate([empty, values[:offset]], axis=0)


def coarse_couple(moments, coarse_coupling, scale):
    node_count = moments.shape[0]
    odd_rows = (jnp.arange(node_count) % 2).astype(jnp.float32)[:, None, None]
    even_rows = 1.0 - odd_rows

    def apply_matrix(which, offset):
        return jnp.einsum(
            "nos,rs->nor",
            shifted(moments, offset),
            coarse_coupling[which],
            preferred_element_type=jnp.float32,
        )

    running = (
        apply_matrix(1, -2)
        + apply_matrix(2, 2)
        + even_rows * apply_matrix(3, 3)
        + odd_rows * apply_matrix(0, -3)
    )
    return scale * running


def coarse_up(moments, pair_transfer):
    node_count, orbits, rank_width = moments.shape
    shaped = moments.reshape(-1, 2, orbits, rank_width)
    return jnp.einsum(
        "apos,psr->aor", shaped, pair_transfer, preferred_element_type=jnp.float32
    ).astype(jnp.bfloat16)


def coarse_down(coeffs, pair_transfer):
    children = jnp.einsum(
        "aor,psr->apos", coeffs, pair_transfer, preferred_element_type=jnp.float32
    )
    return children.reshape(-1, coeffs.shape[1], coeffs.shape[2])


def coarse_tree(cube_moments, coarse_coupling, pair_transfer):
    levels = [cube_moments]
    while levels[-1].shape[0] > 1:
        levels.append(coarse_up(levels[-1], pair_transfer))
    top_level = len(levels) - 1
    coeffs = coarse_couple(levels[top_level], coarse_coupling, 0.5 ** (3 + top_level)).astype(
        jnp.bfloat16
    )
    for depth_level in range(top_level - 1, -1, -1):
        pushed = coarse_down(coeffs, pair_transfer)
        coupled = coarse_couple(levels[depth_level], coarse_coupling, 0.5 ** (3 + depth_level))
        coeffs = (coupled + pushed).astype(jnp.bfloat16)
    return coeffs


def shards(
    orbitals,
    near_source,
    far_leaf,
    far_mid,
    far_top,
    leaf_basis,
    near_table,
    transfer,
    coupling,
    pair_transfer,
    coarse_coupling,
):
    orbits, leaf_count, points = orbitals.shape
    rank_size = leaf_basis.shape[0]
    device = lax.axis_index("space")
    density = (orbitals * orbitals).astype(jnp.bfloat16)
    layer_size = SIDE * SIDE
    reach_leaves = 12 * layer_size
    density_ext = padded(density, (("space", 1),), layer_size)
    near_start = device * leaf_count - layer_size
    local_moments = leaf_project(density, leaf_basis)
    flattened = local_moments.reshape(leaf_count, orbits * rank_size)
    leaf_ext = padded(flattened, (("space", 0),), reach_leaves).reshape(-1, orbits, rank_size)
    near_field = near_sum(density_ext, near_source - near_start, near_table)
    mid_ext = octant_up(leaf_ext, SIDE, transfer)
    top_ext = octant_up(mid_ext, SIDE // 2, transfer)
    top_count = leaf_count // 64
    mid_count = leaf_count // 8
    top_rim = reach_leaves // 64
    mid_rim = reach_leaves // 8
    top_local = top_ext[top_rim : top_rim + top_count]
    cube_local = octant_up(top_local, SIDE // 4, transfer)
    cube_rows = cube_local.shape[0]
    cube_all = lax.all_gather(
        cube_local.reshape(cube_rows, orbits * rank_size), "space", axis=0, tiled=True
    ).reshape(-1, orbits, rank_size)
    cube_coeffs = coarse_tree(cube_all, coarse_coupling, pair_transfer)
    cube_own = lax.dynamic_slice_in_dim(cube_coeffs, device * cube_rows, cube_rows, 0)
    top_coeffs = (
        couple_rows(top_ext, far_top - (device * top_count - top_rim), coupling, 0.25)
        + octant_down(cube_own, SIDE // 8, transfer)
    ).astype(jnp.bfloat16)
    mid_coeffs = (
        couple_rows(mid_ext, far_mid - (device * mid_count - mid_rim), coupling, 0.5)
        + octant_down(top_coeffs, SIDE // 4, transfer)
    ).astype(jnp.bfloat16)
    leaf_coeffs = (
        couple_rows(leaf_ext, far_leaf - (device * leaf_count - reach_leaves), coupling, 1.0)
        + octant_down(mid_coeffs, SIDE // 2, transfer)
    ).astype(jnp.bfloat16)
    far_field = jnp.einsum(
        "lor,rp->olp", leaf_coeffs, leaf_basis, preferred_element_type=jnp.float32
    )
    potential = near_field + far_field
    hartree = lax.psum(jnp.sum(potential, axis=0).astype(jnp.bfloat16), "orb").astype(jnp.float32)
    return orbitals - relax_step * (hartree[None] - potential) * orbitals


def solution(mesh):
    placed = (
        P("orb", "space", None),
        P("space", None),
        P("space", None),
        P("space", None),
        P("space", None),
        P(),
        P(),
        P(),
        P(),
        P(),
        P(),
    )
    return jax.shard_map(
        shards, mesh=mesh, in_specs=placed, out_specs=P("orb", "space", None), check_vma=False
    )
```

profile of v0, /device:TPU:0, one launch (start us, length us, event | category | flops | bytes accessed | tf_op | source)
XLA Modules:
  0.0 1041.6 jit_solution(3446051249596485309)
XLA Ops:
  50.3 7.7 multiply_bitcast_fusion
  95.4 7.3 copy.374
  102.7 72.1 %gather_fusion.2 = bf16[9216,2,256]{2,1,0:T(2,128)(2,1)} fusion(bf16[2,1152,256]{2,0,1:T(2,128)(2,1)S(1)} %copy.374, s32[9216]{0:T(1024)S(1)} %broadcast_clamp_fusion.4), kind=kCustom, calls=%fused_computation.5.clone | custom fusion | bytes 18911232 | tf_op jit(solution)/shard_map/jit(_take)/gather | solution.py:77
  174.8 72.2 %gather_fusion.1 = bf16[9216,2,256]{2,1,0:T(2,128)(2,1)} fusion(bf16[2,1152,256]{2,0,1:T(2,128)(2,1)S(1)} %copy.374, s32[9216]{0:T(1024)S(1)} %broadcast_clamp_fusion.5), kind=kCustom, calls=%fused_computation.4.clone | custom fusion | bytes 18911232 | tf_op jit(solution)/shard_map/jit(_take)/gather | solution.py:77
  247.0 72.3 %gather_fusion = bf16[9216,2,256]{2,1,0:T(2,128)(2,1)} fusion(bf16[2,1152,256]{2,0,1:T(2,128)(2,1)S(1)} %copy.374, s32[9216]{0:T(1024)S(1)} %broadcast_clamp_fusion.6), kind=kCustom, calls=%fused_computation.clone | custom fusion | bytes 18911232 | tf_op jit(solution)/shard_map/jit(_take)/gather | solution.py:77
  319.2 18.5 %fusion.2 = bf16[2,1024,9,256]{3,0,2,1:T(2,128)(2,1)S(1)} fusion(bf16[1024,9,2,256]{3,2,1,0:T(2,128)(2,1)} %bitcast.330, pred[1024,9]{1,0:T(8,128)(4,1)S(1)} %copy.380), kind=kLoop, calls=%fused_computation.20 | loop fusion | flops 4718592 | bytes 18883584 | tf_op jit(solution)/shard_map/jit(_take)/select_n | solution.py:77
  341.8 16.6 %fusion.1 = bf16[2,1024,9,256]{3,0,2,1:T(2,128)(2,1)S(1)} fusion(bf16[1024,9,2,256]{3,2,1,0:T(2,128)(2,1)S(1)} %bitcast.329, pred[1024,9]{1,0:T(8,128)(4,1)S(1)} %copy-done.18), kind=kLoop, calls=%fused_computation.19 | loop fusion | flops 4718592 | bytes 18883584 | tf_op jit(solution)/shard_map/jit(_take)/select_n | solution.py:77
  358.4 17.7 %fusion = bf16[2,1024,9,256]{3,0,2,1:T(2,128)(2,1)} fusion(bf16[1024,9,2,256]{3,2,1,0:T(2,128)(2,1)S(1)} %bitcast.326, pred[1024,9]{1,0:T(8,128)(4,1)S(1)} %copy.372), kind=kLoop, calls=%fused_computation.18 | loop fusion | flops 4718592 | bytes 18883584 | tf_op jit(solution)/shard_map/jit(_take)/select_n | solution.py:77
  383.8 21.9 %all-gather = bf16[8,2,128]{2,1,0:T(2,128)(2,1)S(1)} all-gather(bf16[1,2,128]{2,1,0:T(2,128)(2,1)S(1)} %reshape.381), channel_id=1, replica_groups=mesh['space'=8,'orb'=4] {'space'}, dimensions={0}, use_global_device_ids=true | all-gather | bytes 4608 | tf_op jit(solution)/shard_map/all_gather | solution.py:184
  424.6 8.1 gather_fusion.10
  438.1 7.1 gather_fusion.9
  477.4 97.1 %gather_fusion.3 = bf16[27648,128]{1,0:T(8,128)(2,1)} fusion(bf16[2560,128]{1,0:T(8,128)(2,1)S(1)} %pad_maximum_fusion.1, s32[27648]{0:T(1024)S(1)} %broadcast_clamp_fusion.3), kind=kCustom, calls=%fused_computation.1.clone | custom fusion | bytes 14266368 | tf_op jit(solution)/shard_map/jit(_take)/gather | solution.py:68
  574.5 11.9 %reshape.404 = bf16[1024,27,128]{2,1,0:T(8,128)(2,1)} reshape(bf16[27648,128]{1,0:T(8,128)(2,1)} %gather_fusion.3) | data formatting | bytes 14155776 | tf_op jit(solution)/shard_map/jit(_take)/gather | solution.py:68
  586.5 15.6 %broadcast_select_fusion.6 = bf16[1024,27,128]{2,1,0:T(8,128)(2,1)S(1)} fusion(bf16[1024,27,128]{2,1,0:T(8,128)(2,1)} %reshape.404, pred[1024,27]{1,0:T(8,128)(4,1)S(1)} %copy-done.17), kind=kLoop, calls=%fused_computation.30 | loop fusion | flops 3538944 | bytes 14183424 | tf_op jit(solution)/shard_map/jit(_take)/select_n | solution.py:68
  606.4 97.1 %gather_fusion.4 = bf16[27648,128]{1,0:T(8,128)(2,1)} fusion(bf16[2560,128]{1,0:T(8,128)(2,1)S(1)} %pad_maximum_fusion.1, s32[27648]{0:T(1024)S(1)} %broadcast_clamp_fusion.2), kind=kCustom, calls=%fused_computation.6.clone | custom fusion | bytes 14266368 | tf_op jit(solution)/shard_map/jit(_take)/gather | solution.py:68
  703.5 11.9 %reshape.408 = bf16[1024,27,128]{2,1,0:T(8,128)(2,1)} reshape(bf16[27648,128]{1,0:T(8,128)(2,1)} %gather_fusion.4) | data formatting | bytes 14155776 | tf_op jit(solution)/shard_map/jit(_take)/gather | solution.py:68
  715.4 97.1 %gather_fusion.5 = bf16[27648,128]{1,0:T(8,128)(2,1)} fusion(bf16[2560,128]{1,0:T(8,128)(2,1)S(1)} %pad_maximum_fusion.1, s32[27648]{0:T(1024)S(1)} %broadcast_clamp_fusion.1), kind=kCustom, calls=%fused_computation.7.clone | custom fusion | bytes 14266368 | tf_op jit(solution)/shard_map/jit(_take)/gather | solution.py:68
  812.5 11.9 %reshape.412 = bf16[1024,27,128]{2,1,0:T(8,128)(2,1)} reshape(bf16[27648,128]{1,0:T(8,128)(2,1)} %gather_fusion.5) | data formatting | bytes 14155776 | tf_op jit(solution)/shard_map/jit(_take)/gather | solution.py:68
  824.4 97.0 %gather_fusion.6 = bf16[27648,128]{1,0:T(8,128)(2,1)} fusion(bf16[2560,128]{1,0:T(8,128)(2,1)S(1)} %pad_maximum_fusion.1, s32[27648]{0:T(1024)S(1)} %copy-done.5), kind=kCustom, calls=%fused_computation.8.clone | custom fusion | bytes 14266368 | tf_op jit(solution)/shard_map/jit(_take)/gather | solution.py:68
  921.4 12.0 %reshape.416 = bf16[1024,27,128]{2,1,0:T(8,128)(2,1)} reshape(bf16[27648,128]{1,0:T(8,128)(2,1)} %gather_fusion.6) | data formatting | bytes 14155776 | tf_op jit(solution)/shard_map/jit(_take)/gather | solution.py:68
  933.4 15.4 %broadcast_select_fusion.5 = bf16[1024,27,128]{2,1,0:T(8,128)(2,1)S(1)} fusion(bf16[1024,27,128]{2,1,0:T(8,128)(2,1)} %reshape.408, pred[1024,27]{1,0:T(8,128)(4,1)S(1)} %copy-done.14), kind=kLoop, calls=%fused_computation.29 | loop fusion | flops 3538944 | bytes 14183424 | tf_op jit(solution)/shard_map/jit(_take)/select_n | solution.py:68
  953.2 15.8 %broadcast_select_fusion.4 = bf16[1024,27,128]{2,1,0:T(8,128)(2,1)S(1)} fusion(bf16[1024,27,128]{2,1,0:T(8,128)(2,1)} %reshape.412, pred[1024,27]{1,0:T(8,128)(4,1)S(1)} %copy-done.15), kind=kLoop, calls=%fused_computation.28 | loop fusion | flops 3538944 | bytes 14183424 | tf_op jit(solution)/shard_map/jit(_take)/select_n | solution.py:68
  973.4 13.7 %broadcast_select_fusion.3 = bf16[1024,27,128]{2,1,0:T(8,128)(2,1)S(1)} fusion(bf16[1024,27,128]{2,1,0:T(8,128)(2,1)S(1)} %bitcast.332, pred[1024,27]{1,0:T(8,128)(4,1)S(1)} %copy-done.16), kind=kLoop, calls=%fused_computation.27 | loop fusion | flops 3538944 | bytes 14183424 | tf_op jit(solution)/shard_map/jit(_take)/select_n | solution.py:68
  999.1 30.8 %all-reduce.14.cloned.1.call-done = bf16[1024,256]{1,0:T(8,128)(2,1)} async-done(((bf16[1024,256]{1,0:T(8,128)(2,1)}), bf16[1024,256]{1,0:T(8,128)(2,1)}) %all-reduce.14.cloned.1.call-update) | async-done | bytes 524304 | tf_op jit(solution)/shard_map/psum | solution.py:205
  (325 shorter events, 177.6 us)
Async XLA Ops:
  6.5 375.9 %copy-start = (bf16[8,64,64]{2,1,0:T(8,128)(2,1)S(1)}, bf16[8,64,64]{2,1,0:T(8,128)(2,1)}, u32[]{:S(2)}) copy-start(bf16[8,64,64]{2,1,0:T(8,128)(2,1)} %param.26) | copy-start | bytes 196612
  6.5 27.0 %copy-start.30 = (s32[1024,27]{0,1:T(8,128)S(1)}, s32[1024,27]{0,1:T(8,128)}, u32[]{:S(2)}) copy-start(s32[1024,27]{0,1:T(8,128)} %param.20) | copy-start | bytes 331780
  6.5 29.4 %copy-start.2 = (bf16[108,64,64]{0,2,1:T(8,128)(2,1)S(1)}, bf16[108,64,64]{0,2,1:T(8,128)(2,1)}, u32[]{:S(2)}) copy-start(bf16[108,64,64]{0,2,1:T(8,128)(2,1)} %param.27) | copy-start | bytes 2654212
  6.5 1023.4 %all-reduce.14.cloned.1.call-start = ((), (), s32[]{:S(2)}) async-start(), calls=%async_computation | async-start | bytes 1048576 | tf_op jit(solution)/shard_map/psum | solution.py:205
  10.4 369.7 %collective-permute-start.2 = (bf16[768,128]{1,0:T(8,128)(2,1)}, bf16[768,128]{1,0:T(8,128)(2,1)}, u32[]{:S(2)}, u32[]{:S(2)}) collective-permute-start(bf16[768,128]{1,0:T(8,128)(2,1)} %copy.385), channel_id=1, source_target_pairs={{0,4},{4,8},{8,12},{12,16},{16,20},{20,24},{24,28},{1,5},{5,9},{9,... | collective-permute-start | bytes 589832 | tf_op jit(solution)/shard_map/ppermute | solution.py:20
  16.8 363.3 %collective-permute-start.3 = (bf16[768,128]{1,0:T(8,128)(2,1)}, bf16[768,128]{1,0:T(8,128)(2,1)}, u32[]{:S(2)}, u32[]{:S(2)}) collective-permute-start(bf16[768,128]{1,0:T(8,128)(2,1)} %copy.386), channel_id=1, source_target_pairs={{4,0},{8,4},{12,8},{16,12},{20,16},{24,20},{28,24},{5,1},{9,5},{13... | collective-permute-start | bytes 589832 | tf_op jit(solution)/shard_map/ppermute | solution.py:22
  18.8 75.6 %collective-permute-start = (bf16[2,64,256]{2,1,0:T(8,128)(2,1)}, bf16[2,64,256]{2,1,0:T(8,128)(2,1)}, u32[]{:S(2)}, u32[]{:S(2)}) collective-permute-start(bf16[2,64,256]{2,1,0:T(8,128)(2,1)} %get-tuple-element.6), channel_id=1, source_target_pairs={{0,4},{4,8},{8,12},{12,16},{16,20},{20,24},{24,28},{1,5},{5,9},{9,... | collective-permute-start | bytes 196616 | tf_op jit(solution)/shard_map/ppermute | solution.py:20
  24.0 70.5 %collective-permute-start.1 = (bf16[2,64,256]{2,1,0:T(8,128)(2,1)}, bf16[2,64,256]{2,1,0:T(8,128)(2,1)}, u32[]{:S(2)}, u32[]{:S(2)}) collective-permute-start(bf16[2,64,256]{2,1,0:T(8,128)(2,1)} %get-tuple-element.8), channel_id=1, source_target_pairs={{4,0},{8,4},{12,8},{16,12},{20,16},{24,20},{28,24},{5,1},{9,5},{13... | collective-permute-start | bytes 196616 | tf_op jit(solution)/shard_map/ppermute | solution.py:22
  58.0 25.9 %copy-start.21 = (s32[1024,27]{0,1:T(8,128)S(1)}, s32[1024,27]{0,1:T(8,128)}, u32[]{:S(2)}) copy-start(s32[1024,27]{0,1:T(8,128)} %get-tuple-element.22) | copy-start | bytes 331780
  58.0 26.5 %copy-start.29 = (pred[1024,27]{0,1:T(8,128)(4,1)S(1)}, pred[1024,27]{0,1:T(8,128)(4,1)}, u32[]{:S(2)}) copy-start(pred[1024,27]{0,1:T(8,128)(4,1)} %get-tuple-element.18) | copy-start | bytes 82948
  58.1 27.4 %copy-start.20 = (s32[1024,27]{0,1:T(8,128)S(1)}, s32[1024,27]{0,1:T(8,128)}, u32[]{:S(2)}) copy-start(s32[1024,27]{0,1:T(8,128)} %get-tuple-element.21) | copy-start | bytes 331780
  58.1 28.0 %copy-start.28 = (pred[1024,27]{0,1:T(8,128)(4,1)S(1)}, pred[1024,27]{0,1:T(8,128)(4,1)}, u32[]{:S(2)}) copy-start(pred[1024,27]{0,1:T(8,128)(4,1)} %get-tuple-element.17) | copy-start | bytes 82948
  58.1 28.9 %copy-start.19 = (s32[1024,27]{0,1:T(8,128)S(1)}, s32[1024,27]{0,1:T(8,128)}, u32[]{:S(2)}) copy-start(s32[1024,27]{0,1:T(8,128)} %get-tuple-element.20) | copy-start | bytes 331780
  380.1 32.3 %copy-start.38 = (s32[1024]{0:T(1024)S(1)}, s32[1024]{0:T(1024)}, u32[]{:S(2)}) copy-start(s32[1024]{0:T(1024)} %pad_clamp_fusion.4) | copy-start | bytes 12292
  380.1 34.5 %copy-start.41 = (pred[16,27]{1,0:T(8,128)(4,1)S(1)}, pred[16,27]{1,0:T(8,128)(4,1)}, u32[]{:S(2)}) copy-start(pred[16,27]{1,0:T(8,128)(4,1)} %get-tuple-element.41) | copy-start | bytes 1300
  380.1 34.5 %copy-start.42 = (pred[16,27]{1,0:T(8,128)(4,1)S(1)}, pred[16,27]{1,0:T(8,128)(4,1)}, u32[]{:S(2)}) copy-start(pred[16,27]{1,0:T(8,128)(4,1)} %get-tuple-element.42) | copy-start | bytes 1300
  381.2 34.6 %copy-start.4 = (bf16[27,128,128]{2,1,0:T(8,128)(2,1)S(1)}, bf16[27,128,128]{2,1,0:T(8,128)(2,1)}, u32[]{:S(2)}) copy-start(bf16[27,128,128]{2,1,0:T(8,128)(2,1)} %reshape.215) | copy-start | bytes 2654212
  381.7 34.6 %copy-start.39 = (pred[16,27]{1,0:T(8,128)(4,1)S(1)}, pred[16,27]{1,0:T(8,128)(4,1)}, u32[]{:S(2)}) copy-start(pred[16,27]{1,0:T(8,128)(4,1)} %get-tuple-element.39) | copy-start | bytes 1300
  381.7 34.6 %copy-start.40 = (pred[16,27]{1,0:T(8,128)(4,1)S(1)}, pred[16,27]{1,0:T(8,128)(4,1)}, u32[]{:S(2)}) copy-start(pred[16,27]{1,0:T(8,128)(4,1)} %get-tuple-element.40) | copy-start | bytes 1300
  382.4 33.7 %copy-start.6 = (bf16[27,128,128]{2,1,0:T(8,128)(2,1)S(1)}, bf16[27,128,128]{2,1,0:T(8,128)(2,1)}, u32[]{:S(2)}) copy-start(bf16[27,128,128]{2,1,0:T(8,128)(2,1)} %reshape.216) | copy-start | bytes 2654212
  382.4 38.9 %copy-start.43 = (f32[2,2,2,64]{3,1,0,2:T(2,128)S(1)}, f32[2,2,2,64]{3,1,0,2:T(2,128)}, u32[]{:S(2)}) copy-start(f32[2,2,2,64]{3,1,0,2:T(2,128)} %copy.442) | copy-start | bytes 6148
  382.4 40.8 %copy-start.44 = (f32[8]{0:T(128)S(1)}, f32[8]{0:T(128)}, u32[]{:S(2)}) copy-start(f32[8]{0:T(128)} %fusion.182) | copy-start | bytes 100
  992.1 38.9 %copy-start.3 = (f32[2,1024,256]{2,1,0:T(8,128)S(1)}, f32[2,1024,256]{2,1,0:T(8,128)}, u32[]{:S(2)}) copy-start(f32[2,1024,256]{2,1,0:T(8,128)} %param.19) | copy-start | bytes 6291460
  992.1 42.2 %copy-start.1 = (bf16[8,64,64]{2,1,0:T(8,128)(2,1)S(1)}, bf16[8,64,64]{2,1,0:T(8,128)(2,1)}, u32[]{:S(2)}) copy-start(bf16[8,64,64]{2,1,0:T(8,128)(2,1)} %param.26) | copy-start | bytes 196612
  (40 other events, 609.9 us)
Sparse Core Ops, SparseCore 0:
  999.2 30.6 all-reduce.13
where the time goes:
time: 1050 us; the launch traced here: 1040 us
  local copies, waits for them, and re-layouts  757 us (72%)
  other arithmetic  152 us (14%)
  matrix products  51.2 us (5%)
  waiting for transfers between devices  30.8 us (3%)
  blocking collectives  21.9 us (2%)
  between operations  15.2 us (1%)
  starting transfers between devices  13.3 us (1%)
    gather x24, local copies, waits for them, and re-layouts, couple_rows(): jnp.take(flattened, sources[:, column_start:column_start + 27], axis=0)  479 us
    gather x3, local copies, waits for them, and re-layouts, near_sum(): jnp.take(density, sources[:, column_start:column_start + 9], axis=1)  217 us
    select_n x13, other arithmetic, couple_rows(): jnp.take(flattened, sources[:, column_start:column_start + 27], axis=0)  73.6 us
    select_n x4, other arithmetic, near_sum(): jnp.take(density, sources[:, column_start:column_start + 9], axis=1)  53.4 us
    psum x1, waiting for transfers between devices, shards(): lax.psum(jnp.sum(potential, axis=0).astype(jnp.bfloat16), 'orb')  30.8 us
    dot_general x12, matrix products, couple_rows(): jnp.einsum('lkx,kxy->ly', picked, widened, preferred_element_type=jnp.flo...  26.1 us
    all_gather x1, blocking collectives, shards(): lax.all_gather(cube_local.reshape(cube_rows, orbits * rank_size), 'space'...  21.9 us
  transfers between devices with their start and end apart: 5, of which 1 were waited for; matrix products, arithmetic and copies ran while one was open for 34% of the time, Pallas kernels for 0%

commit v1 on v0

v1 whole, which is shorter than its diff:
```python
import functools

import jax
import jax.numpy as jnp
from jax import lax
from jax.experimental import pallas as pl
from jax.experimental.pallas import tpu as pltpu
from jax.sharding import PartitionSpec as P

SIDE = 8
LAYER = SIDE * SIDE
PAIR = 2 * LAYER
BF = jnp.bfloat16
F32 = jnp.float32
relax_step = 0.1
WIDE_MEMORY = pltpu.CompilerParams(vmem_limit_bytes=60 * 1024 * 1024)


def iota(shape, axis):
    return lax.broadcasted_iota(jnp.int32, shape, axis)


def dot(left, right):
    return jnp.dot(left, right, preferred_element_type=F32)


def dot_tn(left, right):
    return lax.dot_general(left, right, (((0,), (0,)), ((), ())), preferred_element_type=F32)


def dot_nt(left, right):
    return lax.dot_general(left, right, (((1,), (1,)), ((), ())), preferred_element_type=F32)


def pick_matrix(rows, source_of_lane):
    lanes = source_of_lane.shape[1]
    hit = iota((rows, lanes), 0) == jnp.broadcast_to(source_of_lane, (rows, lanes))
    return jnp.where(hit, 1.0, 0.0).astype(BF)


def index_columns(row, rows):
    lanes = row.shape[1]
    thin = jnp.broadcast_to(row, (16, lanes)).astype(BF)
    tall = jnp.concatenate([thin] * (rows // 16), axis=0)
    steps = iota((rows, lanes), 0).astype(F32).astype(BF)
    return jnp.where(steps == tall, jnp.ones((), BF), jnp.zeros((), BF))


def turned(values):
    return jnp.transpose(values)


def up_level(children, side, transfer_ref, rank):
    half_bits = (side // 2).bit_length() - 1
    lane = iota((1, 128), 1)
    depth = lax.shift_right_logical(lane, 2 * half_bits)
    across = lax.shift_right_logical(lane, half_bits) & (side // 2 - 1)
    along = lane & (side // 2 - 1)
    base = 2 * depth * side * side + 2 * across * side + 2 * along
    orbits = children.shape[0] // rank
    totals = [None] * orbits
    for octant in range(8):
        offset = (octant // 4) * side * side + (octant // 2 % 2) * side + octant % 2
        picked = dot(children, pick_matrix(children.shape[1], base + offset)).astype(BF)
        for o in range(orbits):
            part = dot_tn(transfer_ref[octant], picked[o * rank : (o + 1) * rank])
            totals[o] = part if totals[o] is None else totals[o] + part
    return jnp.concatenate(totals, axis=0).astype(BF)


def down_level(parents, child_lanes, side, transfer_ref, rank):
    bits = side.bit_length() - 1
    lane = iota((1, child_lanes), 1)
    depth = lax.shift_right_logical(lane, 2 * bits)
    across = lax.shift_right_logical(lane, bits) & (side - 1)
    along = lane & (side - 1)
    half = side // 2
    parent = (
        lax.shift_right_logical(depth, 1) * half * half
        + lax.shift_right_logical(across, 1) * half
        + lax.shift_right_logical(along, 1)
    )
    octant_of = 4 * (depth & 1) + 2 * (across & 1) + (along & 1)
    spread = dot(parents, pick_matrix(parents.shape[1], parent))
    orbits = parents.shape[0] // rank
    totals = [None] * orbits
    for octant in range(8):
        kept = jnp.where(octant_of == octant, spread, 0.0).astype(BF)
        for o in range(orbits):
            part = dot(transfer_ref[octant], kept[o * rank : (o + 1) * rank])
            totals[o] = part if totals[o] is None else totals[o] + part
    return jnp.concatenate(totals, axis=0)


def moments_kernel(
    place_ref,
    orbitals_ref,
    basis_ref,
    transfer_ref,
    dense_ref,
    whole_ref,
    odd_ref,
    left_ref,
    right_ref,
    cube_ref,
):
    orbits, leaves, points = orbitals_ref.shape
    rank = basis_ref.shape[0]
    wide = orbits * points
    basis = basis_ref[...]
    inner = leaves - 2 * LAYER
    gap = jnp.zeros((LAYER, points), F32)
    moments = []
    moments_odd = []
    for o in range(orbits):
        value = orbitals_ref[o]
        density = value * value
        rows = slice(o * points, (o + 1) * points)
        dense_ref[rows, :] = turned(density[LAYER : leaves - LAYER]).astype(BF)
        first = jnp.concatenate([gap, density[:LAYER]], axis=0)
        last = jnp.concatenate([density[leaves - LAYER :], gap], axis=0)
        left_ref[rows, :] = turned(first).astype(BF)
        right_ref[rows, :] = turned(last).astype(BF)
        moments.append(dot_nt(basis, density.astype(BF)))
        shifted = jnp.concatenate([gap, density, gap], axis=0).astype(BF)
        moments_odd.append(dot_nt(basis, shifted))
    moments = jnp.concatenate(moments, axis=0).astype(BF)
    moments_odd = jnp.concatenate(moments_odd, axis=0).astype(BF)
    blocks = leaves // PAIR
    for b in range(blocks):
        whole_ref[b] = moments[:, b * PAIR : (b + 1) * PAIR]
    for b in range(blocks + 1):
        odd_ref[b] = moments_odd[:, b * PAIR : (b + 1) * PAIR]
    mid = up_level(moments, SIDE, transfer_ref, rank)
    top = up_level(mid, SIDE // 2, transfer_ref, rank)
    cube = up_level(top, SIDE // 4, transfer_ref, rank)
    height = orbits * rank
    for ref, pieces in (
        (left_ref, (moments[:, :PAIR], moments_odd[:, :PAIR], moments_odd[:, PAIR : 2 * PAIR])),
        (
            right_ref,
            (
                moments[:, leaves - PAIR :],
                moments_odd[:, leaves - PAIR : leaves],
                moments_odd[:, leaves:],
            ),
        ),
    ):
        for n, piece in enumerate(pieces + (mid, top)):
            ref[wide + n * height : wide + (n + 1) * height, :] = piece
    own = leaves // (LAYER * SIDE)
    lane = iota((1, 128), 1)
    from_lane = lane - place_ref[0] * own
    from_lane = jnp.where((from_lane >= 0) & (from_lane < own), from_lane, -1)
    cube_ref[...] = dot(cube, pick_matrix(128, from_lane)).astype(BF)


def widen_kernel(coupling_ref, out_ref):
    slots, rank, _ = coupling_ref.shape
    count = slots // 2
    blank = jnp.zeros((rank, rank), F32)
    for half in range(2):
        for j in range(count):
            block = coupling_ref[half * count + j].astype(F32)
            cols = slice(j * 2 * rank, (j + 1) * 2 * rank)
            row = half * 2 * rank
            out_ref[row : row + rank, cols] = jnp.concatenate([block, blank], axis=1).astype(BF)
            out_ref[row + rank : row + 2 * rank, cols] = jnp.concatenate([blank, block], axis=1).astype(BF)


def near_body(start, source_ref, table_hbm, out_ref, sum_ref, side_ref, table_ref, wide_ref, turn_ref, picked_ref, sems):
    step = pl.program_id(0)
    slots, points, _ = table_hbm.shape

    def table_copy(k):
        return pltpu.make_async_copy(
            table_hbm.at[k], table_ref.at[:, pl.ds(k * points, points)], sems.at[k]
        )

    @pl.when(step == 0)
    def _():
        for k in range(slots):
            table_copy(k).start()

    wide_ref[:, :slots] = (source_ref[...] - start).astype(F32)
    turn_ref[...] = turned(wide_ref[...])
    orbits = side_ref.shape[0] // points
    group = 3

    def gather(chunk, carry):
        columns = []
        for n in range(group):
            columns.append(index_columns(turn_ref[pl.ds(chunk * group + n, 1), :], 2 * PAIR))
        picked = dot(side_ref[...], jnp.concatenate(columns, axis=1)).astype(BF)
        for n in range(group):
            row = pl.multiple_of((chunk * group + n) * points, points)
            for o in range(orbits):
                picked_ref[pl.ds(row, points), o * PAIR : (o + 1) * PAIR] = picked[
                    o * points : (o + 1) * points, n * PAIR : (n + 1) * PAIR
                ]
        return carry

    lax.fori_loop(0, slots // group, gather, 0)

    @pl.when(step == 0)
    def _():
        for k in range(slots):
            table_copy(k).wait()

    field = dot(table_ref[...], picked_ref[...])
    out_ref[0] = field
    total = field[:, :PAIR]
    for o in range(1, orbits):
        total = total + field[:, o * PAIR : (o + 1) * PAIR]
    sum_ref[0] = total.astype(BF)


def near_inner_kernel(first, pairs, place_ref, source_ref, early_ref, late_ref, table_hbm, *rest):
    out_ref, sum_ref, side_ref = rest[-8:-5]
    pair = first + pl.program_id(0)
    side_ref[:, :PAIR] = early_ref[...]
    side_ref[:, PAIR:] = late_ref[...]
    start = (place_ref[0] * pairs + pair) * PAIR - LAYER
    near_body(start, source_ref, table_hbm, out_ref, sum_ref, side_ref, *rest[-5:])


def near_outer_kernel(
    pairs, place_ref, source_ref, first_ref, last_ref, left_ref, right_ref, got_left_ref, got_right_ref, table_hbm, *rest
):
    out_ref, sum_ref, side_ref = rest[-8:-5]
    step = pl.program_id(0)

    @pl.when(step == 0)
    def _():
        side_ref[:, :PAIR] = left_ref[...] + got_left_ref[...]
        side_ref[:, PAIR:] = first_ref[...]

    @pl.when(step == 1)
    def _():
        side_ref[:, :PAIR] = last_ref[...]
        side_ref[:, PAIR:] = right_ref[...] + got_right_ref[...]

    start = (place_ref[0] * pairs + step * (pairs - 1)) * PAIR - LAYER
    near_body(start, source_ref, table_hbm, out_ref, sum_ref, side_ref, *rest[-5:])


def near_call(kernel, steps, pair_of, leaves, orbits, table, extra, extra_specs, place, source, before, rows):
    slots, points, _ = table.shape
    pairs = leaves // PAIR
    wide = orbits * points
    shapes = (
        jax.ShapeDtypeStruct((pairs, points, orbits * PAIR), F32),
        jax.ShapeDtypeStruct((pairs, points, PAIR), BF),
    )
    in_specs = [
        pl.BlockSpec(memory_space=pltpu.SMEM),
        pl.BlockSpec((PAIR, slots), lambda i: (pair_of(i), 0)),
        *extra_specs,
        pl.BlockSpec(memory_space=pl.ANY),
    ]
    operands = [place, source, *extra, table]
    aliases = {}
    if before is not None:
        aliases = {len(operands): 0, len(operands) + 1: 1}
        operands += list(before)
        in_specs += [pl.BlockSpec(memory_space=pl.ANY)] * 2
    return pl.pallas_call(
        kernel,
        grid=(steps,),
        in_specs=in_specs,
        out_specs=(
            pl.BlockSpec((1, points, orbits * PAIR), lambda i: (pair_of(i), 0, 0)),
            pl.BlockSpec((1, points, PAIR), lambda i: (pair_of(i), 0, 0)),
        ),
        out_shape=shapes,
        scratch_shapes=[
            pltpu.VMEM((wide, 2 * PAIR), BF),
            pltpu.VMEM((points, slots * points), BF),
            pltpu.VMEM((PAIR, 128), F32),
            pltpu.VMEM((128, PAIR), F32),
            pltpu.VMEM((slots * points, orbits * PAIR), BF),
            pltpu.SemaphoreType.DMA((slots,)),
        ],
        input_output_aliases=aliases,
        compiler_params=WIDE_MEMORY,
        cost_estimate=pl.CostEstimate(
            flops=steps * 4 * slots * points * points * orbits * PAIR,
            transcendentals=0,
            bytes_accessed=2 * slots * points * points + steps * 6 * points * orbits * PAIR,
        ),
    )(*operands)


def rolled(values, shift):
    return pltpu.roll(values, shift, 1)


def coarse_part(cubes, coupling_ref, pair_ref, count, rank):
    orbits = cubes.shape[0] // rank
    sizes = [count]
    while sizes[-1] > 1:
        sizes.append(sizes[-1] // 2)
    starts = [sum(sizes[:j]) for j in range(len(sizes))]
    last = len(sizes) - 1
    lane = iota((1, 128), 1)
    level = jnp.full((1, 128), -1, jnp.int32)
    node = jnp.zeros((1, 128), jnp.int32)
    size = jnp.zeros((1, 128), jnp.int32)
    start = jnp.zeros((1, 128), jnp.int32)
    child = jnp.full((1, 128), -1, jnp.int32)
    parent = jnp.full((1, 128), -1, jnp.int32)
    scale = jnp.zeros((1, 128), F32)
    for j, (begin, n) in enumerate(zip(starts, sizes)):
        here = (lane >= begin) & (lane < begin + n)
        level = jnp.where(here, j, level)
        node = jnp.where(here, lane - begin, node)
        size = jnp.where(here, n, size)
        start = jnp.where(here, begin, start)
        scale = jnp.where(here, 0.5 ** (3 + j), scale)
        if j:
            child = jnp.where(here, starts[j - 1] + 2 * (lane - begin), child)
        if j < last:
            parent = jnp.where(here, starts[j + 1] + lax.shift_right_logical(lane - begin, 1), parent)
    odd = node & 1
    picks = [pick_matrix(128, jnp.where(child >= 0, child + p, -1)) for p in range(2)]
    current = jnp.where(level == 0, cubes.astype(F32), 0.0).astype(BF)

    def split(values, o):
        return values[o * rank : (o + 1) * rank]

    for j in range(1, last + 1):
        sides = [dot(current, picks[p]).astype(BF) for p in range(2)]
        raised = jnp.concatenate(
            [
                dot_tn(pair_ref[0], split(sides[0], o)) + dot_tn(pair_ref[1], split(sides[1], o))
                for o in range(orbits)
            ],
            axis=0,
        )
        current = jnp.where(level == j, raised, current.astype(F32)).astype(BF)
    far = [None] * orbits
    for which, offset, parity in ((1, -2, None), (2, 2, None), (3, 3, 0), (0, -3, 1)):
        there = node + offset
        good = (there >= 0) & (there < size)
        if parity is not None:
            good = good & (odd == parity)
        side = dot(current, pick_matrix(128, jnp.where(good, start + there, -1))).astype(BF)
        for o in range(orbits):
            part = dot(coupling_ref[which], split(side, o))
            far[o] = part if far[o] is None else far[o] + part
    far = scale * jnp.concatenate(far, axis=0)
    coeffs = far.astype(BF)
    widen = pick_matrix(128, parent)
    for j in range(last - 1, -1, -1):
        spread = dot(coeffs, widen)
        parts = [jnp.where(odd == p, spread, 0.0).astype(BF) for p in range(2)]
        pushed = jnp.concatenate(
            [
                dot(pair_ref[0], split(parts[0], o)) + dot(pair_ref[1], split(parts[1], o))
                for o in range(orbits)
            ],
            axis=0,
        )
        coeffs = jnp.where(level == j, far + pushed, coeffs.astype(F32)).astype(BF)
    return coeffs


def tree_kernel(
    count,
    leaves,
    rank,
    place_ref,
    own_mid_ref,
    own_top_ref,
    left_mid_ref,
    left_top_ref,
    right_mid_ref,
    right_top_ref,
    cube_ref,
    weight_ref,
    transfer_ref,
    pair_ref,
    coarse_ref,
    far_mid_ref,
    far_top_ref,
    out_ref,
    wide_ref,
    turn_ref,
    picked_ref,
):
    place = place_ref[0]
    height = own_mid_ref.shape[0]
    slots = far_mid_ref.shape[1]
    half_slots = slots // 2
    mids = far_mid_ref.shape[0]
    tops = far_top_ref.shape[0]
    mid_rim = 3 * (SIDE // 2) ** 2
    top_rim = 3 * (SIDE // 4) ** 2
    lane = iota((height, 128), 1)

    cube_coeffs = coarse_part(cube_ref[...], coarse_ref, pair_ref, count, rank)
    own = leaves // (LAYER * SIDE)
    lane_row = iota((1, 128), 1)
    cube_own = dot(
        cube_coeffs, pick_matrix(128, jnp.where(lane_row < own, lane_row + place * own, -1))
    ).astype(BF)

    left = left_mid_ref[...].astype(F32)
    middle = rolled(own_mid_ref[...].astype(F32), mid_rim)
    right = rolled(right_mid_ref[...].astype(F32), mid_rim)
    left = rolled(left, mid_rim)
    mid_ext = jnp.concatenate(
        [jnp.where(lane < mid_rim, left, middle), jnp.where(lane < mid_rim, middle, right)], axis=1
    ).astype(BF)
    left = rolled(left_top_ref[...].astype(F32), 128 + top_rim - tops)
    middle = rolled(own_top_ref[...].astype(F32), top_rim)
    right = rolled(right_top_ref[...].astype(F32), top_rim + tops)
    top_ext = jnp.where(
        lane < top_rim, left, jnp.where(lane < top_rim + tops, middle, right)
    ).astype(BF)

    wide_ref[...] = jnp.full(wide_ref.shape, -1.0, F32)
    wide_ref[0, :, :slots] = (far_mid_ref[...] - (place * mids - mid_rim)).astype(F32)
    wide_ref[1, :tops, :slots] = (far_top_ref[...] - (place * tops - top_rim)).astype(F32)
    turn_ref[0] = turned(wide_ref[0])
    turn_ref[1] = turned(wide_ref[1])
    group = 6

    def gather(chunk, carry):
        mid_columns = []
        top_columns = []
        for n in range(group):
            mid_columns.append(index_columns(turn_ref[0, pl.ds(chunk * group + n, 1), :], 256))
            top_columns.append(index_columns(turn_ref[1, pl.ds(chunk * group + n, 1), :], 128))
        mid_picked = dot(mid_ext, jnp.concatenate(mid_columns, axis=1)).astype(BF)
        top_picked = dot(top_ext, jnp.concatenate(top_columns, axis=1)).astype(BF)
        for n in range(group):
            row = pl.multiple_of((chunk * group + n) * height, height)
            picked_ref[pl.ds(row, height), :128] = mid_picked[:, n * 128 : (n + 1) * 128]
            picked_ref[pl.ds(row, height), 128:] = top_picked[:, n * 128 : (n + 1) * 128]
        return carry

    lax.fori_loop(0, slots // group, gather, 0)
    depth = half_slots * height
    far = dot(weight_ref[:height], picked_ref[:depth]) + dot(weight_ref[height:], picked_ref[depth:])
    top = (0.25 * far[:, 128:] + down_level(cube_own, 128, SIDE // 4, transfer_ref, rank)).astype(BF)
    mid = (0.5 * far[:, :128] + down_level(top, 128, SIDE // 2, transfer_ref, rank)).astype(BF)
    out_ref[...] = down_level(mid, leaves, SIDE, transfer_ref, rank)


def leaf_kernel(
    pairs,
    place_ref,
    source_ref,
    whole_ref,
    odd_ref,
    left_ref,
    right_ref,
    weight_ref,
    down_ref,
    coeffs_ref,
    sum_ref,
    even_ref,
    shift_ref,
    wide_ref,
    turn_ref,
    rows_ref,
    picked_ref,
):
    step = pl.program_id(0)
    height = whole_ref.shape[1]
    slots = source_ref.shape[1]
    half_slots = slots // 2

    @pl.when(step == 0)
    def _():
        even_ref[0] = left_ref[:height]
        shift_ref[0] = left_ref[height : 2 * height]
        for b in range(pairs):
            even_ref[b + 1] = whole_ref[b]
        for b in range(1, pairs):
            shift_ref[b + 1] = odd_ref[b]
        shift_ref[1] = odd_ref[0] + left_ref[2 * height :]
        shift_ref[pairs + 1] = odd_ref[pairs] + right_ref[height : 2 * height]
        even_ref[pairs + 1] = right_ref[:height]
        shift_ref[pairs + 2] = right_ref[2 * height :]

    source = source_ref[...]
    layer_bits = LAYER.bit_length() - 1
    target_layer = (place_ref[0] * pairs + step) * 2 + lax.shift_right_logical(iota(source.shape, 0), layer_bits)
    away = lax.shift_right_logical(source, layer_bits) - target_layer
    away = jnp.where(away < 0, away + 3, away)
    wide_ref[:, :slots] = (away * LAYER + (source & (LAYER - 1))).astype(F32)
    turn_ref[...] = turned(wide_ref[...])
    early = turn_ref[:half_slots, :]
    late = turn_ref[half_slots:slots, :]
    low = iota((half_slots, PAIR), 1) < LAYER
    rows_ref[0, :half_slots, :] = jnp.where(low, early, rolled(late, LAYER))
    rows_ref[1, :half_slots, :] = jnp.where(low, rolled(early, LAYER), late)
    group = 6

    def gather(chunk, carry):
        for z in range(2):
            if z == 0:
                before, after = shift_ref[step], even_ref[step + 2]
            else:
                before, after = even_ref[step], shift_ref[step + 3]
            side = jnp.concatenate([before, after], axis=1)
            columns = []
            for n in range(group):
                columns.append(index_columns(rows_ref[z, pl.ds(chunk * group + n, 1), :], 256))
            picked = dot(side, jnp.concatenate(columns, axis=1)).astype(BF)
            for n in range(group):
                row = pl.multiple_of((chunk * group + n) * height, height)
                picked_ref[pl.ds(row, height), z * PAIR : (z + 1) * PAIR] = picked[
                    :, n * PAIR : (n + 1) * PAIR
                ]
        return carry

    lax.fori_loop(0, half_slots // group, gather, 0)
    both = dot(weight_ref[...], picked_ref[...])
    low = iota((height, PAIR), 1) < LAYER
    first = both[:height, :PAIR] + rolled(both[height:, :PAIR], LAYER)
    second = rolled(both[:height, PAIR:], LAYER) + both[height:, PAIR:]
    coeffs = (jnp.where(low, first, second) + down_ref[...]).astype(BF)
    coeffs_ref[...] = coeffs
    rank = sum_ref.shape[0]
    total = coeffs[:rank].astype(F32)
    for o in range(1, height // rank):
        total = total + coeffs[o * rank : (o + 1) * rank].astype(F32)
    sum_ref[...] = total.astype(BF)


def final_kernel(
    orbitals_ref, near_ref, sum_ref, other_sum_ref, coeffs_ref, total_ref, other_total_ref, basis_ref, out_ref
):
    orbits = orbitals_ref.shape[0]
    rank = basis_ref.shape[0]
    hartree = sum_ref[0].astype(F32) + other_sum_ref[0].astype(F32)
    total = total_ref[...].astype(F32) + other_total_ref[...].astype(F32)
    for o in range(orbits):
        rest = (total - coeffs_ref[o * rank : (o + 1) * rank].astype(F32)).astype(BF)
        gap = hartree - near_ref[0, :, o * PAIR : (o + 1) * PAIR] + dot_tn(basis_ref[...], rest)
        value = orbitals_ref[o]
        out_ref[o] = value - relax_step * turned(gap) * value


def swap(values, axis, bit):
    count = lax.axis_size(axis)
    return lax.ppermute(values, axis, [(i, i ^ bit) for i in range(count)])


def shards(
    orbitals,
    near_source,
    far_leaf,
    far_mid,
    far_top,
    leaf_basis,
    near_table,
    transfer,
    coupling,
    pair_transfer,
    coarse_coupling,
):
    orbits, leaves, points = orbitals.shape
    rank = leaf_basis.shape[0]
    devices = lax.axis_size("space")
    groups = lax.axis_size("orb")
    height = orbits * rank
    wide = orbits * points
    pairs = leaves // PAIR
    slots = far_leaf.shape[1]
    count = devices * (leaves // (LAYER * SIDE))
    assert height == 128 and leaves == 1024 and 2 * count - 1 <= 128
    assert devices & (devices - 1) == 0 and groups == 4
    place = lax.axis_index("space").astype(jnp.int32).reshape(1)
    message = wide + 5 * height
    smem = pl.BlockSpec(memory_space=pltpu.SMEM)

    dense, whole, odd, to_left, to_right, cubes = pl.pallas_call(
        moments_kernel,
        in_specs=[smem] + [pl.BlockSpec()] * 3,
        out_shape=(
            jax.ShapeDtypeStruct((wide, leaves - PAIR), BF),
            jax.ShapeDtypeStruct((pairs, height, PAIR), BF),
            jax.ShapeDtypeStruct((pairs + 1, height, PAIR), BF),
            jax.ShapeDtypeStruct((message, PAIR), BF),
            jax.ShapeDtypeStruct((message, PAIR), BF),
            jax.ShapeDtypeStruct((height, 128), BF),
        ),
        compiler_params=WIDE_MEMORY,
        name="moments",
    )(place, orbitals, leaf_basis, transfer)

    from_left = lax.ppermute(to_right, "space", [(i, i + 1) for i in range(devices - 1)])
    from_right = lax.ppermute(to_left, "space", [(i + 1, i) for i in range(devices - 1)])
    bit = 1
    while bit < devices:
        cubes = cubes + swap(cubes, "space", bit)
        bit *= 2

    weight = pl.pallas_call(
        widen_kernel,
        out_shape=jax.ShapeDtypeStruct((2 * height, slots // 2 * height), BF),
        compiler_params=WIDE_MEMORY,
        name="widen",
    )(coupling)

    block = lambda which: pl.BlockSpec((wide, PAIR), which)
    inner = pairs - 2
    near = near_call(
        functools.partial(near_inner_kernel, 1, pairs),
        inner,
        lambda i: i + 1,
        leaves,
        orbits,
        near_table,
        (dense, dense),
        (block(lambda i: (0, i)), block(lambda i: (0, i + 1))),
        place,
        near_source,
        None,
        None,
    )
    near, near_sum = near_call(
        functools.partial(near_outer_kernel, pairs),
        2,
        lambda i: i * (pairs - 1),
        leaves,
        orbits,
        near_table,
        (dense, dense, to_left, to_right, from_left, from_right),
        (
            block(lambda i: (0, 0)),
            block(lambda i: (0, inner)),
            block(lambda i: (0, 0)),
            block(lambda i: (0, 0)),
            block(lambda i: (0, 0)),
            block(lambda i: (0, 0)),
        ),
        place,
        near_source,
        near,
        None,
    )
    near_chip = near_sum + swap(near_sum, "orb", 1)

    box = lambda n: pl.BlockSpec((height, 128), lambda i: (n, 0))
    base = wide // height
    full = lambda shape: pl.BlockSpec(shape, lambda i: (0,) * len(shape))
    down = pl.pallas_call(
        functools.partial(tree_kernel, count, leaves, rank),
        grid=(1,),
        in_specs=[
            smem,
            box(base + 3),
            box(base + 4),
            box(base + 3),
            box(base + 4),
            box(base + 3),
            box(base + 4),
            full((height, 128)),
            full(weight.shape),
            full(transfer.shape),
            full(pair_transfer.shape),
            full(coarse_coupling.shape),
            full(far_mid.shape),
            full(far_top.shape),
        ],
        out_specs=full((height, leaves)),
        out_shape=jax.ShapeDtypeStruct((height, leaves), F32),
        scratch_shapes=[
            pltpu.VMEM((2, 128, 128), F32),
            pltpu.VMEM((2, 128, 128), F32),
            pltpu.VMEM((slots * height, 256), BF),
        ],
        compiler_params=WIDE_MEMORY,
        name="tree",
    )(
        place,
        to_left,
        to_left,
        from_left,
        from_left,
        from_right,
        from_right,
        cubes,
        weight,
        transfer,
        pair_transfer,
        coarse_coupling,
        far_mid,
        far_top,
    )
    near_other = swap(near_chip, "orb", 2)

    edge = lambda: pl.BlockSpec((3 * height, PAIR), lambda i: (0, 0))
    coeffs, coeff_sum = pl.pallas_call(
        functools.partial(leaf_kernel, pairs),
        grid=(pairs,),
        in_specs=[
            smem,
            pl.BlockSpec((PAIR, slots), lambda i: (i, 0)),
            full(whole.shape),
            full(odd.shape),
            edge(),
            edge(),
            full(weight.shape),
            pl.BlockSpec((height, PAIR), lambda i: (0, i)),
        ],
        out_specs=(
            pl.BlockSpec((height, PAIR), lambda i: (0, i)),
            pl.BlockSpec((rank, PAIR), lambda i: (0, i)),
        ),
        out_shape=(
            jax.ShapeDtypeStruct((height, leaves), BF),
            jax.ShapeDtypeStruct((rank, leaves), BF),
        ),
        scratch_shapes=[
            pltpu.VMEM((pairs + 2, height, PAIR), BF),
            pltpu.VMEM((pairs + 3, height, PAIR), BF),
            pltpu.VMEM((PAIR, 128), F32),
            pltpu.VMEM((128, PAIR), F32),
            pltpu.VMEM((2, slots // 2 + 2, PAIR), F32),
            pltpu.VMEM((slots // 2 * height, 2 * PAIR), BF),
        ],
        compiler_params=WIDE_MEMORY,
        name="leaf",
    )(
        place,
        far_leaf,
        whole,
        odd,
        from_left[wide : wide + 3 * height],
        from_right[wide : wide + 3 * height],
        weight,
        down,
    )
    coeff_chip = coeff_sum + swap(coeff_sum, "orb", 1)
    coeff_other = swap(coeff_chip, "orb", 2)

    per_pair = pl.BlockSpec((1, points, PAIR), lambda i: (i, 0, 0))
    per_rank = pl.BlockSpec((rank, PAIR), lambda i: (0, i))
    per_leaf = pl.BlockSpec((orbits, PAIR, points), lambda i: (0, i, 0))
    return pl.pallas_call(
        final_kernel,
        grid=(pairs,),
        in_specs=[
            per_leaf,
            pl.BlockSpec((1, points, orbits * PAIR), lambda i: (i, 0, 0)),
            per_pair,
            per_pair,
            pl.BlockSpec((height, PAIR), lambda i: (0, i)),
            per_rank,
            per_rank,
            full(leaf_basis.shape),
        ],
        out_specs=per_leaf,
        out_shape=jax.ShapeDtypeStruct(orbitals.shape, F32),
        compiler_params=WIDE_MEMORY,
        name="final",
    )(orbitals, near, near_chip, near_other, coeffs, coeff_chip, coeff_other, leaf_basis)


def solution(mesh):
    placed = (
        P("orb", "space", None),
        P("space", None),
        P("space", None),
        P("space", None),
        P("space", None),
        P(),
        P(),
        P(),
        P(),
        P(),
        P(),
    )
    return jax.shard_map(
        shards, mesh=mesh, in_specs=placed, out_specs=P("orb", "space", None), check_vma=False
    )
```

time: 1050 us -> 152 us (0.14)
  local copies, waits for them, and re-layouts: 757 us -> 11 us
  other arithmetic: 152 us -> 2.76 us
  Pallas kernels: 0 us -> 107 us
  matrix products: 51.2 us -> 0 us
  blocking collectives: 21.9 us -> 0 us
  waiting for transfers between devices: 30.8 us -> 12.5 us
  between operations: 15.2 us -> 0.15 us
    gather x27 -> x0, local copies, waits for them, and re-layouts: 695 us -> none  [the longest x24 479 us: couple_rows(): jnp.take(flattened, sources[:, column_start:column_start + 27], axis=0)]
    select_n x17 -> x0, other arithmetic: 127 us -> none  [the longest x13 73.6 us: couple_rows(): jnp.take(flattened, sources[:, column_start:column_start + 27], axis=0)]
    pallas_call x0 -> x7, Pallas kernels: none -> 107 us  [the longest x2 38.9 us: near_call(): pl.pallas_call(kernel, grid=(steps,), in_specs=in_specs, out_specs=(pl.Bl...]
    dot_general x46 -> x0, matrix products: 51.2 us -> none  [the longest x12 26.1 us: couple_rows(): jnp.einsum('lkx,kxy->ly', picked, widened, preferred_element_type=jnp.flo...]
    psum x1 -> x0, waiting for transfers between devices: 30.8 us -> none  [shards(): lax.psum(jnp.sum(potential, axis=0).astype(jnp.bfloat16), 'orb')]
    all_gather x1 -> x0, blocking collectives: 21.9 us -> none  [shards(): lax.all_gather(cube_local.reshape(cube_rows, orbits * rank_size), 'space'...]
    reshape x8 -> x0, local copies, waits for them, and re-layouts: 19.6 us -> none  [the longest x4 17.4 us: couple_rows(): jnp.einsum('ab,krs->kasbr', identity, block_coupling)]
    slice x24 -> x2, local copies, waits for them, and re-layouts: 17.1 us -> 3.06 us  [the longest x1 1.53 us: shards(): from_right[wide:wide + 3 * height]]
  transfers between devices with their start and end apart: 5 -> 9, of which waited for: 1 -> 5; matrix products, arithmetic and copies ran while one was open for 34% -> 7% of each run, Pallas kernels for 0% -> 54%
where the time goes in v1:
time: 152 us; the launch traced here: 151 us
  Pallas kernels  107 us (70%)
  starting transfers between devices  17.4 us (11%)
  waiting for transfers between devices  12.5 us (8%)
  local copies, waits for them, and re-layouts  11 us (7%)
  other arithmetic  2.76 us (2%)
    pallas_call x2, Pallas kernels, near_call(): pl.pallas_call(kernel, grid=(steps,), in_specs=in_specs, out_specs=(pl.Bl...  38.9 us
    pallas_call x1, Pallas kernels, shards(): pl.pallas_call(functools.partial(leaf_kernel, pairs), grid=(pairs,), in_s...  35.1 us
    pallas_call x1, Pallas kernels, shards(): pl.pallas_call(functools.partial(tree_kernel, count, leaves, rank), grid=...  14.7 us
    ppermute x7, waiting for transfers between devices, swap(): return lax.ppermute(values, axis, [(i, i ^ bit) for i in range(count)])  12.5 us
    ppermute x7, starting transfers between devices, swap(): return lax.ppermute(values, axis, [(i, i ^ bit) for i in range(count)])  11 us
    unnamed x26, local copies, waits for them, and re-layouts  7.91 us
    pallas_call x1, Pallas kernels, shards(): pl.pallas_call(moments_kernel, in_specs=[smem] + [pl.BlockSpec()] * 3, ou...  7.36 us
    pallas_call x1, Pallas kernels, shards(): pl.pallas_call(final_kernel, grid=(pairs,), in_specs=[per_leaf, pl.BlockS...  7.26 us
  transfers between devices with their start and end apart: 9, of which 5 were waited for; matrix products, arithmetic and copies ran while one was open for 7% of the time, Pallas kernels for 54%

profile of v1, /device:TPU:0, one launch (start us, length us, event | category | flops | bytes accessed | tf_op | source)
XLA Modules:
  0.0 151.1 jit_solution(7144795736936829810)
XLA Ops:
  0.0 7.4 %moments.1 = (bf16[512,896]{1,0:T(8,128)(2,1)}, bf16[8,128,128]{2,1,0:T(8,128)(2,1)}, bf16[9,128,128]{2,1,0:T(8,128)(2,1)}, bf16[1152,128]{1,0:T(8,128)(2,1)}, b...) custom-call(s32[1]{0:T(128)} %bitcast.place_ref, f32[2,1024,256]{2,1,0:T(8,128)} %orbitals_ref.3, ...), custom_call_target="tpu_custom_call" | custom-call | tf_op jit(solution)/shard_map/moments/pallas_call | solution.py:581
  7.4 4.9 %collective-permute-start = (bf16[1152,128]{1,0:T(8,128)(2,1)}, bf16[1152,128]{1,0:T(8,128)(2,1)S(1)}, u32[]{:S(2)}, u32[]{:S(2)}) collective-permute-start(bf16[1152,128]{1,0:T(8,128)(2,1)} %get-tuple-element.19.right_ref), channel_id=1, source_target_pairs={{0,4},{4,8},{8,12},{12,16},{16,20},{20,24},{24,28},{1,5},{5,9},{9,... | collective-permute-start | bytes 884744 | tf_op jit(solution)/shard_map/ppermute | solution.py:596
  12.3 1.5 collective-permute-start.1
  13.8 1.0 copy.15.source_ref
  14.8 28.0 %shard_map.109 = (f32[8,256,256]{2,1,0:T(8,128)}, bf16[8,256,128]{2,1,0:T(8,128)(2,1)}) custom-call(s32[1]{0:T(128)} %bitcast.place_ref, s32[1024,27]{1,0:T(8,128)} %copy.15.source_ref, bf16[512,896]{1,0:T(8,128)(2,1)} %get-tuple-element.17.early_ref.late_ref.first_ref.last_ref, bf16[512,896]{1,0:T(8,128)(2,1)} %get-tuple-element.17.early_ref.late_ref.first_ref.last_ref, ...), custom_call_target="tpu_custom_call" | custom-call | flops 10871635968 | bytes 5898240 | tf_op jit(solution)/shard_map/pallas_call | solution.py:267
  43.6 10.9 %shard_map.110 = (f32[8,256,256]{2,1,0:T(8,128)}, bf16[8,256,128]{2,1,0:T(8,128)(2,1)}) custom-call(s32[1]{0:T(128)} %bitcast.place_ref, s32[1024,27]{1,0:T(8,128)} %copy.15.source_ref, bf16[512,896]{1,0:T(8,128)(2,1)} %get-tuple-element.17.early_ref.late_ref.first_ref.last_ref, ...), custom_call_target="tpu_custom_call", output_to_operand_aliasing={{0}: (9, {}), {1}: (10, {})} | custom-call | flops 3623878656 | bytes 4325376 | tf_op jit(solution)/shard_map/pallas_call | solution.py:267
  54.6 2.1 %collective-permute-done.2 = bf16[8,256,128]{2,1,0:T(8,128)(2,1)S(1)} collective-permute-done((bf16[8,256,128]{2,1,0:T(8,128)(2,1)}, bf16[8,256,128]{2,1,0:T(8,128)(2,1)S(1)}, u32[]{:S(2)}, u32[]{:S(2)}) %collective-permute-start.2) | collective-permute-done | bytes 524320 | tf_op jit(solution)/shard_map/ppermute | solution.py:550
  56.7 1.2 add.15.sum_ref
  57.9 1.6 %collective-permute-start.3 = (bf16[8,256,128]{2,1,0:T(8,128)(2,1)S(1)}, bf16[8,256,128]{2,1,0:T(8,128)(2,1)S(1)}, u32[]{:S(2)}, u32[]{:S(2)}) collective-permute-start(bf16[8,256,128]{2,1,0:T(8,128)(2,1)S(1)} %add.15.sum_ref), channel_id=1, source_target_pairs={{0,2},{1,3},{2,0},{3,1},{4,6},{5,7},{6,4},{7,5},{8,10},{9,11},{10,... | collective-permute-start | bytes 1572872 | tf_op jit(solution)/shard_map/ppermute | solution.py:550
  59.5 2.6 %collective-permute-start.4 = (bf16[128,128]{1,0:T(8,128)(2,1)S(1)}, bf16[128,128]{1,0:T(8,128)(2,1)S(1)}, u32[]{:S(2)}, u32[]{:S(2)}) collective-permute-start(bf16[128,128]{1,0:T(8,128)(2,1)S(1)} %copy-done.10), channel_id=1, source_target_pairs={{0,4},{4,0},{8,12},{12,8},{16,20},{20,16},{24,28},{28,24},{1,5},{5... | collective-permute-start | bytes 98312 | tf_op jit(solution)/shard_map/ppermute | solution.py:550
  62.2 1.9 %collective-permute-done.4 = bf16[128,128]{1,0:T(8,128)(2,1)S(1)} collective-permute-done((bf16[128,128]{1,0:T(8,128)(2,1)S(1)}, bf16[128,128]{1,0:T(8,128)(2,1)S(1)}, u32[]{:S(2)}, u32[]{:S(2)}) %collective-permute-start.4) | collective-permute-done | bytes 32800 | tf_op jit(solution)/shard_map/ppermute | solution.py:550
  64.1 3.0 %collective-permute-start.5 = (bf16[128,128]{1,0:T(8,128)(2,1)S(1)}, bf16[128,128]{1,0:T(8,128)(2,1)S(1)}, u32[]{:S(2)}, u32[]{:S(2)}) collective-permute-start(bf16[128,128]{1,0:T(8,128)(2,1)S(1)} %add.16), channel_id=1, source_target_pairs={{0,8},{4,12},{8,0},{12,4},{16,24},{20,28},{24,16},{28,20},{1,9},{5... | collective-permute-start | bytes 98312 | tf_op jit(solution)/shard_map/ppermute | solution.py:550
  67.1 1.9 %collective-permute-done.5 = bf16[128,128]{1,0:T(8,128)(2,1)S(1)} collective-permute-done((bf16[128,128]{1,0:T(8,128)(2,1)S(1)}, bf16[128,128]{1,0:T(8,128)(2,1)S(1)}, u32[]{:S(2)}, u32[]{:S(2)}) %collective-permute-start.5) | collective-permute-done | bytes 32800 | tf_op jit(solution)/shard_map/ppermute | solution.py:550
  69.0 3.1 %collective-permute-start.6 = (bf16[128,128]{1,0:T(8,128)(2,1)S(1)}, bf16[128,128]{1,0:T(8,128)(2,1)S(1)}, u32[]{:S(2)}, u32[]{:S(2)}) collective-permute-start(bf16[128,128]{1,0:T(8,128)(2,1)S(1)} %add.17), channel_id=1, source_target_pairs={{0,16},{4,20},{8,24},{12,28},{16,0},{20,4},{24,8},{28,12},{1,17},{... | collective-permute-start | bytes 98312 | tf_op jit(solution)/shard_map/ppermute | solution.py:550
  72.8 1.0 copy.18.source_ref
  73.8 3.5 %copy.16.coupling_ref = bf16[108,64,64]{2,1,0:T(8,128)(2,1)} copy(bf16[108,64,64]{0,2,1:T(8,128)(2,1)S(1)} %copy-done.3) | data formatting | bytes 1769472 | tf_op args[8]
  77.3 4.0 %widen.1.weight_ref = bf16[256,6912]{1,0:T(8,128)(2,1)} custom-call(bf16[108,64,64]{2,1,0:T(8,128)(2,1)} %copy.16.coupling_ref), custom_call_target="tpu_custom_call" | custom-call | tf_op jit(solution)/shard_map/widen/pallas_call | solution.py:603
  81.9 1.5 %slice.8.left_ref = bf16[384,128]{1,0:T(8,128)(2,1)} slice(bf16[1152,128]{1,0:T(8,128)(2,1)} %copy-done.1), slice={[512:896], [0:128]} | slice | bytes 196608 | tf_op jit(solution)/shard_map/slice | solution.py:735
  83.5 1.5 %slice.9.right_ref = bf16[384,128]{1,0:T(8,128)(2,1)} slice(bf16[1152,128]{1,0:T(8,128)(2,1)} %copy-done.2), slice={[512:896], [0:128]} | slice | bytes 196608 | tf_op jit(solution)/shard_map/slice | solution.py:736
  85.0 14.7 %tree.1.down_ref = f32[128,1024]{1,0:T(8,128)} custom-call(s32[1]{0:T(128)} %bitcast.place_ref, bf16[1152,128]{1,0:T(8,128)(2,1)} %get-tuple-element.18.left_ref.own_mid_ref.own_top_ref, bf16[1152,128]{1,0:T(8,128)(2,1)} %get-tuple-element.18.left_ref.own_mid_ref.own_top_ref, bf16[1152,128]{1,0:T(8,128)(2,1)} %copy-done.1, bf16[1152,128]{1,0:T(8,128)(2,1)} %copy-done.1, ...), custom_call_target="tpu_custom_call" | custom-call | tf_op jit(solution)/shard_map/tree/pallas_call | solution.py:652
  99.7 35.1 %leaf.1 = (bf16[128,1024]{1,0:T(8,128)(2,1)}, bf16[64,1024]{1,0:T(8,128)(2,1)}) custom-call(s32[1]{0:T(128)} %bitcast.place_ref, s32[1024,108]{1,0:T(8,128)} %copy.18.source_ref, bf16[8,128,128]{2,1,0:T(8,128)(2,1)} %get-tuple-element.24.whole_ref, bf16[9,128,128]{2,1,0:T(8,128)(2,1)} %get-tuple-element.25.odd_ref, bf16[384,128]{1,0:T(8,128)(2,1)} %slice.8.left_ref, ...), custom_call_target="tpu_custom_call" | custom-call | tf_op jit(solution)/shard_map/leaf/pallas_call | solution.py:699
  134.8 1.6 %collective-permute-done.7 = bf16[64,1024]{1,0:T(8,128)(2,1)S(1)} collective-permute-done((bf16[64,1024]{1,0:T(8,128)(2,1)}, bf16[64,1024]{1,0:T(8,128)(2,1)S(1)}, u32[]{:S(2)}, u32[]{:S(2)}) %collective-permute-start.7) | collective-permute-done | bytes 131104 | tf_op jit(solution)/shard_map/ppermute | solution.py:550
  137.9 5.0 %collective-permute-done.8.other_total_ref = bf16[64,1024]{1,0:T(8,128)(2,1)S(1)} collective-permute-done((bf16[64,1024]{1,0:T(8,128)(2,1)S(1)}, bf16[64,1024]{1,0:T(8,128)(2,1)S(1)}, u32[]{:S(2)}, u32[]{:S(2)}) %collective-permute-start.8) | collective-permute-done | bytes 131104 | tf_op jit(solution)/shard_map/ppermute | solution.py:550
  143.8 7.3 %final.1 = f32[2,1024,256]{2,1,0:T(8,128)} custom-call(f32[2,1024,256]{2,1,0:T(8,128)} %orbitals_ref.3, f32[8,256,256]{2,1,0:T(8,128)} %get-tuple-element.22.near_ref, bf16[8,256,128]{2,1,0:T(8,128)(2,1)} %copy-done, bf16[8,256,128]{2,1,0:T(8,128)(2,1)} %copy-done.5, bf16[128,1024]{1,0:T(8,128)(2,1)} %get-tuple-element.27.coeffs_ref, ...), custom_call_target="tpu_custom_call" | custom-call | tf_op jit(solution)/shard_map/final/pallas_call | solution.py:746
  (34 shorter events, 4.6 us)
Async XLA Ops:
  0.0 13.8 %copy-start.8 = (s32[1024,27]{0,1:T(8,128)S(1)}, s32[1024,27]{0,1:T(8,128)}, u32[]{:S(2)}) copy-start(s32[1024,27]{0,1:T(8,128)} %param.12) | copy-start | bytes 331780
  7.4 35.4 %collective-permute-start = (bf16[1152,128]{1,0:T(8,128)(2,1)}, bf16[1152,128]{1,0:T(8,128)(2,1)S(1)}, u32[]{:S(2)}, u32[]{:S(2)}) collective-permute-start(bf16[1152,128]{1,0:T(8,128)(2,1)} %get-tuple-element.19.right_ref), channel_id=1, source_target_pairs={{0,4},{4,8},{8,12},{12,16},{16,20},{20,24},{24,28},{1,5},{5,9},{9,... | collective-permute-start | bytes 884744 | tf_op jit(solution)/shard_map/ppermute | solution.py:596
  12.3 30.5 %collective-permute-start.1 = (bf16[1152,128]{1,0:T(8,128)(2,1)}, bf16[1152,128]{1,0:T(8,128)(2,1)S(1)}, u32[]{:S(2)}, u32[]{:S(2)}) collective-permute-start(bf16[1152,128]{1,0:T(8,128)(2,1)} %get-tuple-element.18.left_ref.own_mid_ref.own_top_ref), channel_id=1, source_target_pairs={{4,0},{8,4},{12,8},{16,12},{20,16},{24,20},{28,24},{5,1},{9,5},{13... | collective-permute-start | bytes 884744 | tf_op jit(solution)/shard_map/ppermute | solution.py:597
  42.8 0.7 copy-start.1
  42.8 0.8 copy-start.2
  43.6 15.9 %copy-start.10 = (bf16[128,128]{1,0:T(8,128)(2,1)S(1)}, bf16[128,128]{1,0:T(8,128)(2,1)}, u32[]{:S(2)}) copy-start(bf16[128,128]{1,0:T(8,128)(2,1)} %get-tuple-element.26) | copy-start | bytes 98308
  43.6 28.5 %copy-start.9 = (s32[128,108]{0,1:T(8,128)S(1)}, s32[128,108]{0,1:T(8,128)}, u32[]{:S(2)}) copy-start(s32[128,108]{0,1:T(8,128)} %param.14) | copy-start | bytes 165892
  54.5 18.3 %copy-start.6 = (s32[1024,108]{0,1:T(8,128)S(1)}, s32[1024,108]{0,1:T(8,128)}, u32[]{:S(2)}) copy-start(s32[1024,108]{0,1:T(8,128)} %param.13) | copy-start | bytes 1327108
  54.5 19.3 %copy-start.3 = (bf16[108,64,64]{0,2,1:T(8,128)(2,1)S(1)}, bf16[108,64,64]{0,2,1:T(8,128)(2,1)}, u32[]{:S(2)}) copy-start(bf16[108,64,64]{0,2,1:T(8,128)(2,1)} %param.19) | copy-start | bytes 2654212
  54.6 2.2 %collective-permute-start.2 = (bf16[8,256,128]{2,1,0:T(8,128)(2,1)}, bf16[8,256,128]{2,1,0:T(8,128)(2,1)S(1)}, u32[]{:S(2)}, u32[]{:S(2)}) collective-permute-start(bf16[8,256,128]{2,1,0:T(8,128)(2,1)} %get-tuple-element.23), channel_id=1, source_target_pairs={{0,1},{1,0},{2,3},{3,2},{4,5},{5,4},{6,7},{7,6},{8,9},{9,8},{10,11... | collective-permute-start | bytes 1572872 | tf_op jit(solution)/shard_map/ppermute | solution.py:550
  57.9 23.4 %copy-start = (bf16[8,256,128]{2,1,0:T(8,128)(2,1)}, bf16[8,256,128]{2,1,0:T(8,128)(2,1)S(1)}, u32[]{:S(2)}) copy-start(bf16[8,256,128]{2,1,0:T(8,128)(2,1)S(1)} %add.15.sum_ref) | copy-start | bytes 1572868
  57.9 85.0 %collective-permute-start.3 = (bf16[8,256,128]{2,1,0:T(8,128)(2,1)S(1)}, bf16[8,256,128]{2,1,0:T(8,128)(2,1)S(1)}, u32[]{:S(2)}, u32[]{:S(2)}) collective-permute-start(bf16[8,256,128]{2,1,0:T(8,128)(2,1)S(1)} %add.15.sum_ref), channel_id=1, source_target_pairs={{0,2},{1,3},{2,0},{3,1},{4,6},{5,7},{6,4},{7,5},{8,10},{9,11},{10,... | collective-permute-start | bytes 1572872 | tf_op jit(solution)/shard_map/ppermute | solution.py:550
  59.5 4.5 %collective-permute-start.4 = (bf16[128,128]{1,0:T(8,128)(2,1)S(1)}, bf16[128,128]{1,0:T(8,128)(2,1)S(1)}, u32[]{:S(2)}, u32[]{:S(2)}) collective-permute-start(bf16[128,128]{1,0:T(8,128)(2,1)S(1)} %copy-done.10), channel_id=1, source_target_pairs={{0,4},{4,0},{8,12},{12,8},{16,20},{20,16},{24,28},{28,24},{1,5},{5... | collective-permute-start | bytes 98312 | tf_op jit(solution)/shard_map/ppermute | solution.py:550
  64.1 4.9 %collective-permute-start.5 = (bf16[128,128]{1,0:T(8,128)(2,1)S(1)}, bf16[128,128]{1,0:T(8,128)(2,1)S(1)}, u32[]{:S(2)}, u32[]{:S(2)}) collective-permute-start(bf16[128,128]{1,0:T(8,128)(2,1)S(1)} %add.16), channel_id=1, source_target_pairs={{0,8},{4,12},{8,0},{12,4},{16,24},{20,28},{24,16},{28,20},{1,9},{5... | collective-permute-start | bytes 98312 | tf_op jit(solution)/shard_map/ppermute | solution.py:550
  69.0 12.3 %collective-permute-start.6 = (bf16[128,128]{1,0:T(8,128)(2,1)S(1)}, bf16[128,128]{1,0:T(8,128)(2,1)S(1)}, u32[]{:S(2)}, u32[]{:S(2)}) collective-permute-start(bf16[128,128]{1,0:T(8,128)(2,1)S(1)} %add.17), channel_id=1, source_target_pairs={{0,16},{4,20},{8,24},{12,28},{16,0},{20,4},{24,8},{28,12},{1,17},{... | collective-permute-start | bytes 98312 | tf_op jit(solution)/shard_map/ppermute | solution.py:550
  134.8 1.6 %collective-permute-start.7 = (bf16[64,1024]{1,0:T(8,128)(2,1)}, bf16[64,1024]{1,0:T(8,128)(2,1)S(1)}, u32[]{:S(2)}, u32[]{:S(2)}) collective-permute-start(bf16[64,1024]{1,0:T(8,128)(2,1)} %get-tuple-element.28), channel_id=1, source_target_pairs={{0,1},{1,0},{2,3},{3,2},{4,5},{5,4},{6,7},{7,6},{8,9},{9,8},{10,11... | collective-permute-start | bytes 393224 | tf_op jit(solution)/shard_map/ppermute | solution.py:550
  137.3 5.6 %copy-start.4 = (bf16[64,1024]{1,0:T(8,128)(2,1)}, bf16[64,1024]{1,0:T(8,128)(2,1)S(1)}, u32[]{:S(2)}) copy-start(bf16[64,1024]{1,0:T(8,128)(2,1)S(1)} %add.19.total_ref) | copy-start | bytes 393220
  137.3 5.6 %collective-permute-start.8 = (bf16[64,1024]{1,0:T(8,128)(2,1)S(1)}, bf16[64,1024]{1,0:T(8,128)(2,1)S(1)}, u32[]{:S(2)}, u32[]{:S(2)}) collective-permute-start(bf16[64,1024]{1,0:T(8,128)(2,1)S(1)} %add.19.total_ref), channel_id=1, source_target_pairs={{0,2},{1,3},{2,0},{3,1},{4,6},{5,7},{6,4},{7,5},{8,10},{9,11},{10,... | collective-permute-start | bytes 393224 | tf_op jit(solution)/shard_map/ppermute | solution.py:550
  143.0 0.7 copy-start.7
  143.0 0.8 copy-start.5

commit v2 on v1

--- a/solution.py
+++ b/solution.py
@@ -6,6 +6,7 @@
 from jax.experimental import pallas as pl
 from jax.experimental.pallas import tpu as pltpu
 from jax.sharding import PartitionSpec as P
+
 
 SIDE = 8
 LAYER = SIDE * SIDE
@@ -50,7 +51,7 @@
     return jnp.transpose(values)
 
 
-def up_level(children, side, transfer_ref, rank):
+def up_level(children, side, transfer, rank):
     half_bits = (side // 2).bit_length() - 1
     lane = iota((1, 128), 1)
     depth = lax.shift_right_logical(lane, 2 * half_bits)
@@ -58,17 +59,18 @@
     along = lane & (side // 2 - 1)
     base = 2 * depth * side * side + 2 * across * side + 2 * along
     orbits = children.shape[0] // rank
-    totals = [None] * orbits
+    pieces = []
     for octant in range(8):
         offset = (octant // 4) * side * side + (octant // 2 % 2) * side + octant % 2
-        picked = dot(children, pick_matrix(children.shape[1], base + offset)).astype(BF)
-        for o in range(orbits):
-            part = dot_tn(transfer_ref[octant], picked[o * rank : (o + 1) * rank])
-            totals[o] = part if totals[o] is None else totals[o] + part
+        pieces.append(dot(children, pick_matrix(children.shape[1], base + offset)).astype(BF))
+    totals = []
+    for o in range(orbits):
+        stacked = jnp.concatenate([piece[o * rank : (o + 1) * rank] for piece in pieces], axis=0)
+        totals.append(dot_tn(transfer, stacked))
     return jnp.concatenate(totals, axis=0).astype(BF)
 
 
-def down_level(parents, child_lanes, side, transfer_ref, rank):
+def down_level(parents, child_lanes, side, transfer, rank):
     bits = side.bit_length() - 1
     lane = iota((1, child_lanes), 1)
     depth = lax.shift_right_logical(lane, 2 * bits)
@@ -81,14 +83,14 @@
         + lax.shift_right_logical(along, 1)
     )
     octant_of = 4 * (depth & 1) + 2 * (across & 1) + (along & 1)
-    spread = dot(parents, pick_matrix(parents.shape[1], parent))
-    orbits = parents.shape[0] // rank
-    totals = [None] * orbits
-    for octant in range(8):
-        kept = jnp.where(octant_of == octant, spread, 0.0).astype(BF)
-        for o in range(orbits):
-            part = dot(transfer_ref[octant], kept[o * rank : (o + 1) * rank])
-            totals[o] = part if totals[o] is None else totals[o] + part
+    spread = dot(parents, pick_matrix(parents.shape[1], parent)).astype(BF)
+    thin = jnp.broadcast_to(octant_of.astype(F32), (16, child_lanes)).astype(BF)
+    tall = jnp.concatenate([thin] * (rank // 16), axis=0)
+    totals = []
+    for o in range(parents.shape[0] // rank):
+        own = spread[o * rank : (o + 1) * rank]
+        kept = [jnp.where(tall == jnp.full((), octant, BF), own, jnp.zeros((), BF)) for octant in range(8)]
+        totals.append(dot(transfer, jnp.concatenate(kept, axis=0)))
     return jnp.concatenate(totals, axis=0)
 
 
@@ -102,13 +104,11 @@
     odd_ref,
     left_ref,
     right_ref,
-    cube_ref,
 ):
     orbits, leaves, points = orbitals_ref.shape
     rank = basis_ref.shape[0]
     wide = orbits * points
     basis = basis_ref[...]
-    inner = leaves - 2 * LAYER
     gap = jnp.zeros((LAYER, points), F32)
     moments = []
     moments_odd = []
@@ -131,9 +131,15 @@
         whole_ref[b] = moments[:, b * PAIR : (b + 1) * PAIR]
     for b in range(blocks + 1):
         odd_ref[b] = moments_odd[:, b * PAIR : (b + 1) * PAIR]
-    mid = up_level(moments, SIDE, transfer_ref, rank)
-    top = up_level(mid, SIDE // 2, transfer_ref, rank)
-    cube = up_level(top, SIDE // 4, transfer_ref, rank)
+    transfer = transfer_ref[...]
+    mid = up_level(moments, SIDE, transfer, rank)
+    top = up_level(mid, SIDE // 2, transfer, rank)
+    cube = up_level(top, SIDE // 4, transfer, rank)
+    own = leaves // (LAYER * SIDE)
+    lane = iota((1, 128), 1)
+    from_lane = lane - place_ref[0] * own
+    from_lane = jnp.where((from_lane >= 0) & (from_lane < own), from_lane, -1)
+    cube = dot(cube, pick_matrix(128, from_lane)).astype(BF)
     height = orbits * rank
     for ref, pieces in (
         (left_ref, (moments[:, :PAIR], moments_odd[:, :PAIR], moments_odd[:, PAIR : 2 * PAIR])),
@@ -146,13 +152,8 @@
             ),
         ),
     ):
-        for n, piece in enumerate(pieces + (mid, top)):
+        for n, piece in enumerate(pieces + (mid, top, cube)):
             ref[wide + n * height : wide + (n + 1) * height, :] = piece
-    own = leaves // (LAYER * SIDE)
-    lane = iota((1, 128), 1)
-    from_lane = lane - place_ref[0] * own
-    from_lane = jnp.where((from_lane >= 0) & (from_lane < own), from_lane, -1)
-    cube_ref[...] = dot(cube, pick_matrix(128, from_lane)).astype(BF)
 
 
 def widen_kernel(coupling_ref, out_ref):
@@ -168,7 +169,7 @@
             out_ref[row + rank : row + 2 * rank, cols] = jnp.concatenate([blank, block], axis=1).astype(BF)
 
 
-def near_body(start, source_ref, table_hbm, out_ref, sum_ref, side_ref, table_ref, wide_ref, turn_ref, picked_ref, sems):
+def near_body(start, source_ref, table_hbm, out_ref, sum_ref, side_ref, table_ref, turn_ref, picked_ref, sems):
     step = pl.program_id(0)
     slots, points, _ = table_hbm.shape
 
@@ -182,52 +183,47 @@
         for k in range(slots):
             table_copy(k).start()
 
-    wide_ref[:, :slots] = (source_ref[...] - start).astype(F32)
-    turn_ref[...] = turned(wide_ref[...])
+    turn_ref[:slots, :] = (source_ref[...] - start).astype(F32)
     orbits = side_ref.shape[0] // points
-    group = 3
-
-    def gather(chunk, carry):
-        columns = []
-        for n in range(group):
-            columns.append(index_columns(turn_ref[pl.ds(chunk * group + n, 1), :], 2 * PAIR))
-        picked = dot(side_ref[...], jnp.concatenate(columns, axis=1)).astype(BF)
-        for n in range(group):
-            row = pl.multiple_of((chunk * group + n) * points, points)
-            for o in range(orbits):
-                picked_ref[pl.ds(row, points), o * PAIR : (o + 1) * PAIR] = picked[
-                    o * points : (o + 1) * points, n * PAIR : (n + 1) * PAIR
+    group = 2
+    for begin in range(0, slots, group):
+        chunk = range(begin, min(begin + group, slots))
+        columns = [index_columns(turn_ref[k : k + 1, :], 2 * PAIR) for k in chunk]
+        columns = jnp.concatenate(columns, axis=1)
+        for o in range(orbits):
+            picked = dot(side_ref[o * points : (o + 1) * points], columns).astype(BF)
+            for n, k in enumerate(chunk):
+                picked_ref[k * points : (k + 1) * points, o * PAIR : (o + 1) * PAIR] = picked[
+                    :, n * PAIR : (n + 1) * PAIR
                 ]
-        return carry
-
-    lax.fori_loop(0, slots // group, gather, 0)
 
     @pl.when(step == 0)
     def _():
         for k in range(slots):
             table_copy(k).wait()
 
-    field = dot(table_ref[...], picked_ref[...])
-    out_ref[0] = field
-    total = field[:, :PAIR]
-    for o in range(1, orbits):
-        total = total + field[:, o * PAIR : (o + 1) * PAIR]
-    sum_ref[0] = total.astype(BF)
+    for rows in (slice(0, points // 2), slice(points // 2, points)):
+        field = dot(table_ref[rows, :], picked_ref[...])
+        out_ref[0, rows, :] = field
+        total = field[:, :PAIR]
+        for o in range(1, orbits):
+            total = total + field[:, o * PAIR : (o + 1) * PAIR]
+        sum_ref[0, rows, :] = total.astype(BF)
 
 
 def near_inner_kernel(first, pairs, place_ref, source_ref, early_ref, late_ref, table_hbm, *rest):
-    out_ref, sum_ref, side_ref = rest[-8:-5]
+    out_ref, sum_ref, side_ref = rest[-7:-4]
     pair = first + pl.program_id(0)
     side_ref[:, :PAIR] = early_ref[...]
     side_ref[:, PAIR:] = late_ref[...]
     start = (place_ref[0] * pairs + pair) * PAIR - LAYER
-    near_body(start, source_ref, table_hbm, out_ref, sum_ref, side_ref, *rest[-5:])
+    near_body(start, source_ref, table_hbm, out_ref, sum_ref, side_ref, *rest[-4:])
 
 
 def near_outer_kernel(
     pairs, place_ref, source_ref, first_ref, last_ref, left_ref, right_ref, got_left_ref, got_right_ref, table_hbm, *rest
 ):
-    out_ref, sum_ref, side_ref = rest[-8:-5]
+    out_ref, sum_ref, side_ref = rest[-7:-4]
     step = pl.program_id(0)
 
     @pl.when(step == 0)
@@ -241,10 +237,10 @@
         side_ref[:, PAIR:] = right_ref[...] + got_right_ref[...]
 
     start = (place_ref[0] * pairs + step * (pairs - 1)) * PAIR - LAYER
-    near_body(start, source_ref, table_hbm, out_ref, sum_ref, side_ref, *rest[-5:])
-
-
-def near_call(kernel, steps, pair_of, leaves, orbits, table, extra, extra_specs, place, source, before, rows):
+    near_body(start, source_ref, table_hbm, out_ref, sum_ref, side_ref, *rest[-4:])
+
+
+def near_call(kernel, steps, pair_of, leaves, orbits, table, extra, extra_specs, place, source, before):
     slots, points, _ = table.shape
     pairs = leaves // PAIR
     wide = orbits * points
@@ -254,7 +250,7 @@
     )
     in_specs = [
         pl.BlockSpec(memory_space=pltpu.SMEM),
-        pl.BlockSpec((PAIR, slots), lambda i: (pair_of(i), 0)),
+        pl.BlockSpec((slots, PAIR), lambda i: (0, pair_of(i))),
         *extra_specs,
         pl.BlockSpec(memory_space=pl.ANY),
     ]
@@ -276,8 +272,7 @@
         scratch_shapes=[
             pltpu.VMEM((wide, 2 * PAIR), BF),
             pltpu.VMEM((points, slots * points), BF),
-            pltpu.VMEM((PAIR, 128), F32),
-            pltpu.VMEM((128, PAIR), F32),
+            pltpu.VMEM((32, PAIR), F32),
             pltpu.VMEM((slots * points, orbits * PAIR), BF),
             pltpu.SemaphoreType.DMA((slots,)),
         ],
@@ -377,6 +372,7 @@
     right_mid_ref,
     right_top_ref,
     cube_ref,
+    other_cube_ref,
     weight_ref,
     transfer_ref,
     pair_ref,
@@ -390,15 +386,16 @@
 ):
     place = place_ref[0]
     height = own_mid_ref.shape[0]
-    slots = far_mid_ref.shape[1]
+    slots = far_mid_ref.shape[0]
     half_slots = slots // 2
-    mids = far_mid_ref.shape[0]
+    mids = far_mid_ref.shape[1]
     tops = far_top_ref.shape[0]
     mid_rim = 3 * (SIDE // 2) ** 2
     top_rim = 3 * (SIDE // 4) ** 2
     lane = iota((height, 128), 1)
 
-    cube_coeffs = coarse_part(cube_ref[...], coarse_ref, pair_ref, count, rank)
+    transfer = jnp.concatenate([transfer_ref[n].astype(F32) for n in range(8)], axis=1).astype(BF)
+    cube_coeffs = coarse_part(cube_ref[...] + other_cube_ref[...], coarse_ref, pair_ref, count, rank)
     own = leaves // (LAYER * SIDE)
     lane_row = iota((1, 128), 1)
     cube_own = dot(
@@ -420,32 +417,39 @@
     ).astype(BF)
 
     wide_ref[...] = jnp.full(wide_ref.shape, -1.0, F32)
-    wide_ref[0, :, :slots] = (far_mid_ref[...] - (place * mids - mid_rim)).astype(F32)
-    wide_ref[1, :tops, :slots] = (far_top_ref[...] - (place * tops - top_rim)).astype(F32)
-    turn_ref[0] = turned(wide_ref[0])
-    turn_ref[1] = turned(wide_ref[1])
-    group = 6
-
-    def gather(chunk, carry):
-        mid_columns = []
-        top_columns = []
+    wide_ref[:tops, :slots] = (far_top_ref[...] - (place * tops - top_rim)).astype(F32)
+    turn_ref[0, :slots, :] = (far_mid_ref[...] - (place * mids - mid_rim)).astype(F32)
+    packed = 128 // tops
+    lanes = iota((1, 128), 1)
+    tall = dot_tn(wide_ref[:tops, :].astype(BF), pick_matrix(tops, lanes & (tops - 1)))
+    mine = iota((128, 128), 0) & (packed - 1)
+    tall = jnp.where(mine == iota((128, 128), 1) // tops, tall, 0.0).astype(BF)
+    rows = 128 // packed
+    of_group = jnp.where(iota((rows, 128), 0) == iota((rows, 128), 1) // packed, 1.0, 0.0).astype(BF)
+    turn_ref[1, :rows, :] = dot(of_group, tall)
+    group = 2
+    for begin in range(0, slots, packed * group):
+        first = begin // packed
+        here = range(min(group, pl.cdiv(slots - begin, packed)))
+        top_columns = [index_columns(turn_ref[1, first + n : first + n + 1, :], 128) for n in here]
+        top_picked = dot(top_ext, jnp.concatenate(top_columns, axis=1))
+        for k in range(begin, min(slots, begin + packed * group)):
+            block = top_picked[:, (k - begin) // packed * 128 :][:, :128]
+            shift = (k % packed) * tops
+            block = rolled(block, 128 - shift) if shift else block
+            picked_ref[k * height : (k + 1) * height, 128:] = block.astype(BF)
+    for begin in range(0, slots, group):
+        mid_columns = [index_columns(turn_ref[0, begin + n : begin + n + 1, :], 256) for n in range(group)]
+        mid_picked = dot(mid_ext, jnp.concatenate(mid_columns, axis=1)).astype(BF)
         for n in range(group):
-            mid_columns.append(index_columns(turn_ref[0, pl.ds(chunk * group + n, 1), :], 256))
-            top_columns.append(index_columns(turn_ref[1, pl.ds(chunk * group + n, 1), :], 128))
-        mid_picked = dot(mid_ext, jnp.concatenate(mid_columns, axis=1)).astype(BF)
-        top_picked = dot(top_ext, jnp.concatenate(top_columns, axis=1)).astype(BF)
-        for n in range(group):
-            row = pl.multiple_of((chunk * group + n) * height, height)
-            picked_ref[pl.ds(row, height), :128] = mid_picked[:, n * 128 : (n + 1) * 128]
-            picked_ref[pl.ds(row, height), 128:] = top_picked[:, n * 128 : (n + 1) * 128]
-        return carry
-
-    lax.fori_loop(0, slots // group, gather, 0)
+            row = (begin + n) * height
+            picked_ref[row : row + height, :128] = mid_picked[:, n * 128 : (n + 1) * 128]
+
     depth = half_slots * height
     far = dot(weight_ref[:height], picked_ref[:depth]) + dot(weight_ref[height:], picked_ref[depth:])
-    top = (0.25 * far[:, 128:] + down_level(cube_own, 128, SIDE // 4, transfer_ref, rank)).astype(BF)
-    mid = (0.5 * far[:, :128] + down_level(top, 128, SIDE // 2, transfer_ref, rank)).astype(BF)
-    out_ref[...] = down_level(mid, leaves, SIDE, transfer_ref, rank)
+    top = (0.25 * far[:, 128:] + down_level(cube_own, 128, SIDE // 4, transfer, rank)).astype(BF)
+    mid = (0.5 * far[:, :128] + down_level(top, 128, SIDE // 2, transfer, rank)).astype(BF)
+    out_ref[...] = down_level(mid, leaves, SIDE, transfer, rank)
 
 
 def leaf_kernel(
@@ -462,62 +466,58 @@
     sum_ref,
     even_ref,
     shift_ref,
-    wide_ref,
     turn_ref,
     rows_ref,
     picked_ref,
 ):
     step = pl.program_id(0)
     height = whole_ref.shape[1]
-    slots = source_ref.shape[1]
+    slots = source_ref.shape[0]
     half_slots = slots // 2
 
     @pl.when(step == 0)
     def _():
-        even_ref[0] = left_ref[:height]
-        shift_ref[0] = left_ref[height : 2 * height]
+        def piece(ref, n):
+            first = ref.shape[0] - (6 - n) * height
+            return ref[first : first + height]
+
+        even_ref[0] = piece(left_ref, 0)
+        shift_ref[0] = piece(left_ref, 1)
         for b in range(pairs):
             even_ref[b + 1] = whole_ref[b]
         for b in range(1, pairs):
             shift_ref[b + 1] = odd_ref[b]
-        shift_ref[1] = odd_ref[0] + left_ref[2 * height :]
-        shift_ref[pairs + 1] = odd_ref[pairs] + right_ref[height : 2 * height]
-        even_ref[pairs + 1] = right_ref[:height]
-        shift_ref[pairs + 2] = right_ref[2 * height :]
+        shift_ref[1] = odd_ref[0] + piece(left_ref, 2)
+        shift_ref[pairs + 1] = odd_ref[pairs] + piece(right_ref, 1)
+        even_ref[pairs + 1] = piece(right_ref, 0)
+        shift_ref[pairs + 2] = piece(right_ref, 2)
 
     source = source_ref[...]
     layer_bits = LAYER.bit_length() - 1
-    target_layer = (place_ref[0] * pairs + step) * 2 + lax.shift_right_logical(iota(source.shape, 0), layer_bits)
+    target_layer = (place_ref[0] * pairs + step) * 2 + lax.shift_right_logical(iota(source.shape, 1), layer_bits)
     away = lax.shift_right_logical(source, layer_bits) - target_layer
     away = jnp.where(away < 0, away + 3, away)
-    wide_ref[:, :slots] = (away * LAYER + (source & (LAYER - 1))).astype(F32)
-    turn_ref[...] = turned(wide_ref[...])
+    turn_ref[:slots, :] = (away * LAYER + (source & (LAYER - 1))).astype(F32)
     early = turn_ref[:half_slots, :]
     late = turn_ref[half_slots:slots, :]
     low = iota((half_slots, PAIR), 1) < LAYER
     rows_ref[0, :half_slots, :] = jnp.where(low, early, rolled(late, LAYER))
     rows_ref[1, :half_slots, :] = jnp.where(low, rolled(early, LAYER), late)
-    group = 6
-
-    def gather(chunk, carry):
+    group = 2
+    sides = (
+        jnp.concatenate([shift_ref[step], even_ref[step + 2]], axis=1),
+        jnp.concatenate([even_ref[step], shift_ref[step + 3]], axis=1),
+    )
+    for begin in range(0, half_slots, group):
         for z in range(2):
-            if z == 0:
-                before, after = shift_ref[step], even_ref[step + 2]
-            else:
-                before, after = even_ref[step], shift_ref[step + 3]
-            side = jnp.concatenate([before, after], axis=1)
-            columns = []
+            columns = [index_columns(rows_ref[z, begin + n : begin + n + 1, :], 256) for n in range(group)]
+            picked = dot(sides[z], jnp.concatenate(columns, axis=1)).astype(BF)
             for n in range(group):
-                columns.append(index_columns(rows_ref[z, pl.ds(chunk * group + n, 1), :], 256))
-            picked = dot(side, jnp.concatenate(columns, axis=1)).astype(BF)
-            for n in range(group):
-                row = pl.multiple_of((chunk * group + n) * height, height)
-                picked_ref[pl.ds(row, height), z * PAIR : (z + 1) * PAIR] = picked[
+                row = (begin + n) * height
+                picked_ref[row : row + height, z * PAIR : (z + 1) * PAIR] = picked[
                     :, n * PAIR : (n + 1) * PAIR
                 ]
-        return carry
-
-    lax.fori_loop(0, half_slots // group, gather, 0)
+
     both = dot(weight_ref[...], picked_ref[...])
     low = iota((height, PAIR), 1) < LAYER
     first = both[:height, :PAIR] + rolled(both[height:, :PAIR], LAYER)
@@ -536,18 +536,25 @@
 ):
     orbits = orbitals_ref.shape[0]
     rank = basis_ref.shape[0]
-    hartree = sum_ref[0].astype(F32) + other_sum_ref[0].astype(F32)
-    total = total_ref[...].astype(F32) + other_total_ref[...].astype(F32)
-    for o in range(orbits):
-        rest = (total - coeffs_ref[o * rank : (o + 1) * rank].astype(F32)).astype(BF)
-        gap = hartree - near_ref[0, :, o * PAIR : (o + 1) * PAIR] + dot_tn(basis_ref[...], rest)
-        value = orbitals_ref[o]
-        out_ref[o] = value - relax_step * turned(gap) * value
+    for pair in range(near_ref.shape[0]):
+        lanes = slice(pair * PAIR, (pair + 1) * PAIR)
+        hartree = sum_ref[pair].astype(F32) + other_sum_ref[pair].astype(F32)
+        total = total_ref[:, lanes].astype(F32) + other_total_ref[:, lanes].astype(F32)
+        for o in range(orbits):
+            rest = (total - coeffs_ref[o * rank : (o + 1) * rank, lanes].astype(F32)).astype(BF)
+            gap = hartree - near_ref[pair, :, o * PAIR : (o + 1) * PAIR] + dot_tn(basis_ref[...], rest)
+            value = orbitals_ref[o, lanes]
+            out_ref[o, lanes] = value - relax_step * turned(gap) * value
 
 
 def swap(values, axis, bit):
     count = lax.axis_size(axis)
     return lax.ppermute(values, axis, [(i, i ^ bit) for i in range(count)])
+
+
+def step_along(values, distance, devices):
+    pairs = [(i, i + distance) for i in range(devices) if 0 <= i + distance < devices]
+    return lax.ppermute(values, "space", pairs)
 
 
 def shards(
@@ -575,10 +582,10 @@
     assert height == 128 and leaves == 1024 and 2 * count - 1 <= 128
     assert devices & (devices - 1) == 0 and groups == 4
     place = lax.axis_index("space").astype(jnp.int32).reshape(1)
-    message = wide + 5 * height
+    message = wide + 6 * height
     smem = pl.BlockSpec(memory_space=pltpu.SMEM)
 
-    dense, whole, odd, to_left, to_right, cubes = pl.pallas_call(
+    dense, whole, odd, to_left, to_right = pl.pallas_call(
         moments_kernel,
         in_specs=[smem] + [pl.BlockSpec()] * 3,
         out_shape=(
@@ -587,18 +594,21 @@
             jax.ShapeDtypeStruct((pairs + 1, height, PAIR), BF),
             jax.ShapeDtypeStruct((message, PAIR), BF),
             jax.ShapeDtypeStruct((message, PAIR), BF),
-            jax.ShapeDtypeStruct((height, 128), BF),
         ),
         compiler_params=WIDE_MEMORY,
         name="moments",
-    )(place, orbitals, leaf_basis, transfer)
-
-    from_left = lax.ppermute(to_right, "space", [(i, i + 1) for i in range(devices - 1)])
-    from_right = lax.ppermute(to_left, "space", [(i + 1, i) for i in range(devices - 1)])
-    bit = 1
-    while bit < devices:
+    )(place, orbitals, leaf_basis, transfer.reshape(-1, rank))
+
+    from_left = step_along(to_right, 1, devices)
+    from_right = step_along(to_left, -1, devices)
+    cube_at = message - height
+    beside = jnp.where(place[0] % 2 == 0, from_right[cube_at:], from_left[cube_at:])
+    cubes = to_left[cube_at:] + beside
+    bit = 2
+    while 2 * bit < devices:
         cubes = cubes + swap(cubes, "space", bit)
         bit *= 2
+    cubes = (cubes, swap(cubes, "space", bit))
 
     weight = pl.pallas_call(
         widen_kernel,
@@ -619,8 +629,7 @@
         (dense, dense),
         (block(lambda i: (0, i)), block(lambda i: (0, i + 1))),
         place,
-        near_source,
-        None,
+        near_source.T,
         None,
     )
     near, near_sum = near_call(
@@ -640,9 +649,8 @@
             block(lambda i: (0, 0)),
         ),
         place,
-        near_source,
+        near_source.T,
         near,
-        None,
     )
     near_chip = near_sum + swap(near_sum, "orb", 1)
 
@@ -661,17 +669,18 @@
             box(base + 3),
             box(base + 4),
             full((height, 128)),
+            full((height, 128)),
             full(weight.shape),
             full(transfer.shape),
             full(pair_transfer.shape),
             full(coarse_coupling.shape),
-            full(far_mid.shape),
+            full(far_mid.T.shape),
             full(far_top.shape),
         ],
         out_specs=full((height, leaves)),
         out_shape=jax.ShapeDtypeStruct((height, leaves), F32),
         scratch_shapes=[
-            pltpu.VMEM((2, 128, 128), F32),
+            pltpu.VMEM((128, 128), F32),
             pltpu.VMEM((2, 128, 128), F32),
             pltpu.VMEM((slots * height, 256), BF),
         ],
@@ -685,23 +694,23 @@
         from_left,
         from_right,
         from_right,
-        cubes,
+        *cubes,
         weight,
         transfer,
         pair_transfer,
         coarse_coupling,
-        far_mid,
+        far_mid.T,
         far_top,
     )
     near_other = swap(near_chip, "orb", 2)
 
-    edge = lambda: pl.BlockSpec((3 * height, PAIR), lambda i: (0, 0))
+    edge = lambda: full(from_left.shape)
     coeffs, coeff_sum = pl.pallas_call(
         functools.partial(leaf_kernel, pairs),
         grid=(pairs,),
         in_specs=[
             smem,
-            pl.BlockSpec((PAIR, slots), lambda i: (i, 0)),
+            pl.BlockSpec((slots, PAIR), lambda i: (0, i)),
             full(whole.shape),
             full(odd.shape),
             edge(),
@@ -720,8 +729,7 @@
         scratch_shapes=[
             pltpu.VMEM((pairs + 2, height, PAIR), BF),
             pltpu.VMEM((pairs + 3, height, PAIR), BF),
-            pltpu.VMEM((PAIR, 128), F32),
-            pltpu.VMEM((128, PAIR), F32),
+            pltpu.VMEM((slots + 4, PAIR), F32),
             pltpu.VMEM((2, slots // 2 + 2, PAIR), F32),
             pltpu.VMEM((slots // 2 * height, 2 * PAIR), BF),
         ],
@@ -729,29 +737,30 @@
         name="leaf",
     )(
         place,
-        far_leaf,
+        far_leaf.T,
         whole,
         odd,
-        from_left[wide : wide + 3 * height],
-        from_right[wide : wide + 3 * height],
+        from_left,
+        from_right,
         weight,
         down,
     )
     coeff_chip = coeff_sum + swap(coeff_sum, "orb", 1)
     coeff_other = swap(coeff_chip, "orb", 2)
 
-    per_pair = pl.BlockSpec((1, points, PAIR), lambda i: (i, 0, 0))
-    per_rank = pl.BlockSpec((rank, PAIR), lambda i: (0, i))
-    per_leaf = pl.BlockSpec((orbits, PAIR, points), lambda i: (0, i, 0))
+    batch = 2
+    per_pair = pl.BlockSpec((batch, points, PAIR), lambda i: (i, 0, 0))
+    per_rank = pl.BlockSpec((rank, batch * PAIR), lambda i: (0, i))
+    per_leaf = pl.BlockSpec((orbits, batch * PAIR, points), lambda i: (0, i, 0))
     return pl.pallas_call(
         final_kernel,
-        grid=(pairs,),
+        grid=(pairs // batch,),
         in_specs=[
             per_leaf,
-            pl.BlockSpec((1, points, orbits * PAIR), lambda i: (i, 0, 0)),
+            pl.BlockSpec((batch, points, orbits * PAIR), lambda i: (i, 0, 0)),
             per_pair,
             per_pair,
-            pl.BlockSpec((height, PAIR), lambda i: (0, i)),
+            pl.BlockSpec((height, batch * PAIR), lambda i: (0, i)),
             per_rank,
             per_rank,
             full(leaf_basis.shape),
@@ -777,6 +786,7 @@
         P(),
         P(),
     )
+
     return jax.shard_map(
         shards, mesh=mesh, in_specs=placed, out_specs=P("orb", "space", None), check_vma=False
     )

time: 152 us -> 106 us (0.70)
  Pallas kernels: 107 us -> 70.7 us
  local copies, waits for them, and re-layouts: 11 us -> 5.77 us
  starting transfers between devices: 17.4 us -> 15.1 us
  waiting for transfers between devices: 12.5 us -> 10.6 us
    pallas_call x1, Pallas kernels: 35.1 us -> 21.1 us  [shards(): pl.pallas_call(functools.partial(leaf_kernel, pairs), grid=(pairs,), in_s...]
    pallas_call x2, Pallas kernels: 38.9 us -> 25.1 us  [near_call(): pl.pallas_call(kernel, grid=(steps,), in_specs=in_specs, out_specs=(pl.Bl...]
    pallas_call x1, Pallas kernels: 14.7 us -> 10.4 us  [shards(): pl.pallas_call(functools.partial(tree_kernel, count, leaves, rank), grid=...]
    slice x2 -> x0, local copies, waits for them, and re-layouts: 3.06 us -> none  [the longest x1 1.53 us: shards(): from_right[wide:wide + 3 * height]]
    pallas_call x1, Pallas kernels: 7.36 us -> 5.06 us  [shards(): pl.pallas_call(moments_kernel, in_specs=[smem] + [pl.BlockSpec()] * 3, ou...]
    unnamed x26 -> x19, local copies, waits for them, and re-layouts: 7.91 us -> 5.77 us
    pallas_call x1, Pallas kernels: 7.26 us -> 5.14 us  [shards(): pl.pallas_call(final_kernel, grid=(pairs // batch,), in_specs=[per_leaf,...]
    ppermute x7 -> x6, starting transfers between devices: 11 us -> 8.91 us  [swap(): return lax.ppermute(values, axis, [(i, i ^ bit) for i in range(count)])]
  transfers between devices with their start and end apart: 9 -> 8, of which waited for: 5 -> 4; matrix products, arithmetic and copies ran while one was open for 7% -> 5% of each run, Pallas kernels for 54% -> 49%
where the time goes in v2:
time: 106 us; the launch traced here: 105 us
  Pallas kernels  70.7 us (67%)
  starting transfers between devices  15.1 us (14%)
  waiting for transfers between devices  10.6 us (10%)
  local copies, waits for them, and re-layouts  5.77 us (5%)
  other arithmetic  2.93 us (3%)
    pallas_call x2, Pallas kernels, near_call(): pl.pallas_call(kernel, grid=(steps,), in_specs=in_specs, out_specs=(pl.Bl...  25.1 us
    pallas_call x1, Pallas kernels, shards(): pl.pallas_call(functools.partial(leaf_kernel, pairs), grid=(pairs,), in_s...  21.1 us
    ppermute x6, waiting for transfers between devices, swap(): return lax.ppermute(values, axis, [(i, i ^ bit) for i in range(count)])  10.5 us
    pallas_call x1, Pallas kernels, shards(): pl.pallas_call(functools.partial(tree_kernel, count, leaves, rank), grid=...  10.4 us
    ppermute x6, starting transfers between devices, swap(): return lax.ppermute(values, axis, [(i, i ^ bit) for i in range(count)])  8.91 us
    ppermute x2, starting transfers between devices, step_along(): return lax.ppermute(values, 'space', pairs)  6.2 us
    unnamed x19, local copies, waits for them, and re-layouts  5.77 us
    pallas_call x1, Pallas kernels, shards(): pl.pallas_call(final_kernel, grid=(pairs // batch,), in_specs=[per_leaf,...  5.14 us
  transfers between devices with their start and end apart: 8, of which 4 were waited for; matrix products, arithmetic and copies ran while one was open for 5% of the time, Pallas kernels for 49%

profile of v2, /device:TPU:0, one launch (start us, length us, event | category | flops | bytes accessed | tf_op | source)
XLA Modules:
  0.0 105.2 jit_solution(15832544463259017308)
XLA Ops:
  0.0 5.1 %moments.1 = (bf16[512,896]{1,0:T(8,128)(2,1)}, bf16[8,128,128]{2,1,0:T(8,128)(2,1)}, bf16[9,128,128]{2,1,0:T(8,128)(2,1)}, bf16[1280,128]{1,0:T(8,128)(2,1)}, bf16[1280,128]{1,0:T(8,128)(2,1)}) custom-call(s32[1]{0:T(128)} %bitcast.place_ref, f32[2,1024,256]{2,1,0:T(8,128)} %orbitals_ref.3, bf16[64,256]{1,0:T(8,128)(2,1)} %basis_ref.3, bf16[512,64]{1,0:T(8,128)(2,1)} %bitcast.5), custom_call_target="tpu_custom_call" | custom-call | tf_op jit(solution)/shard_map/moments/pallas_call | solution.py:588
  5.1 4.9 %collective-permute-start = (bf16[1280,128]{1,0:T(8,128)(2,1)}, bf16[1280,128]{1,0:T(8,128)(2,1)S(1)}, u32[]{:S(2)}, u32[]{:S(2)}) collective-permute-start(bf16[1280,128]{1,0:T(8,128)(2,1)} %get-tuple-element.18.right_ref), channel_id=1, source_target_pairs={{0,4},{4,8},{8,12},{12,16},{16,20},{20,24},{24,28},{1,5},{5,9},{9,... | collective-permute-start | bytes 983048 | tf_op jit(solution)/shard_map/ppermute | solution.py:557
  10.0 1.3 %collective-permute-start.1 = (bf16[1280,128]{1,0:T(8,128)(2,1)}, bf16[1280,128]{1,0:T(8,128)(2,1)S(1)}, u32[]{:S(2)}, u32[]{:S(2)}) collective-permute-start(bf16[1280,128]{1,0:T(8,128)(2,1)} %get-tuple-element.17.left_ref.own_mid_ref.own_top_ref), channel_id=1, source_target_pairs={{4,0},{8,4},{12,8},{16,12},{20,16},{24,20},{28,24},{5,1},{9,5},{13... | collective-permute-start | bytes 983048 | tf_op jit(solution)/shard_map/ppermute | solution.py:557
  11.3 16.6 %shard_map.109 = (f32[8,256,256]{2,1,0:T(8,128)}, bf16[8,256,128]{2,1,0:T(8,128)(2,1)}) custom-call(s32[1]{0:T(128)} %bitcast.place_ref, s32[27,1024]{1,0:T(8,128)} %bitcast.8, bf16[512,896]{1,0:T(8,128)(2,1)} %get-tuple-element.16.early_ref.late_ref.first_ref.last_ref, bf16[512,896]{1,0:T(8,128)(2,1)} %get-tuple-element.16.early_ref.late_ref.first_ref.last_ref, ...), custom_call_target="tpu_custom_call" | custom-call | flops 10871635968 | bytes 5898240 | tf_op jit(solution)/shard_map/pallas_call | solution.py:263
  27.9 0.7 copy-done
  28.7 8.5 %shard_map.110 = (f32[8,256,256]{2,1,0:T(8,128)}, bf16[8,256,128]{2,1,0:T(8,128)(2,1)}) custom-call(s32[1]{0:T(128)} %bitcast.place_ref, s32[27,1024]{1,0:T(8,128)} %bitcast.9, bf16[512,896]{1,0:T(8,128)(2,1)} %get-tuple-element.16.early_ref.late_ref.first_ref.last_ref, ...), custom_call_target="tpu_custom_call", output_to_operand_aliasing={{0}: (9, {}), {1}: (10, {})} | custom-call | flops 3623878656 | bytes 4325376 | tf_op jit(solution)/shard_map/pallas_call | solution.py:263
  37.3 2.1 %collective-permute-done.2 = bf16[8,256,128]{2,1,0:T(8,128)(2,1)S(1)} collective-permute-done((bf16[8,256,128]{2,1,0:T(8,128)(2,1)}, bf16[8,256,128]{2,1,0:T(8,128)(2,1)S(1)}, u32[]{:S(2)}, u32[]{:S(2)}) %collective-permute-start.2) | collective-permute-done | bytes 524320 | tf_op jit(solution)/shard_map/ppermute | solution.py:552
  39.4 1.2 %add.16.sum_ref = bf16[8,256,128]{2,1,0:T(8,128)(2,1)S(1)} add(bf16[8,256,128]{2,1,0:T(8,128)(2,1)} %get-tuple-element.22, bf16[8,256,128]{2,1,0:T(8,128)(2,1)S(1)} %collective-permute-done.2) | non-fusion elementwise | flops 262144 | bytes 1572864 | tf_op jit(solution)/shard_map/add | solution.py:655
  40.6 1.6 %collective-permute-start.3 = (bf16[8,256,128]{2,1,0:T(8,128)(2,1)S(1)}, bf16[8,256,128]{2,1,0:T(8,128)(2,1)S(1)}, u32[]{:S(2)}, u32[]{:S(2)}) collective-permute-start(bf16[8,256,128]{2,1,0:T(8,128)(2,1)S(1)} %add.16.sum_ref), channel_id=1, source_target_pairs={{0,2},{1,3},{2,0},{3,1},{4,6},{5,7},{6,4},{7,5},{8,10},{9,11},{10,... | collective-permute-start | bytes 1572872 | tf_op jit(solution)/shard_map/ppermute | solution.py:552
  42.2 0.8 fusion
  43.0 3.6 %collective-permute-start.4 = (bf16[128,128]{1,0:T(8,128)(2,1)S(1)}, bf16[128,128]{1,0:T(8,128)(2,1)S(1)}, u32[]{:S(2)}, u32[]{:S(2)}) collective-permute-start(bf16[128,128]{1,0:T(8,128)(2,1)S(1)} %fusion), channel_id=1, source_target_pairs={{0,8},{4,12},{8,0},{12,4},{16,24},{20,28},{24,16},{28,20},{1,9},{5... | collective-permute-start | bytes 98312 | tf_op jit(solution)/shard_map/ppermute | solution.py:552
  46.5 1.9 %collective-permute-done.4 = bf16[128,128]{1,0:T(8,128)(2,1)S(1)} collective-permute-done((bf16[128,128]{1,0:T(8,128)(2,1)S(1)}, bf16[128,128]{1,0:T(8,128)(2,1)S(1)}, u32[]{:S(2)}, u32[]{:S(2)}) %collective-permute-start.4) | collective-permute-done | bytes 32800 | tf_op jit(solution)/shard_map/ppermute | solution.py:552
  48.4 3.1 %collective-permute-start.5 = (bf16[128,128]{1,0:T(8,128)(2,1)S(1)}, bf16[128,128]{1,0:T(8,128)(2,1)S(1)}, u32[]{:S(2)}, u32[]{:S(2)}) collective-permute-start(bf16[128,128]{1,0:T(8,128)(2,1)S(1)} %add.19.cube_ref), channel_id=1, source_target_pairs={{0,16},{4,20},{8,24},{12,28},{16,0},{20,4},{24,8},{28,12},{1,17},{... | collective-permute-start | bytes 98312 | tf_op jit(solution)/shard_map/ppermute | solution.py:552
  51.5 3.5 %copy.14.coupling_ref = bf16[108,64,64]{2,1,0:T(8,128)(2,1)} copy(bf16[108,64,64]{0,2,1:T(8,128)(2,1)S(1)} %copy-done.3) | data formatting | bytes 1769472 | tf_op args[8]
  55.0 4.0 %widen.1.weight_ref = bf16[256,6912]{1,0:T(8,128)(2,1)} custom-call(bf16[108,64,64]{2,1,0:T(8,128)(2,1)} %copy.14.coupling_ref), custom_call_target="tpu_custom_call" | custom-call | tf_op jit(solution)/shard_map/widen/pallas_call | solution.py:613
  59.0 0.6 copy-done.8
  59.6 10.4 %tree.1.down_ref = f32[128,1024]{1,0:T(8,128)} custom-call(s32[1]{0:T(128)} %bitcast.place_ref, bf16[1280,128]{1,0:T(8,128)(2,1)} %get-tuple-element.17.left_ref.own_mid_ref.own_top_ref, bf16[1280,128]{1,0:T(8,128)(2,1)} %get-tuple-element.17.left_ref.own_mid_ref.own_top_ref, bf16[1280,128]{1,0:T(8,128)(2,1)} %copy-done, bf16[1280,128]{1,0:T(8,128)(2,1)} %copy-done, ...), custom_call_target="tpu_custom_call" | custom-call | tf_op jit(solution)/shard_map/tree/pallas_call | solution.py:660
  70.0 21.1 %leaf.1 = (bf16[128,1024]{1,0:T(8,128)(2,1)}, bf16[64,1024]{1,0:T(8,128)(2,1)}) custom-call(s32[1]{0:T(128)} %bitcast.place_ref, s32[108,1024]{1,0:T(8,128)} %bitcast.6, bf16[8,128,128]{2,1,0:T(8,128)(2,1)} %get-tuple-element.23.whole_ref, bf16[9,128,128]{2,1,0:T(8,128)(2,1)} %get-tuple-element.24.odd_ref, bf16[1280,128]{1,0:T(8,128)(2,1)} %copy-done, ...), custom_call_target="tpu_custom_call" | custom-call | tf_op jit(solution)/shard_map/leaf/pallas_call | solution.py:708
  91.1 1.6 %collective-permute-done.6 = bf16[64,1024]{1,0:T(8,128)(2,1)S(1)} collective-permute-done((bf16[64,1024]{1,0:T(8,128)(2,1)}, bf16[64,1024]{1,0:T(8,128)(2,1)S(1)}, u32[]{:S(2)}, u32[]{:S(2)}) %collective-permute-start.6) | collective-permute-done | bytes 131104 | tf_op jit(solution)/shard_map/ppermute | solution.py:552
  92.6 0.9 add.20.total_ref
  93.6 0.6 collective-permute-start.7
  94.2 5.0 %collective-permute-done.7.other_total_ref = bf16[64,1024]{1,0:T(8,128)(2,1)S(1)} collective-permute-done((bf16[64,1024]{1,0:T(8,128)(2,1)S(1)}, bf16[64,1024]{1,0:T(8,128)(2,1)S(1)}, u32[]{:S(2)}, u32[]{:S(2)}) %collective-permute-start.7) | collective-permute-done | bytes 131104 | tf_op jit(solution)/shard_map/ppermute | solution.py:552
  99.2 0.7 copy-done.6
  100.1 5.1 %final.1 = f32[2,1024,256]{2,1,0:T(8,128)} custom-call(f32[2,1024,256]{2,1,0:T(8,128)} %orbitals_ref.3, f32[8,256,256]{2,1,0:T(8,128)} %get-tuple-element.21.near_ref, bf16[8,256,128]{2,1,0:T(8,128)(2,1)} %copy-done.2, bf16[8,256,128]{2,1,0:T(8,128)(2,1)} %copy-done.5, bf16[128,1024]{1,0:T(8,128)(2,1)} %get-tuple-element.25.coeffs_ref, ...), custom_call_target="tpu_custom_call" | custom-call | tf_op jit(solution)/shard_map/final/pallas_call | solution.py:755
  (22 shorter events, 0.4 us)
Async XLA Ops:
  5.1 22.8 %collective-permute-start = (bf16[1280,128]{1,0:T(8,128)(2,1)}, bf16[1280,128]{1,0:T(8,128)(2,1)S(1)}, u32[]{:S(2)}, u32[]{:S(2)}) collective-permute-start(bf16[1280,128]{1,0:T(8,128)(2,1)} %get-tuple-element.18.right_ref), channel_id=1, source_target_pairs={{0,4},{4,8},{8,12},{12,16},{16,20},{20,24},{24,28},{1,5},{5,9},{9,... | collective-permute-start | bytes 983048 | tf_op jit(solution)/shard_map/ppermute | solution.py:557
  10.0 17.9 %collective-permute-start.1 = (bf16[1280,128]{1,0:T(8,128)(2,1)}, bf16[1280,128]{1,0:T(8,128)(2,1)S(1)}, u32[]{:S(2)}, u32[]{:S(2)}) collective-permute-start(bf16[1280,128]{1,0:T(8,128)(2,1)} %get-tuple-element.17.left_ref.own_mid_ref.own_top_ref), channel_id=1, source_target_pairs={{4,0},{8,4},{12,8},{16,12},{20,16},{24,20},{28,24},{5,1},{9,5},{13... | collective-permute-start | bytes 983048 | tf_op jit(solution)/shard_map/ppermute | solution.py:557
  27.9 0.7 copy-start
  27.9 0.8 copy-start.1
  37.2 14.3 %copy-start.3 = (bf16[108,64,64]{0,2,1:T(8,128)(2,1)S(1)}, bf16[108,64,64]{0,2,1:T(8,128)(2,1)}, u32[]{:S(2)}) copy-start(bf16[108,64,64]{0,2,1:T(8,128)(2,1)} %param.19) | copy-start | bytes 2654212
  37.2 2.2 %collective-permute-start.2 = (bf16[8,256,128]{2,1,0:T(8,128)(2,1)}, bf16[8,256,128]{2,1,0:T(8,128)(2,1)S(1)}, u32[]{:S(2)}, u32[]{:S(2)}) collective-permute-start(bf16[8,256,128]{2,1,0:T(8,128)(2,1)} %get-tuple-element.22), channel_id=1, source_target_pairs={{0,1},{1,0},{2,3},{3,2},{4,5},{5,4},{6,7},{7,6},{8,9},{9,8},{10,11... | collective-permute-start | bytes 1572872 | tf_op jit(solution)/shard_map/ppermute | solution.py:552
  40.6 18.4 %copy-start.2 = (bf16[8,256,128]{2,1,0:T(8,128)(2,1)}, bf16[8,256,128]{2,1,0:T(8,128)(2,1)S(1)}, u32[]{:S(2)}) copy-start(bf16[8,256,128]{2,1,0:T(8,128)(2,1)S(1)} %add.16.sum_ref) | copy-start | bytes 1572868
  40.6 58.6 %collective-permute-start.3 = (bf16[8,256,128]{2,1,0:T(8,128)(2,1)S(1)}, bf16[8,256,128]{2,1,0:T(8,128)(2,1)S(1)}, u32[]{:S(2)}, u32[]{:S(2)}) collective-permute-start(bf16[8,256,128]{2,1,0:T(8,128)(2,1)S(1)} %add.16.sum_ref), channel_id=1, source_target_pairs={{0,2},{1,3},{2,0},{3,1},{4,6},{5,7},{6,4},{7,5},{8,10},{9,11},{10,... | collective-permute-start | bytes 1572872 | tf_op jit(solution)/shard_map/ppermute | solution.py:552
  43.0 5.5 %collective-permute-start.4 = (bf16[128,128]{1,0:T(8,128)(2,1)S(1)}, bf16[128,128]{1,0:T(8,128)(2,1)S(1)}, u32[]{:S(2)}, u32[]{:S(2)}) collective-permute-start(bf16[128,128]{1,0:T(8,128)(2,1)S(1)} %fusion), channel_id=1, source_target_pairs={{0,8},{4,12},{8,0},{12,4},{16,24},{20,28},{24,16},{28,20},{1,9},{5... | collective-permute-start | bytes 98312 | tf_op jit(solution)/shard_map/ppermute | solution.py:552
  48.4 10.6 %copy-start.7 = (bf16[128,128]{1,0:T(8,128)(2,1)}, bf16[128,128]{1,0:T(8,128)(2,1)S(1)}, u32[]{:S(2)}) copy-start(bf16[128,128]{1,0:T(8,128)(2,1)S(1)} %add.19.cube_ref) | copy-start | bytes 98308
  48.4 10.6 %collective-permute-start.5 = (bf16[128,128]{1,0:T(8,128)(2,1)S(1)}, bf16[128,128]{1,0:T(8,128)(2,1)S(1)}, u32[]{:S(2)}, u32[]{:S(2)}) collective-permute-start(bf16[128,128]{1,0:T(8,128)(2,1)S(1)} %add.19.cube_ref), channel_id=1, source_target_pairs={{0,16},{4,20},{8,24},{12,28},{16,0},{20,4},{24,8},{28,12},{1,17},{... | collective-permute-start | bytes 98312 | tf_op jit(solution)/shard_map/ppermute | solution.py:552
  59.0 0.6 copy-start.8
  91.1 1.6 %collective-permute-start.6 = (bf16[64,1024]{1,0:T(8,128)(2,1)}, bf16[64,1024]{1,0:T(8,128)(2,1)S(1)}, u32[]{:S(2)}, u32[]{:S(2)}) collective-permute-start(bf16[64,1024]{1,0:T(8,128)(2,1)} %get-tuple-element.26), channel_id=1, source_target_pairs={{0,1},{1,0},{2,3},{3,2},{4,5},{5,4},{6,7},{7,6},{8,9},{9,8},{10,11... | collective-permute-start | bytes 393224 | tf_op jit(solution)/shard_map/ppermute | solution.py:552
  93.6 5.6 %copy-start.4 = (bf16[64,1024]{1,0:T(8,128)(2,1)}, bf16[64,1024]{1,0:T(8,128)(2,1)S(1)}, u32[]{:S(2)}) copy-start(bf16[64,1024]{1,0:T(8,128)(2,1)S(1)} %add.20.total_ref) | copy-start | bytes 393220
  93.6 5.6 %collective-permute-start.7 = (bf16[64,1024]{1,0:T(8,128)(2,1)S(1)}, bf16[64,1024]{1,0:T(8,128)(2,1)S(1)}, u32[]{:S(2)}, u32[]{:S(2)}) collective-permute-start(bf16[64,1024]{1,0:T(8,128)(2,1)S(1)} %add.20.total_ref), channel_id=1, source_target_pairs={{0,2},{1,3},{2,0},{3,1},{4,6},{5,7},{6,4},{7,5},{8,10},{9,11},{10,... | collective-permute-start | bytes 393224 | tf_op jit(solution)/shard_map/ppermute | solution.py:552
  99.2 0.7 copy-start.6
  99.2 0.9 copy-start.5

commit v3 on v2

--- a/solution.py
+++ b/solution.py
@@ -14,7 +14,12 @@
 BF = jnp.bfloat16
 F32 = jnp.float32
 relax_step = 0.1
-WIDE_MEMORY = pltpu.CompilerParams(vmem_limit_bytes=60 * 1024 * 1024)
+MID_RIM = 3 * (SIDE // 2) ** 2
+TOP_RIM = 3 * (SIDE // 4) ** 2
+MID_AT = LAYER
+TOP_AT = MID_AT + MID_RIM
+CUBE_AT = TOP_AT + TOP_RIM
+WIDE_MEMORY = pltpu.CompilerParams(vmem_limit_bytes=40 * 1024 * 1024)
 
 
 def iota(shape, axis):
@@ -95,35 +100,42 @@
 
 
 def moments_kernel(
-    place_ref,
     orbitals_ref,
     basis_ref,
     transfer_ref,
     dense_ref,
+    first_ref,
+    last_ref,
     whole_ref,
     odd_ref,
+    mid_ref,
+    top_ref,
+    cube_ref,
     left_ref,
     right_ref,
 ):
     orbits, leaves, points = orbitals_ref.shape
     rank = basis_ref.shape[0]
-    wide = orbits * points
     basis = basis_ref[...]
     gap = jnp.zeros((LAYER, points), F32)
     moments = []
     moments_odd = []
+    first = []
+    last = []
     for o in range(orbits):
         value = orbitals_ref[o]
         density = value * value
         rows = slice(o * points, (o + 1) * points)
         dense_ref[rows, :] = turned(density[LAYER : leaves - LAYER]).astype(BF)
-        first = jnp.concatenate([gap, density[:LAYER]], axis=0)
-        last = jnp.concatenate([density[leaves - LAYER :], gap], axis=0)
-        left_ref[rows, :] = turned(first).astype(BF)
-        right_ref[rows, :] = turned(last).astype(BF)
+        first.append(density[:LAYER])
+        last.append(density[leaves - LAYER :])
+        first_ref[rows, :] = turned(jnp.concatenate([gap, first[o]], axis=0)).astype(BF)
+        last_ref[rows, :] = turned(jnp.concatenate([last[o], gap], axis=0)).astype(BF)
         moments.append(dot_nt(basis, density.astype(BF)))
         shifted = jnp.concatenate([gap, density, gap], axis=0).astype(BF)
         moments_odd.append(dot_nt(basis, shifted))
+    left_ref[:points, :] = turned(jnp.concatenate(first[::-1], axis=0)).astype(BF)
+    right_ref[:points, :] = turned(jnp.concatenate(last, axis=0)).astype(BF)
     moments = jnp.concatenate(moments, axis=0).astype(BF)
     moments_odd = jnp.concatenate(moments_odd, axis=0).astype(BF)
     blocks = leaves // PAIR
@@ -135,25 +147,45 @@
     mid = up_level(moments, SIDE, transfer, rank)
     top = up_level(mid, SIDE // 2, transfer, rank)
     cube = up_level(top, SIDE // 4, transfer, rank)
-    own = leaves // (LAYER * SIDE)
+    mid_ref[...] = mid
+    top_ref[...] = top
+    cube_ref[...] = cube
+    height = orbits * rank
+    lane = iota((height, 128), 1)
+    mid = mid.astype(F32)
+    top = top.astype(F32)
+    cube = rolled(cube.astype(F32), CUBE_AT)
+    tops = leaves // LAYER
+    left_ref[points : points + height, :] = moments[:, :PAIR]
+    right_ref[points : points + height, :] = moments[:, leaves - PAIR :]
+    for ref, third, mid_lane, top_lane in (
+        (left_ref, moments[:, PAIR : 2 * PAIR], 0, 0),
+        (right_ref, moments_odd[:, leaves - PAIR : leaves], 128 - MID_RIM, tops - TOP_RIM),
+    ):
+        mixed = jnp.where(
+            lane < MID_AT,
+            third.astype(F32),
+            jnp.where(
+                lane < TOP_AT,
+                rolled(mid, (MID_AT - mid_lane) % 128),
+                jnp.where(lane < CUBE_AT, rolled(top, (TOP_AT - top_lane) % 128), cube),
+            ),
+        )
+        ref[points + height :, :] = mixed.astype(BF)
+
+
+def join_kernel(own, place_ref, cube_ref, left_ref, right_ref, out_ref):
+    place = place_ref[0]
     lane = iota((1, 128), 1)
-    from_lane = lane - place_ref[0] * own
-    from_lane = jnp.where((from_lane >= 0) & (from_lane < own), from_lane, -1)
-    cube = dot(cube, pick_matrix(128, from_lane)).astype(BF)
-    height = orbits * rank
-    for ref, pieces in (
-        (left_ref, (moments[:, :PAIR], moments_odd[:, :PAIR], moments_odd[:, PAIR : 2 * PAIR])),
-        (
-            right_ref,
-            (
-                moments[:, leaves - PAIR :],
-                moments_odd[:, leaves - PAIR : leaves],
-                moments_odd[:, leaves:],
-            ),
-        ),
-    ):
-        for n, piece in enumerate(pieces + (mid, top, cube)):
-            ref[wide + n * height : wide + (n + 1) * height, :] = piece
+
+    def placed(values, device, start):
+        which = lane - device * own
+        return dot(values, pick_matrix(128, jnp.where((which >= 0) & (which < own), which + start, -1)))
+
+    even = place % 2 == 0
+    other = jnp.where(even, right_ref[...].astype(F32), left_ref[...].astype(F32)).astype(BF)
+    beside = jnp.where(even, place + 1, place - 1)
+    out_ref[...] = (placed(cube_ref[...], place, 0) + placed(other, beside, CUBE_AT)).astype(BF)
 
 
 def widen_kernel(coupling_ref, out_ref):
@@ -204,86 +236,51 @@
 
     for rows in (slice(0, points // 2), slice(points // 2, points)):
         field = dot(table_ref[rows, :], picked_ref[...])
-        out_ref[0, rows, :] = field
+        out_ref[step, rows, :] = field
         total = field[:, :PAIR]
         for o in range(1, orbits):
             total = total + field[:, o * PAIR : (o + 1) * PAIR]
         sum_ref[0, rows, :] = total.astype(BF)
 
 
-def near_inner_kernel(first, pairs, place_ref, source_ref, early_ref, late_ref, table_hbm, *rest):
-    out_ref, sum_ref, side_ref = rest[-7:-4]
-    pair = first + pl.program_id(0)
+def near_kernel(
+    place_ref,
+    source_ref,
+    early_ref,
+    late_ref,
+    first_ref,
+    last_ref,
+    got_left_ref,
+    got_right_ref,
+    table_hbm,
+    out_ref,
+    sum_ref,
+    side_ref,
+    *scratch,
+):
+    step = pl.program_id(0)
+    pairs = pl.num_programs(0)
+    points = got_left_ref.shape[0]
     side_ref[:, :PAIR] = early_ref[...]
     side_ref[:, PAIR:] = late_ref[...]
-    start = (place_ref[0] * pairs + pair) * PAIR - LAYER
-    near_body(start, source_ref, table_hbm, out_ref, sum_ref, side_ref, *rest[-4:])
-
-
-def near_outer_kernel(
-    pairs, place_ref, source_ref, first_ref, last_ref, left_ref, right_ref, got_left_ref, got_right_ref, table_hbm, *rest
-):
-    out_ref, sum_ref, side_ref = rest[-7:-4]
-    step = pl.program_id(0)
+    low = iota((points, PAIR), 1) < LAYER
 
     @pl.when(step == 0)
     def _():
-        side_ref[:, :PAIR] = left_ref[...] + got_left_ref[...]
-        side_ref[:, PAIR:] = first_ref[...]
-
-    @pl.when(step == 1)
+        got = got_left_ref[...].astype(F32)
+        for o, part in ((0, got), (1, rolled(got, LAYER))):
+            rows = slice(o * points, (o + 1) * points)
+            side_ref[rows, :PAIR] = jnp.where(low, part, first_ref[rows, :].astype(F32)).astype(BF)
+
+    @pl.when(step == pairs - 1)
     def _():
-        side_ref[:, :PAIR] = last_ref[...]
-        side_ref[:, PAIR:] = right_ref[...] + got_right_ref[...]
-
-    start = (place_ref[0] * pairs + step * (pairs - 1)) * PAIR - LAYER
-    near_body(start, source_ref, table_hbm, out_ref, sum_ref, side_ref, *rest[-4:])
-
-
-def near_call(kernel, steps, pair_of, leaves, orbits, table, extra, extra_specs, place, source, before):
-    slots, points, _ = table.shape
-    pairs = leaves // PAIR
-    wide = orbits * points
-    shapes = (
-        jax.ShapeDtypeStruct((pairs, points, orbits * PAIR), F32),
-        jax.ShapeDtypeStruct((pairs, points, PAIR), BF),
-    )
-    in_specs = [
-        pl.BlockSpec(memory_space=pltpu.SMEM),
-        pl.BlockSpec((slots, PAIR), lambda i: (0, pair_of(i))),
-        *extra_specs,
-        pl.BlockSpec(memory_space=pl.ANY),
-    ]
-    operands = [place, source, *extra, table]
-    aliases = {}
-    if before is not None:
-        aliases = {len(operands): 0, len(operands) + 1: 1}
-        operands += list(before)
-        in_specs += [pl.BlockSpec(memory_space=pl.ANY)] * 2
-    return pl.pallas_call(
-        kernel,
-        grid=(steps,),
-        in_specs=in_specs,
-        out_specs=(
-            pl.BlockSpec((1, points, orbits * PAIR), lambda i: (pair_of(i), 0, 0)),
-            pl.BlockSpec((1, points, PAIR), lambda i: (pair_of(i), 0, 0)),
-        ),
-        out_shape=shapes,
-        scratch_shapes=[
-            pltpu.VMEM((wide, 2 * PAIR), BF),
-            pltpu.VMEM((points, slots * points), BF),
-            pltpu.VMEM((32, PAIR), F32),
-            pltpu.VMEM((slots * points, orbits * PAIR), BF),
-            pltpu.SemaphoreType.DMA((slots,)),
-        ],
-        input_output_aliases=aliases,
-        compiler_params=WIDE_MEMORY,
-        cost_estimate=pl.CostEstimate(
-            flops=steps * 4 * slots * points * points * orbits * PAIR,
-            transcendentals=0,
-            bytes_accessed=2 * slots * points * points + steps * 6 * points * orbits * PAIR,
-        ),
-    )(*operands)
+        got = got_right_ref[...].astype(F32)
+        for o, part in ((0, got), (1, rolled(got, LAYER))):
+            rows = slice(o * points, (o + 1) * points)
+            side_ref[rows, PAIR:] = jnp.where(low, last_ref[rows, :].astype(F32), part).astype(BF)
+
+    start = (place_ref[0] * pairs + step) * PAIR - LAYER
+    near_body(start, source_ref, table_hbm, out_ref, sum_ref, side_ref, *scratch)
 
 
 def rolled(values, shift):
@@ -367,12 +364,12 @@
     place_ref,
     own_mid_ref,
     own_top_ref,
-    left_mid_ref,
-    left_top_ref,
-    right_mid_ref,
-    right_top_ref,
+    left_ref,
+    right_ref,
     cube_ref,
-    other_cube_ref,
+    cube_one_ref,
+    cube_two_ref,
+    cube_three_ref,
     weight_ref,
     transfer_ref,
     pair_ref,
@@ -390,30 +387,34 @@
     half_slots = slots // 2
     mids = far_mid_ref.shape[1]
     tops = far_top_ref.shape[0]
-    mid_rim = 3 * (SIDE // 2) ** 2
-    top_rim = 3 * (SIDE // 4) ** 2
+    mid_rim = MID_RIM
+    top_rim = TOP_RIM
     lane = iota((height, 128), 1)
 
     transfer = jnp.concatenate([transfer_ref[n].astype(F32) for n in range(8)], axis=1).astype(BF)
-    cube_coeffs = coarse_part(cube_ref[...] + other_cube_ref[...], coarse_ref, pair_ref, count, rank)
+    cubes = (cube_ref[...] + cube_one_ref[...]) + (cube_two_ref[...] + cube_three_ref[...])
+    cube_coeffs = coarse_part(cubes, coarse_ref, pair_ref, count, rank)
     own = leaves // (LAYER * SIDE)
     lane_row = iota((1, 128), 1)
     cube_own = dot(
         cube_coeffs, pick_matrix(128, jnp.where(lane_row < own, lane_row + place * own, -1))
     ).astype(BF)
 
-    left = left_mid_ref[...].astype(F32)
+    left = left_ref[...].astype(F32)
+    right = right_ref[...].astype(F32)
     middle = rolled(own_mid_ref[...].astype(F32), mid_rim)
-    right = rolled(right_mid_ref[...].astype(F32), mid_rim)
-    left = rolled(left, mid_rim)
     mid_ext = jnp.concatenate(
-        [jnp.where(lane < mid_rim, left, middle), jnp.where(lane < mid_rim, middle, right)], axis=1
+        [
+            jnp.where(lane < mid_rim, rolled(left, 128 - MID_AT), middle),
+            jnp.where(lane < mid_rim, middle, rolled(right, (mid_rim - MID_AT) % 128)),
+        ],
+        axis=1,
     ).astype(BF)
-    left = rolled(left_top_ref[...].astype(F32), 128 + top_rim - tops)
     middle = rolled(own_top_ref[...].astype(F32), top_rim)
-    right = rolled(right_top_ref[...].astype(F32), top_rim + tops)
     top_ext = jnp.where(
-        lane < top_rim, left, jnp.where(lane < top_rim + tops, middle, right)
+        lane < top_rim,
+        rolled(left, 128 - TOP_AT),
+        jnp.where(lane < top_rim + tops, middle, rolled(right, (top_rim + tops - TOP_AT) % 128)),
     ).astype(BF)
 
     wide_ref[...] = jnp.full(wide_ref.shape, -1.0, F32)
@@ -477,52 +478,63 @@
 
     @pl.when(step == 0)
     def _():
-        def piece(ref, n):
-            first = ref.shape[0] - (6 - n) * height
-            return ref[first : first + height]
-
-        even_ref[0] = piece(left_ref, 0)
-        shift_ref[0] = piece(left_ref, 1)
+        first = left_ref.shape[0] - 2 * height
+        left = left_ref[first : first + height]
+        right = right_ref[first : first + height]
+        left_third = left_ref[first + height :].astype(F32)
+        right_third = rolled(right_ref[first + height :].astype(F32), LAYER)
+        left_turned = rolled(left.astype(F32), LAYER)
+        right_turned = rolled(right.astype(F32), LAYER)
+        low = iota((height, PAIR), 1) < LAYER
+        even_ref[0] = left
         for b in range(pairs):
             even_ref[b + 1] = whole_ref[b]
+        even_ref[pairs + 1] = right
+        shift_ref[0] = jnp.where(low, left_third, left_turned).astype(BF)
+        shift_ref[1] = jnp.where(low, left_turned, odd_ref[0].astype(F32)).astype(BF)
         for b in range(1, pairs):
             shift_ref[b + 1] = odd_ref[b]
-        shift_ref[1] = odd_ref[0] + piece(left_ref, 2)
-        shift_ref[pairs + 1] = odd_ref[pairs] + piece(right_ref, 1)
-        even_ref[pairs + 1] = piece(right_ref, 0)
-        shift_ref[pairs + 2] = piece(right_ref, 2)
+        shift_ref[pairs + 1] = jnp.where(low, odd_ref[pairs].astype(F32), right_turned).astype(BF)
+        shift_ref[pairs + 2] = jnp.where(low, right_turned, right_third).astype(BF)
 
     source = source_ref[...]
+    batch = source.shape[1] // PAIR
     layer_bits = LAYER.bit_length() - 1
-    target_layer = (place_ref[0] * pairs + step) * 2 + lax.shift_right_logical(iota(source.shape, 1), layer_bits)
+    target_layer = (place_ref[0] * pairs + step * batch) * 2 + lax.shift_right_logical(iota(source.shape, 1), layer_bits)
     away = lax.shift_right_logical(source, layer_bits) - target_layer
     away = jnp.where(away < 0, away + 3, away)
     turn_ref[:slots, :] = (away * LAYER + (source & (LAYER - 1))).astype(F32)
-    early = turn_ref[:half_slots, :]
-    late = turn_ref[half_slots:slots, :]
     low = iota((half_slots, PAIR), 1) < LAYER
-    rows_ref[0, :half_slots, :] = jnp.where(low, early, rolled(late, LAYER))
-    rows_ref[1, :half_slots, :] = jnp.where(low, rolled(early, LAYER), late)
+    for p in range(batch):
+        early = turn_ref[:half_slots, p * PAIR : (p + 1) * PAIR]
+        late = turn_ref[half_slots:slots, p * PAIR : (p + 1) * PAIR]
+        rows_ref[p, 0, :half_slots, :] = jnp.where(low, early, rolled(late, LAYER))
+        rows_ref[p, 1, :half_slots, :] = jnp.where(low, rolled(late, LAYER), early)
     group = 2
-    sides = (
-        jnp.concatenate([shift_ref[step], even_ref[step + 2]], axis=1),
-        jnp.concatenate([even_ref[step], shift_ref[step + 3]], axis=1),
-    )
-    for begin in range(0, half_slots, group):
-        for z in range(2):
-            columns = [index_columns(rows_ref[z, begin + n : begin + n + 1, :], 256) for n in range(group)]
-            picked = dot(sides[z], jnp.concatenate(columns, axis=1)).astype(BF)
-            for n in range(group):
-                row = (begin + n) * height
-                picked_ref[row : row + height, z * PAIR : (z + 1) * PAIR] = picked[
-                    :, n * PAIR : (n + 1) * PAIR
-                ]
-
-    both = dot(weight_ref[...], picked_ref[...])
-    low = iota((height, PAIR), 1) < LAYER
-    first = both[:height, :PAIR] + rolled(both[height:, :PAIR], LAYER)
-    second = rolled(both[:height, PAIR:], LAYER) + both[height:, PAIR:]
-    coeffs = (jnp.where(low, first, second) + down_ref[...]).astype(BF)
+    low = (iota((height, group * PAIR), 1) & (PAIR - 1)).astype(F32).astype(BF) < jnp.full((), LAYER, BF)
+    for p in range(batch):
+        pair = step * batch + p
+        sides = (
+            jnp.concatenate([shift_ref[pair], even_ref[pair + 2]], axis=1),
+            jnp.concatenate([even_ref[pair], shift_ref[pair + 3]], axis=1),
+        )
+        for begin in range(0, half_slots, group):
+            picked = []
+            for z in range(2):
+                columns = [index_columns(rows_ref[p, z, begin + n : begin + n + 1, :], 256) for n in range(group)]
+                picked.append(dot(sides[z], jnp.concatenate(columns, axis=1)).astype(BF))
+            mixed = (jnp.where(low, picked[0], picked[1]), jnp.where(low, picked[1], picked[0]))
+            for half in range(2):
+                for n in range(group):
+                    row = (begin + n) * height
+                    picked_ref[half, row : row + height, p * PAIR : (p + 1) * PAIR] = mixed[half][
+                        :, n * PAIR : (n + 1) * PAIR
+                    ]
+
+    straight = dot(weight_ref[:height], picked_ref[0])
+    crossed = dot(weight_ref[height:], picked_ref[1])
+    crossed = [rolled(crossed[:, p * PAIR : (p + 1) * PAIR], LAYER) for p in range(batch)]
+    coeffs = (straight + jnp.concatenate(crossed, axis=1) + down_ref[...]).astype(BF)
     coeffs_ref[...] = coeffs
     rank = sum_ref.shape[0]
     total = coeffs[:rank].astype(F32)
@@ -536,9 +548,11 @@
 ):
     orbits = orbitals_ref.shape[0]
     rank = basis_ref.shape[0]
-    for pair in range(near_ref.shape[0]):
-        lanes = slice(pair * PAIR, (pair + 1) * PAIR)
-        hartree = sum_ref[pair].astype(F32) + other_sum_ref[pair].astype(F32)
+    batch = orbitals_ref.shape[1] // PAIR
+    for n in range(batch):
+        lanes = slice(n * PAIR, (n + 1) * PAIR)
+        pair = pl.program_id(0) * batch + n
+        hartree = sum_ref[n].astype(F32) + other_sum_ref[pair].astype(F32)
         total = total_ref[:, lanes].astype(F32) + other_total_ref[:, lanes].astype(F32)
         for o in range(orbits):
             rest = (total - coeffs_ref[o * rank : (o + 1) * rank, lanes].astype(F32)).astype(BF)
@@ -582,33 +596,49 @@
     assert height == 128 and leaves == 1024 and 2 * count - 1 <= 128
     assert devices & (devices - 1) == 0 and groups == 4
     place = lax.axis_index("space").astype(jnp.int32).reshape(1)
-    message = wide + 6 * height
+    own = leaves // (LAYER * SIDE)
+    assert CUBE_AT + own <= 128
+    message = points + 2 * height
     smem = pl.BlockSpec(memory_space=pltpu.SMEM)
-
-    dense, whole, odd, to_left, to_right = pl.pallas_call(
+    square = jax.ShapeDtypeStruct((height, 128), BF)
+
+    dense, first, last, whole, odd, own_mid, own_top, own_cube, to_left, to_right = pl.pallas_call(
         moments_kernel,
-        in_specs=[smem] + [pl.BlockSpec()] * 3,
         out_shape=(
             jax.ShapeDtypeStruct((wide, leaves - PAIR), BF),
+            jax.ShapeDtypeStruct((wide, PAIR), BF),
+            jax.ShapeDtypeStruct((wide, PAIR), BF),
             jax.ShapeDtypeStruct((pairs, height, PAIR), BF),
             jax.ShapeDtypeStruct((pairs + 1, height, PAIR), BF),
+            square,
+            square,
+            square,
             jax.ShapeDtypeStruct((message, PAIR), BF),
             jax.ShapeDtypeStruct((message, PAIR), BF),
         ),
         compiler_params=WIDE_MEMORY,
         name="moments",
-    )(place, orbitals, leaf_basis, transfer.reshape(-1, rank))
+    )(orbitals, leaf_basis, transfer.reshape(-1, rank))
 
     from_left = step_along(to_right, 1, devices)
     from_right = step_along(to_left, -1, devices)
-    cube_at = message - height
-    beside = jnp.where(place[0] % 2 == 0, from_right[cube_at:], from_left[cube_at:])
-    cubes = to_left[cube_at:] + beside
+    mixed = pl.BlockSpec((height, 128), lambda i: (message // height - 1, 0))
+    full = lambda shape: pl.BlockSpec(shape, lambda i: (0,) * len(shape))
+    cubes = pl.pallas_call(
+        functools.partial(join_kernel, own),
+        grid=(1,),
+        in_specs=[smem, full((height, 128)), mixed, mixed],
+        out_specs=full((height, 128)),
+        out_shape=square,
+        compiler_params=WIDE_MEMORY,
+        name="join",
+    )(place, own_cube, from_left, from_right)
     bit = 2
-    while 2 * bit < devices:
+    while 4 * bit < devices:
         cubes = cubes + swap(cubes, "space", bit)
         bit *= 2
-    cubes = (cubes, swap(cubes, "space", bit))
+    assert 4 * bit == devices
+    cubes = [cubes] + [swap(cubes, "space", n * bit) for n in (1, 2, 3)]
 
     weight = pl.pallas_call(
         widen_kernel,
@@ -618,58 +648,47 @@
     )(coupling)
 
     block = lambda which: pl.BlockSpec((wide, PAIR), which)
-    inner = pairs - 2
-    near = near_call(
-        functools.partial(near_inner_kernel, 1, pairs),
-        inner,
-        lambda i: i + 1,
-        leaves,
-        orbits,
-        near_table,
-        (dense, dense),
-        (block(lambda i: (0, i)), block(lambda i: (0, i + 1))),
-        place,
-        near_source.T,
-        None,
-    )
-    near, near_sum = near_call(
-        functools.partial(near_outer_kernel, pairs),
-        2,
-        lambda i: i * (pairs - 1),
-        leaves,
-        orbits,
-        near_table,
-        (dense, dense, to_left, to_right, from_left, from_right),
-        (
-            block(lambda i: (0, 0)),
-            block(lambda i: (0, inner)),
-            block(lambda i: (0, 0)),
-            block(lambda i: (0, 0)),
-            block(lambda i: (0, 0)),
-            block(lambda i: (0, 0)),
+    near_slots = near_table.shape[0]
+    in_vmem = pl.BlockSpec(memory_space=pltpu.VMEM)
+    near, near_sum = pl.pallas_call(
+        near_kernel,
+        grid=(pairs,),
+        in_specs=[
+            smem,
+            pl.BlockSpec((near_slots, PAIR), lambda i: (0, i)),
+            block(lambda i: (0, jnp.maximum(i - 1, 0))),
+            block(lambda i: (0, jnp.minimum(i, pairs - 2))),
+            *[block(lambda i: (0, 0))] * 2,
+            *[pl.BlockSpec((points, PAIR), lambda i: (0, 0))] * 2,
+            pl.BlockSpec(memory_space=pl.ANY),
+        ],
+        out_specs=(in_vmem, pl.BlockSpec((1, points, PAIR), lambda i: (i, 0, 0))),
+        out_shape=(
+            jax.ShapeDtypeStruct((pairs, points, orbits * PAIR), F32),
+            jax.ShapeDtypeStruct((pairs, points, PAIR), BF),
         ),
-        place,
-        near_source.T,
-        near,
-    )
+        scratch_shapes=[
+            pltpu.VMEM((wide, 2 * PAIR), BF),
+            pltpu.VMEM((points, near_slots * points), BF),
+            pltpu.VMEM((32, PAIR), F32),
+            pltpu.VMEM((near_slots * points, orbits * PAIR), BF),
+            pltpu.SemaphoreType.DMA((near_slots,)),
+        ],
+        compiler_params=WIDE_MEMORY,
+        name="near",
+    )(place, near_source.T, dense, dense, first, last, from_left, from_right, near_table)
     near_chip = near_sum + swap(near_sum, "orb", 1)
 
-    box = lambda n: pl.BlockSpec((height, 128), lambda i: (n, 0))
-    base = wide // height
-    full = lambda shape: pl.BlockSpec(shape, lambda i: (0,) * len(shape))
     down = pl.pallas_call(
         functools.partial(tree_kernel, count, leaves, rank),
         grid=(1,),
         in_specs=[
             smem,
-            box(base + 3),
-            box(base + 4),
-            box(base + 3),
-            box(base + 4),
-            box(base + 3),
-            box(base + 4),
             full((height, 128)),
             full((height, 128)),
+            mixed,
+            mixed,
+            *[full((height, 128))] * 4,
             full(weight.shape),
             full(transfer.shape),
             full(pair_transfer.shape),
@@ -688,11 +707,9 @@
         name="tree",
     )(
         place,
-        to_left,
-        to_left,
+        own_mid,
+        own_top,
         from_left,
-        from_left,
-        from_right,
         from_right,
         *cubes,
         weight,
@@ -707,20 +724,20 @@
     edge = lambda: full(from_left.shape)
     coeffs, coeff_sum = pl.pallas_call(
         functools.partial(leaf_kernel, pairs),
-        grid=(pairs,),
+        grid=(pairs // 2,),
         in_specs=[
             smem,
-            pl.BlockSpec((slots, PAIR), lambda i: (0, i)),
+            pl.BlockSpec((slots, 2 * PAIR), lambda i: (0, i)),
             full(whole.shape),
             full(odd.shape),
             edge(),
             edge(),
             full(weight.shape),
-            pl.BlockSpec((height, PAIR), lambda i: (0, i)),
+            pl.BlockSpec((height, 2 * PAIR), lambda i: (0, i)),
         ],
         out_specs=(
-            pl.BlockSpec((height, PAIR), lambda i: (0, i)),
-            pl.BlockSpec((rank, PAIR), lambda i: (0, i)),
+            pl.BlockSpec((height, 2 * PAIR), lambda i: (0, i)),
+            pl.BlockSpec((rank, 2 * PAIR), lambda i: (0, i)),
         ),
         out_shape=(
             jax.ShapeDtypeStruct((height, leaves), BF),
@@ -729,9 +746,9 @@
         scratch_shapes=[
             pltpu.VMEM((pairs + 2, height, PAIR), BF),
             pltpu.VMEM((pairs + 3, height, PAIR), BF),
-            pltpu.VMEM((slots + 4, PAIR), F32),
-            pltpu.VMEM((2, slots // 2 + 2, PAIR), F32),
-            pltpu.VMEM((slots // 2 * height, 2 * PAIR), BF),
+            pltpu.VMEM((slots + 4, 2 * PAIR), F32),
+            pltpu.VMEM((2, 2, slots // 2 + 2, PAIR), F32),
+            pltpu.VMEM((2, slots // 2 * height, 2 * PAIR), BF),
         ],
         compiler_params=WIDE_MEMORY,
         name="leaf",
@@ -757,9 +774,9 @@
         grid=(pairs // batch,),
         in_specs=[
             per_leaf,
-            pl.BlockSpec((batch, points, orbits * PAIR), lambda i: (i, 0, 0)),
+            in_vmem,
             per_pair,
-            per_pair,
+            in_vmem,
             pl.BlockSpec((height, batch * PAIR), lambda i: (0, i)),
             per_rank,
             per_rank,

time: 106 us -> 87.3 us (0.82)
  Pallas kernels: 70.7 us -> 48.3 us
  local copies, waits for them, and re-layouts: 5.77 us -> 11.1 us
  waiting for transfers between devices: 10.6 us -> 13.8 us
  other arithmetic: 2.93 us -> 0.17 us
  starting transfers between devices: 15.1 us -> 13.3 us
    pallas_call x4, Pallas kernels: 51.2 us -> 36.3 us  [the longest x1 19.7 us: shards(): pl.pallas_call(near_kernel, grid=(pairs,), in_specs=[smem, pl.BlockSpec((...]
    ppermute x2, waiting for transfers between devices: 0.01 us -> 5.56 us  [step_along(): return lax.ppermute(values, 'space', pairs)]
    unnamed x19 -> x35, local copies, waits for them, and re-layouts: 5.77 us -> 11.1 us
    pallas_call x1, Pallas kernels: 3.99 us -> 0.76 us  [shards(): pl.pallas_call(widen_kernel, out_shape=jax.ShapeDtypeStruct((2 * height,...]
    ppermute x6 -> x7, waiting for transfers between devices: 10.5 us -> 8.26 us  [swap(): return lax.ppermute(values, axis, [(i, i ^ bit) for i in range(count)])]
    pallas_call x1, Pallas kernels: 10.4 us -> 8.14 us  [shards(): pl.pallas_call(functools.partial(tree_kernel, count, leaves, rank), grid=...]
    pallas_call x1, Pallas kernels: 5.14 us -> 3.06 us  [shards(): pl.pallas_call(final_kernel, grid=(pairs // batch,), in_specs=[per_leaf,...]
    ppermute x6 -> x7, starting transfers between devices: 8.91 us -> 7.08 us  [swap(): return lax.ppermute(values, axis, [(i, i ^ bit) for i in range(count)])]
  transfers between devices with their start and end apart: 8 -> 9, of which waited for: 4 -> 5; matrix products, arithmetic and copies ran while one was open for 5% -> 4% of each run, Pallas kernels for 49% -> 27%
where the time goes in v3:
time: 87.3 us; the launch traced here: 86.9 us
  Pallas kernels  48.3 us (55%)
  waiting for transfers between devices  13.8 us (16%)
  starting transfers between devices  13.3 us (15%)
  local copies, waits for them, and re-layouts  11.1 us (13%)
    pallas_call x1, Pallas kernels, shards(): pl.pallas_call(near_kernel, grid=(pairs,), in_specs=[smem, pl.BlockSpec((...  19.7 us
    pallas_call x1, Pallas kernels, shards(): pl.pallas_call(functools.partial(leaf_kernel, pairs), grid=(pairs // 2,),...  14.1 us
    unnamed x35, local copies, waits for them, and re-layouts  11.1 us
    ppermute x7, waiting for transfers between devices, swap(): return lax.ppermute(values, axis, [(i, i ^ bit) for i in range(count)])  8.26 us
    pallas_call x1, Pallas kernels, shards(): pl.pallas_call(functools.partial(tree_kernel, count, leaves, rank), grid=...  8.14 us
    ppermute x7, starting transfers between devices, swap(): return lax.ppermute(values, axis, [(i, i ^ bit) for i in range(count)])  7.08 us
    ppermute x2, starting transfers between devices, step_along(): return lax.ppermute(values, 'space', pairs)  6.19 us
    ppermute x2, waiting for transfers between devices, step_along(): return lax.ppermute(values, 'space', pairs)  5.56 us
  transfers between devices with their start and end apart: 9, of which 5 were waited for; matrix products, arithmetic and copies ran while one was open for 4% of the time, Pallas kernels for 27%

profile of v3, /device:TPU:0, one launch (start us, length us, event | category | flops | bytes accessed | tf_op | source)
XLA Modules:
  0.0 86.9 jit_solution(11992991993596278225)
XLA Ops:
  0.0 1.6 %copy-done = f32[2,1024,256]{2,1,0:T(8,128)S(1)} copy-done((f32[2,1024,256]{2,1,0:T(8,128)S(1)}, f32[2,1024,256]{2,1,0:T(8,128)}, u32[]{:S(2)}) %copy-start) | copy-done | bytes 2097176
  1.6 0.9 %copy-done.5 = bf16[8,64,64]{2,1,0:T(8,128)(2,1)S(1)} copy-done((bf16[8,64,64]{2,1,0:T(8,128)(2,1)S(1)}, bf16[8,64,64]{2,1,0:T(8,128)(2,1)}, u32[]{:S(2)}) %copy-start.5) | copy-done | bytes 65560
  2.5 0.8 copy-done.10
  3.3 2.4 %moments.1 = (bf16[512,896]{1,0:T(8,128)(2,1)S(1)}, bf16[512,128]{1,0:T(8,128)(2,1)S(1)}, bf16[512,128]{1,0:T(8,128)(2,1)S(1)}, bf16[8,128,128]{2,1,0:T(8,128)(2...) custom-call(f32[2,1024,256]{2,1,0:T(8,128)S(1)} %copy-done, ...), custom_call_target="tpu_custom_call" | custom-call | tf_op jit(solution)/shard_map/moments/pallas_call | solution.py:605
  5.6 0.7 copy-done.8
  6.3 4.9 %collective-permute-start = (bf16[512,128]{1,0:T(8,128)(2,1)S(1)}, bf16[512,128]{1,0:T(8,128)(2,1)S(1)}, u32[]{:S(2)}, u32[]{:S(2)}) collective-permute-start(bf16[512,128]{1,0:T(8,128)(2,1)S(1)} %get-tuple-element.22), channel_id=1, source_target_pairs={{0,4},{4,8},{8,12},{12,16},{16,20},{20,24},{24,28},{1,5},{5,9},{9,... | collective-permute-start | bytes 393224 | tf_op jit(solution)/shard_map/ppermute | solution.py:571
  11.3 1.3 %collective-permute-start.1 = (bf16[512,128]{1,0:T(8,128)(2,1)S(1)}, bf16[512,128]{1,0:T(8,128)(2,1)S(1)}, u32[]{:S(2)}, u32[]{:S(2)}) collective-permute-start(bf16[512,128]{1,0:T(8,128)(2,1)S(1)} %get-tuple-element.23), channel_id=1, source_target_pairs={{4,0},{8,4},{12,8},{16,12},{20,16},{24,20},{28,24},{5,1},{9,5},{13... | collective-permute-start | bytes 393224 | tf_op jit(solution)/shard_map/ppermute | solution.py:571
  12.6 1.4 %collective-permute-done.got_left_ref.left_ref = bf16[512,128]{1,0:T(8,128)(2,1)S(1)} collective-permute-done((bf16[512,128]{1,0:T(8,128)(2,1)S(1)}, bf16[512,128]{1,0:T(8,128)(2,1)S(1)}, u32[]{:S(2)}, u32[]{:S(2)}) %collective-permute-start) | collective-permute-done | bytes 131104 | tf_op jit(solution)/shard_map/ppermute | solution.py:571
  14.0 4.1 %collective-permute-done.1.got_right_ref.right_ref = bf16[512,128]{1,0:T(8,128)(2,1)S(1)} collective-permute-done((bf16[512,128]{1,0:T(8,128)(2,1)S(1)}, bf16[512,128]{1,0:T(8,128)(2,1)S(1)}, u32[]{:S(2)}, u32[]{:S(2)}) %collective-permute-start.1) | collective-permute-done | bytes 131104 | tf_op jit(solution)/shard_map/ppermute | solution.py:571
  18.1 2.0 %copy-done.2 = bf16[27,256,256]{2,1,0:T(8,128)(2,1)S(1)} copy-done((bf16[27,256,256]{2,1,0:T(8,128)(2,1)S(1)}, bf16[27,256,256]{2,1,0:T(8,128)(2,1)}, u32[]{:S(2)}) %copy-start.2) | copy-done | bytes 3538968
  20.1 19.7 %near.1 = (f32[8,256,256]{2,1,0:T(8,128)S(1)}, bf16[8,256,128]{2,1,0:T(8,128)(2,1)S(1)}) custom-call(s32[1]{0:T(128)} %bitcast.place_ref, s32[27,1024]{1,0:T(8,128)S(1)} %bitcast.7, bf16[512,896]{1,0:T(8,128)(2,1)S(1)} %get-tuple-element.19.early_ref.late_ref, bf16[512,896]{1,0:T(8,128)(2,1)S(1)} %get-tuple-element.19.early_ref.late_ref, ...), custom_call_target="tpu_custom_call" | custom-call | tf_op jit(solution)/shard_map/near/pallas_call | solution.py:653
  39.9 1.3 %copy-done.3 = f32[8,256,256]{2,1,0:T(8,128)} copy-done((f32[8,256,256]{2,1,0:T(8,128)}, f32[8,256,256]{2,1,0:T(8,128)S(1)}, u32[]{:S(2)}) %copy-start.3) | copy-done | bytes 2097176
  41.2 1.9 %collective-permute-done.2 = bf16[8,256,128]{2,1,0:T(8,128)(2,1)S(1)} collective-permute-done((bf16[8,256,128]{2,1,0:T(8,128)(2,1)S(1)}, bf16[8,256,128]{2,1,0:T(8,128)(2,1)S(1)}, u32[]{:S(2)}, u32[]{:S(2)}) %collective-permute-start.2) | collective-permute-done | bytes 524320 | tf_op jit(solution)/shard_map/ppermute | solution.py:566
  43.2 1.6 %collective-permute-start.3 = (bf16[8,256,128]{2,1,0:T(8,128)(2,1)S(1)}, bf16[8,256,128]{2,1,0:T(8,128)(2,1)S(1)}, u32[]{:S(2)}, u32[]{:S(2)}) collective-permute-start(bf16[8,256,128]{2,1,0:T(8,128)(2,1)S(1)} %add.6.sum_ref), channel_id=1, source_target_pairs={{0,2},{1,3},{2,0},{3,1},{4,6},{5,7},{6,4},{7,5},{8,10},{9,11},{10,... | collective-permute-start | bytes 1572872 | tf_op jit(solution)/shard_map/ppermute | solution.py:566
  44.9 4.2 %collective-permute-start.6 = (bf16[128,128]{1,0:T(8,128)(2,1)S(1)}, bf16[128,128]{1,0:T(8,128)(2,1)S(1)}, u32[]{:S(2)}, u32[]{:S(2)}) collective-permute-start(bf16[128,128]{1,0:T(8,128)(2,1)S(1)} %join.1.cube_ref), channel_id=1, source_target_pairs={{0,24},{4,28},{8,16},{12,20},{16,8},{20,12},{24,0},{28,4},{1,25},{... | collective-permute-start | bytes 98312 | tf_op jit(solution)/shard_map/ppermute | solution.py:566
  49.2 0.6 collective-permute-start.4
  49.8 3.8 %copy.12.coupling_ref = bf16[108,64,64]{2,1,0:T(8,128)(2,1)S(1)} copy(bf16[108,64,64]{0,2,1:T(8,128)(2,1)} %param.19) | data formatting | bytes 1769472 | tf_op args[8]
  53.6 0.8 widen.1.weight_ref
  54.5 8.1 %tree.1.down_ref = f32[128,1024]{1,0:T(8,128)S(1)} custom-call(s32[1]{0:T(128)} %bitcast.place_ref, bf16[128,128]{1,0:T(8,128)(2,1)S(1)} %get-tuple-element.28.own_mid_ref, bf16[128,128]{1,0:T(8,128)(2,1)S(1)} %get-tuple-element.29.own_top_ref, bf16[512,128]{1,0:T(8,128)(2,1)S(1)} %collective-permute-done.got_left_ref.left_ref, ...), custom_call_target="tpu_custom_call" | custom-call | tf_op jit(solution)/shard_map/tree/pallas_call | solution.py:682
  62.7 14.1 %leaf.1 = (bf16[128,1024]{1,0:T(8,128)(2,1)S(1)}, bf16[64,1024]{1,0:T(8,128)(2,1)S(1)}) custom-call(s32[1]{0:T(128)} %bitcast.place_ref, s32[108,1024]{1,0:T(8,128)S(1)} %bitcast.6, bf16[8,128,128]{2,1,0:T(8,128)(2,1)S(1)} %copy-done.9, bf16[9,128,128]{2,1,0:T(8,128)(2,1)S(1)} %get-tuple-element.27.odd_ref, ...), custom_call_target="tpu_custom_call" | custom-call | tf_op jit(solution)/shard_map/leaf/pallas_call | solution.py:725
  76.9 1.3 %collective-permute-done.7 = bf16[64,1024]{1,0:T(8,128)(2,1)S(1)} collective-permute-done((bf16[64,1024]{1,0:T(8,128)(2,1)S(1)}, bf16[64,1024]{1,0:T(8,128)(2,1)S(1)}, u32[]{:S(2)}, u32[]{:S(2)}) %collective-permute-start.7) | collective-permute-done | bytes 131104 | tf_op jit(solution)/shard_map/ppermute | solution.py:566
  78.2 0.6 collective-permute-start.8
  78.8 5.0 %collective-permute-done.8.other_total_ref = bf16[64,1024]{1,0:T(8,128)(2,1)S(1)} collective-permute-done((bf16[64,1024]{1,0:T(8,128)(2,1)S(1)}, bf16[64,1024]{1,0:T(8,128)(2,1)S(1)}, u32[]{:S(2)}, u32[]{:S(2)}) %collective-permute-start.8) | collective-permute-done | bytes 131104 | tf_op jit(solution)/shard_map/ppermute | solution.py:566
  83.9 3.1 %final.1 = f32[2,1024,256]{2,1,0:T(8,128)} custom-call(f32[2,1024,256]{2,1,0:T(8,128)S(1)} %copy-done.1, f32[8,256,256]{2,1,0:T(8,128)S(1)} %copy-done.4, bf16[8,256,128]{2,1,0:T(8,128)(2,1)S(1)} %add.6.sum_ref, bf16[8,256,128]{2,1,0:T(8,128)(2,1)S(1)} %collective-permute-done.3.other_sum_ref, bf16[128,1024]{1,0:T(8,128)(2,1)S(1)} %get-tuple-element.31.coeffs_ref, ...), custom_call_target="tpu_custom_call" | custom-call | tf_op jit(solution)/shard_map/final/pallas_call | solution.py:772
  (38 shorter events, 0.5 us)
Async XLA Ops:
  0.0 1.6 %copy-start = (f32[2,1024,256]{2,1,0:T(8,128)S(1)}, f32[2,1024,256]{2,1,0:T(8,128)}, u32[]{:S(2)}) copy-start(f32[2,1024,256]{2,1,0:T(8,128)} %orbitals_ref.3) | copy-start | bytes 6291460
  1.6 0.9 %copy-start.5 = (bf16[8,64,64]{2,1,0:T(8,128)(2,1)S(1)}, bf16[8,64,64]{2,1,0:T(8,128)(2,1)}, u32[]{:S(2)}) copy-start(bf16[8,64,64]{2,1,0:T(8,128)(2,1)} %transfer_ref.1) | copy-start | bytes 196612
  3.3 14.9 %copy-start.12 = (s32[1024,27]{0,1:T(8,128)S(1)}, s32[1024,27]{0,1:T(8,128)}, u32[]{:S(2)}) copy-start(s32[1024,27]{0,1:T(8,128)} %param.12) | copy-start | bytes 331780
  6.3 7.6 %collective-permute-start = (bf16[512,128]{1,0:T(8,128)(2,1)S(1)}, bf16[512,128]{1,0:T(8,128)(2,1)S(1)}, u32[]{:S(2)}, u32[]{:S(2)}) collective-permute-start(bf16[512,128]{1,0:T(8,128)(2,1)S(1)} %get-tuple-element.22), channel_id=1, source_target_pairs={{0,4},{4,8},{8,12},{12,16},{16,20},{20,24},{24,28},{1,5},{5,9},{9,... | collective-permute-start | bytes 393224 | tf_op jit(solution)/shard_map/ppermute | solution.py:571
  11.3 6.9 %collective-permute-start.1 = (bf16[512,128]{1,0:T(8,128)(2,1)S(1)}, bf16[512,128]{1,0:T(8,128)(2,1)S(1)}, u32[]{:S(2)}, u32[]{:S(2)}) collective-permute-start(bf16[512,128]{1,0:T(8,128)(2,1)S(1)} %get-tuple-element.23), channel_id=1, source_target_pairs={{4,0},{8,4},{12,8},{16,12},{20,16},{24,20},{28,24},{5,1},{9,5},{13... | collective-permute-start | bytes 393224 | tf_op jit(solution)/shard_map/ppermute | solution.py:571
  18.1 2.0 %copy-start.2 = (bf16[27,256,256]{2,1,0:T(8,128)(2,1)S(1)}, bf16[27,256,256]{2,1,0:T(8,128)(2,1)}, u32[]{:S(2)}) copy-start(bf16[27,256,256]{2,1,0:T(8,128)(2,1)} %table_hbm.1) | copy-start | bytes 10616836
  39.8 1.3 %copy-start.3 = (f32[8,256,256]{2,1,0:T(8,128)}, f32[8,256,256]{2,1,0:T(8,128)S(1)}, u32[]{:S(2)}) copy-start(f32[8,256,256]{2,1,0:T(8,128)S(1)} %get-tuple-element.24.near_ref) | copy-start | bytes 6291460
  41.2 1.9 %collective-permute-start.2 = (bf16[8,256,128]{2,1,0:T(8,128)(2,1)S(1)}, bf16[8,256,128]{2,1,0:T(8,128)(2,1)S(1)}, u32[]{:S(2)}, u32[]{:S(2)}) collective-permute-start(bf16[8,256,128]{2,1,0:T(8,128)(2,1)S(1)} %get-tuple-element.25), channel_id=1, source_target_pairs={{0,1},{1,0},{2,3},{3,2},{4,5},{5,4},{6,7},{7,6},{8,9},{9,8},{10,11... | collective-permute-start | bytes 1572872 | tf_op jit(solution)/shard_map/ppermute | solution.py:566
  43.2 40.6 %collective-permute-start.3 = (bf16[8,256,128]{2,1,0:T(8,128)(2,1)S(1)}, bf16[8,256,128]{2,1,0:T(8,128)(2,1)S(1)}, u32[]{:S(2)}, u32[]{:S(2)}) collective-permute-start(bf16[8,256,128]{2,1,0:T(8,128)(2,1)S(1)} %add.6.sum_ref), channel_id=1, source_target_pairs={{0,2},{1,3},{2,0},{3,1},{4,6},{5,7},{6,4},{7,5},{8,10},{9,11},{10,... | collective-permute-start | bytes 1572872 | tf_op jit(solution)/shard_map/ppermute | solution.py:566
  44.9 9.4 %collective-permute-start.6 = (bf16[128,128]{1,0:T(8,128)(2,1)S(1)}, bf16[128,128]{1,0:T(8,128)(2,1)S(1)}, u32[]{:S(2)}, u32[]{:S(2)}) collective-permute-start(bf16[128,128]{1,0:T(8,128)(2,1)S(1)} %join.1.cube_ref), channel_id=1, source_target_pairs={{0,24},{4,28},{8,16},{12,20},{16,8},{20,12},{24,0},{28,4},{1,25},{... | collective-permute-start | bytes 98312 | tf_op jit(solution)/shard_map/ppermute | solution.py:566
  49.1 5.2 %collective-permute-start.5 = (bf16[128,128]{1,0:T(8,128)(2,1)S(1)}, bf16[128,128]{1,0:T(8,128)(2,1)S(1)}, u32[]{:S(2)}, u32[]{:S(2)}) collective-permute-start(bf16[128,128]{1,0:T(8,128)(2,1)S(1)} %join.1.cube_ref), channel_id=1, source_target_pairs={{0,16},{4,20},{8,24},{12,28},{16,0},{20,4},{24,8},{28,12},{1,17},{... | collective-permute-start | bytes 98312 | tf_op jit(solution)/shard_map/ppermute | solution.py:566
  49.2 5.3 %collective-permute-start.4 = (bf16[128,128]{1,0:T(8,128)(2,1)S(1)}, bf16[128,128]{1,0:T(8,128)(2,1)}, u32[]{:S(2)}, u32[]{:S(2)}) collective-permute-start(bf16[128,128]{1,0:T(8,128)(2,1)S(1)} %join.1.cube_ref), channel_id=1, source_target_pairs={{0,8},{4,12},{8,0},{12,4},{16,24},{20,28},{24,16},{28,20},{1,9},{5... | collective-permute-start | bytes 98312 | tf_op jit(solution)/shard_map/ppermute | solution.py:566
  53.6 0.9 %copy-start.6 = (bf16[8,64,64]{2,1,0:T(8,128)(2,1)S(1)}, bf16[8,64,64]{2,1,0:T(8,128)(2,1)}, u32[]{:S(2)}) copy-start(bf16[8,64,64]{2,1,0:T(8,128)(2,1)} %transfer_ref.1) | copy-start | bytes 196612
  53.6 0.9 %copy-start.13 = (bf16[4,64,64]{2,1,0:T(8,128)(2,1)S(1)}, bf16[4,64,64]{2,1,0:T(8,128)(2,1)}, u32[]{:S(2)}) copy-start(bf16[4,64,64]{2,1,0:T(8,128)(2,1)} %coarse_ref.1) | copy-start | bytes 98308
  53.6 0.9 %copy-start.14 = (s32[128,108]{0,1:T(8,128)S(1)}, s32[128,108]{0,1:T(8,128)}, u32[]{:S(2)}) copy-start(s32[128,108]{0,1:T(8,128)} %param.14) | copy-start | bytes 165892
  53.6 0.9 %copy-start.15 = (bf16[2,64,64]{2,1,0:T(8,128)(2,1)S(1)}, bf16[2,64,64]{2,1,0:T(8,128)(2,1)}, u32[]{:S(2)}) copy-start(bf16[2,64,64]{2,1,0:T(8,128)(2,1)} %pair_ref.1) | copy-start | bytes 49156
  53.6 0.9 %copy-start.16 = (s32[16,108]{1,0:T(8,128)S(1)}, s32[16,108]{1,0:T(8,128)}, u32[]{:S(2)}) copy-start(s32[16,108]{1,0:T(8,128)} %far_top_ref.1) | copy-start | bytes 20740
  54.5 8.2 %copy-start.7 = (s32[1024,108]{0,1:T(8,128)S(1)}, s32[1024,108]{0,1:T(8,128)}, u32[]{:S(2)}) copy-start(s32[1024,108]{0,1:T(8,128)} %param.13) | copy-start | bytes 1327108
  54.5 8.2 %copy-start.9 = (bf16[8,128,128]{2,1,0:T(8,128)(2,1)S(1)}, bf16[8,128,128]{2,1,0:T(8,128)(2,1)}, u32[]{:S(2)}) copy-start(bf16[8,128,128]{2,1,0:T(8,128)(2,1)} %copy-done.8) | copy-start | bytes 786436
  62.7 21.2 %copy-start.1 = (f32[2,1024,256]{2,1,0:T(8,128)S(1)}, f32[2,1024,256]{2,1,0:T(8,128)}, u32[]{:S(2)}) copy-start(f32[2,1024,256]{2,1,0:T(8,128)} %orbitals_ref.3) | copy-start | bytes 6291460
  62.7 21.2 %copy-start.4 = (f32[8,256,256]{2,1,0:T(8,128)S(1)}, f32[8,256,256]{2,1,0:T(8,128)}, u32[]{:S(2)}) copy-start(f32[8,256,256]{2,1,0:T(8,128)} %copy-done.3) | copy-start | bytes 6291460
  62.7 21.2 %copy-start.11 = (bf16[64,256]{1,0:T(8,128)(2,1)S(1)}, bf16[64,256]{1,0:T(8,128)(2,1)}, u32[]{:S(2)}) copy-start(bf16[64,256]{1,0:T(8,128)(2,1)} %basis_ref.3) | copy-start | bytes 98308
  76.8 1.4 %collective-permute-start.7 = (bf16[64,1024]{1,0:T(8,128)(2,1)S(1)}, bf16[64,1024]{1,0:T(8,128)(2,1)S(1)}, u32[]{:S(2)}, u32[]{:S(2)}) collective-permute-start(bf16[64,1024]{1,0:T(8,128)(2,1)S(1)} %get-tuple-element.32), channel_id=1, source_target_pairs={{0,1},{1,0},{2,3},{3,2},{4,5},{5,4},{6,7},{7,6},{8,9},{9,8},{10,11... | collective-permute-start | bytes 393224 | tf_op jit(solution)/shard_map/ppermute | solution.py:566
  78.2 5.6 %collective-permute-start.8 = (bf16[64,1024]{1,0:T(8,128)(2,1)S(1)}, bf16[64,1024]{1,0:T(8,128)(2,1)S(1)}, u32[]{:S(2)}, u32[]{:S(2)}) collective-permute-start(bf16[64,1024]{1,0:T(8,128)(2,1)S(1)} %add.7.total_ref), channel_id=1, source_target_pairs={{0,2},{1,3},{2,0},{3,1},{4,6},{5,7},{6,4},{7,5},{8,10},{9,11},{10,... | collective-permute-start | bytes 393224 | tf_op jit(solution)/shard_map/ppermute | solution.py:566
  (2 other events, 1.5 us)

commit v4 on v3

--- a/solution.py
+++ b/solution.py
@@ -100,9 +100,9 @@
 
 
 def moments_kernel(
-    orbitals_ref,
-    basis_ref,
-    transfer_ref,
+    orbitals_hbm,
+    basis_hbm,
+    transfer_hbm,
     dense_ref,
     first_ref,
     last_ref,
@@ -113,9 +113,23 @@
     cube_ref,
     left_ref,
     right_ref,
+    orbitals_ref,
+    basis_ref,
+    transfer_ref,
+    sems,
 ):
     orbits, leaves, points = orbitals_ref.shape
     rank = basis_ref.shape[0]
+    fetch_basis = pltpu.make_async_copy(basis_hbm, basis_ref, sems.at[orbits])
+    fetch_transfer = pltpu.make_async_copy(transfer_hbm, transfer_ref, sems.at[orbits + 1])
+    fetches = [
+        pltpu.make_async_copy(orbitals_hbm.at[o], orbitals_ref.at[o], sems.at[o]) for o in range(orbits)
+    ]
+    fetch_basis.start()
+    for fetch in fetches:
+        fetch.start()
+    fetch_transfer.start()
+    fetch_basis.wait()
     basis = basis_ref[...]
     gap = jnp.zeros((LAYER, points), F32)
     moments = []
@@ -123,6 +137,7 @@
     first = []
     last = []
     for o in range(orbits):
+        fetches[o].wait()
         value = orbitals_ref[o]
         density = value * value
         rows = slice(o * points, (o + 1) * points)
@@ -143,6 +158,7 @@
         whole_ref[b] = moments[:, b * PAIR : (b + 1) * PAIR]
     for b in range(blocks + 1):
         odd_ref[b] = moments_odd[:, b * PAIR : (b + 1) * PAIR]
+    fetch_transfer.wait()
     transfer = transfer_ref[...]
     mid = up_level(moments, SIDE, transfer, rank)
     top = up_level(mid, SIDE // 2, transfer, rank)
@@ -600,10 +616,12 @@
     assert CUBE_AT + own <= 128
     message = points + 2 * height
     smem = pl.BlockSpec(memory_space=pltpu.SMEM)
+    in_vmem = pl.BlockSpec(memory_space=pltpu.VMEM)
     square = jax.ShapeDtypeStruct((height, 128), BF)
 
     dense, first, last, whole, odd, own_mid, own_top, own_cube, to_left, to_right = pl.pallas_call(
         moments_kernel,
+        in_specs=[pl.BlockSpec(memory_space=pl.ANY)] * 3,
         out_shape=(
             jax.ShapeDtypeStruct((wide, leaves - PAIR), BF),
             jax.ShapeDtypeStruct((wide, PAIR), BF),
@@ -616,7 +634,13 @@
             jax.ShapeDtypeStruct((message, PAIR), BF),
             jax.ShapeDtypeStruct((message, PAIR), BF),
         ),
-        compiler_params=WIDE_MEMORY,
+        scratch_shapes=[
+            pltpu.VMEM((orbits, leaves, points), F32),
+            pltpu.VMEM((rank, points), BF),
+            pltpu.VMEM((8 * rank, rank), BF),
+            pltpu.SemaphoreType.DMA((orbits + 2,)),
+        ],
+        compiler_params=pltpu.CompilerParams(vmem_limit_bytes=60 * 1024 * 1024),
         name="moments",
     )(orbitals, leaf_basis, transfer.reshape(-1, rank))
 
@@ -649,7 +673,6 @@
 
     block = lambda which: pl.BlockSpec((wide, PAIR), which)
     near_slots = near_table.shape[0]
-    in_vmem = pl.BlockSpec(memory_space=pltpu.VMEM)
     near, near_sum = pl.pallas_call(
         near_kernel,
         grid=(pairs,),

time: 87.3 us -> 88.3 us (1.011)
  Pallas kernels: 48.3 us -> 50 us
  local copies, waits for them, and re-layouts: 11.1 us -> 10.2 us
    pallas_call x1, Pallas kernels: 2.37 us -> 4.94 us  [shards(): pl.pallas_call(moments_kernel, in_specs=[pl.BlockSpec(memory_space=pl.ANY...]
    unnamed x35 -> x41, local copies, waits for them, and re-layouts: 11.1 us -> 10.2 us
  transfers between devices with their start and end apart: 9 -> 9, of which waited for: 5 -> 5; matrix products, arithmetic and copies ran while one was open for 4% -> 4% of each run, Pallas kernels for 27% -> 25%
where the time goes in v4:
time: 88.3 us; the launch traced here: 88 us
  Pallas kernels  50 us (57%)
  waiting for transfers between devices  14 us (16%)
  starting transfers between devices  13.3 us (15%)
  local copies, waits for them, and re-layouts  10.2 us (12%)
    pallas_call x1, Pallas kernels, shards(): pl.pallas_call(near_kernel, grid=(pairs,), in_specs=[smem, pl.BlockSpec((...  19.7 us
    pallas_call x1, Pallas kernels, shards(): pl.pallas_call(functools.partial(leaf_kernel, pairs), grid=(pairs // 2,),...  14.1 us
    unnamed x41, local copies, waits for them, and re-layouts  10.2 us
    ppermute x7, waiting for transfers between devices, swap(): return lax.ppermute(values, axis, [(i, i ^ bit) for i in range(count)])  8.27 us
    pallas_call x1, Pallas kernels, shards(): pl.pallas_call(functools.partial(tree_kernel, count, leaves, rank), grid=...  7.28 us
    ppermute x7, starting transfers between devices, swap(): return lax.ppermute(values, axis, [(i, i ^ bit) for i in range(count)])  7.07 us
    ppermute x2, starting transfers between devices, step_along(): return lax.ppermute(values, 'space', pairs)  6.2 us
    ppermute x2, waiting for transfers between devices, step_along(): return lax.ppermute(values, 'space', pairs)  5.77 us
  transfers between devices with their start and end apart: 9, of which 5 were waited for; matrix products, arithmetic and copies ran while one was open for 4% of the time, Pallas kernels for 25%

profile of v4, /device:TPU:0, one launch (start us, length us, event | category | flops | bytes accessed | tf_op | source)
XLA Modules:
  0.0 88.0 jit_solution(1177573099867180006)
XLA Ops:
  0.0 4.9 %moments.1 = (bf16[512,896]{1,0:T(8,128)(2,1)}, bf16[512,128]{1,0:T(8,128)(2,1)}, bf16[512,128]{1,0:T(8,128)(2,1)}, bf16[8,128,128]{2,1,0:T(8,128)(2,1)}, bf16[9...) custom-call(f32[2,1024,256]{2,1,0:T(8,128)} %orbitals_ref.1, ...), custom_call_target="tpu_custom_call" | custom-call | tf_op jit(solution)/shard_map/moments/pallas_call | solution.py:622
  4.9 4.9 %collective-permute-start = (bf16[512,128]{1,0:T(8,128)(2,1)}, bf16[512,128]{1,0:T(8,128)(2,1)S(1)}, u32[]{:S(2)}, u32[]{:S(2)}) collective-permute-start(bf16[512,128]{1,0:T(8,128)(2,1)} %get-tuple-element.22), channel_id=1, source_target_pairs={{0,4},{4,8},{8,12},{12,16},{16,20},{20,24},{24,28},{1,5},{5,9},{9,... | collective-permute-start | bytes 393224 | tf_op jit(solution)/shard_map/ppermute | solution.py:587
  9.9 1.3 %collective-permute-start.1 = (bf16[512,128]{1,0:T(8,128)(2,1)}, bf16[512,128]{1,0:T(8,128)(2,1)S(1)}, u32[]{:S(2)}, u32[]{:S(2)}) collective-permute-start(bf16[512,128]{1,0:T(8,128)(2,1)} %get-tuple-element.23), channel_id=1, source_target_pairs={{4,0},{8,4},{12,8},{16,12},{20,16},{24,20},{28,24},{5,1},{9,5},{13... | collective-permute-start | bytes 393224 | tf_op jit(solution)/shard_map/ppermute | solution.py:587
  11.2 1.7 %collective-permute-done.got_left_ref.left_ref = bf16[512,128]{1,0:T(8,128)(2,1)S(1)} collective-permute-done((bf16[512,128]{1,0:T(8,128)(2,1)}, bf16[512,128]{1,0:T(8,128)(2,1)S(1)}, u32[]{:S(2)}, u32[]{:S(2)}) %collective-permute-start) | collective-permute-done | bytes 131104 | tf_op jit(solution)/shard_map/ppermute | solution.py:587
  12.9 4.0 %collective-permute-done.1.got_right_ref.right_ref = bf16[512,128]{1,0:T(8,128)(2,1)S(1)} collective-permute-done((bf16[512,128]{1,0:T(8,128)(2,1)}, bf16[512,128]{1,0:T(8,128)(2,1)S(1)}, u32[]{:S(2)}, u32[]{:S(2)}) %collective-permute-start.1) | collective-permute-done | bytes 131104 | tf_op jit(solution)/shard_map/ppermute | solution.py:587
  16.9 1.2 %copy-done.1 = bf16[512,896]{1,0:T(8,128)(2,1)S(1)} copy-done((bf16[512,896]{1,0:T(8,128)(2,1)S(1)}, bf16[512,896]{1,0:T(8,128)(2,1)}, u32[]{:S(2)}) %copy-start.1) | copy-done | bytes 917528
  18.1 2.0 %copy-done.2 = bf16[27,256,256]{2,1,0:T(8,128)(2,1)S(1)} copy-done((bf16[27,256,256]{2,1,0:T(8,128)(2,1)S(1)}, bf16[27,256,256]{2,1,0:T(8,128)(2,1)}, u32[]{:S(2)}) %copy-start.2) | copy-done | bytes 3538968
  20.1 0.9 %copy-done.11 = bf16[512,128]{1,0:T(8,128)(2,1)S(1)} copy-done((bf16[512,128]{1,0:T(8,128)(2,1)S(1)}, bf16[512,128]{1,0:T(8,128)(2,1)}, u32[]{:S(2)}) %copy-start.11) | copy-done | bytes 131096
  21.0 0.9 %copy-done.12 = bf16[512,128]{1,0:T(8,128)(2,1)S(1)} copy-done((bf16[512,128]{1,0:T(8,128)(2,1)S(1)}, bf16[512,128]{1,0:T(8,128)(2,1)}, u32[]{:S(2)}) %copy-start.12) | copy-done | bytes 131096
  21.9 19.7 %near.1 = (f32[8,256,256]{2,1,0:T(8,128)S(1)}, bf16[8,256,128]{2,1,0:T(8,128)(2,1)S(1)}) custom-call(s32[1]{0:T(128)} %bitcast.place_ref, s32[27,1024]{1,0:T(8,128)S(1)} %bitcast.7, bf16[512,896]{1,0:T(8,128)(2,1)S(1)} %copy-done.1, bf16[512,896]{1,0:T(8,128)(2,1)S(1)} %copy-done.1, bf16[512,128]{1,0:T(8,128)(2,1)S(1)} %copy-done.11, ...), custom_call_target="tpu_custom_call" | custom-call | tf_op jit(solution)/shard_map/near/pallas_call | solution.py:676
  41.7 1.3 %copy-done.3 = f32[8,256,256]{2,1,0:T(8,128)} copy-done((f32[8,256,256]{2,1,0:T(8,128)}, f32[8,256,256]{2,1,0:T(8,128)S(1)}, u32[]{:S(2)}) %copy-start.3) | copy-done | bytes 2097176
  43.0 1.9 %collective-permute-done.2 = bf16[8,256,128]{2,1,0:T(8,128)(2,1)S(1)} collective-permute-done((bf16[8,256,128]{2,1,0:T(8,128)(2,1)S(1)}, bf16[8,256,128]{2,1,0:T(8,128)(2,1)S(1)}, u32[]{:S(2)}, u32[]{:S(2)}) %collective-permute-start.2) | collective-permute-done | bytes 524320 | tf_op jit(solution)/shard_map/ppermute | solution.py:582
  45.0 1.6 %collective-permute-start.3 = (bf16[8,256,128]{2,1,0:T(8,128)(2,1)S(1)}, bf16[8,256,128]{2,1,0:T(8,128)(2,1)S(1)}, u32[]{:S(2)}, u32[]{:S(2)}) collective-permute-start(bf16[8,256,128]{2,1,0:T(8,128)(2,1)S(1)} %add.6.sum_ref), channel_id=1, source_target_pairs={{0,2},{1,3},{2,0},{3,1},{4,6},{5,7},{6,4},{7,5},{8,10},{9,11},{10,... | collective-permute-start | bytes 1572872 | tf_op jit(solution)/shard_map/ppermute | solution.py:582
  46.6 0.2 join.1.cube_ref
  46.8 4.2 %collective-permute-start.6 = (bf16[128,128]{1,0:T(8,128)(2,1)S(1)}, bf16[128,128]{1,0:T(8,128)(2,1)S(1)}, u32[]{:S(2)}, u32[]{:S(2)}) collective-permute-start(bf16[128,128]{1,0:T(8,128)(2,1)S(1)} %join.1.cube_ref), channel_id=1, source_target_pairs={{0,24},{4,28},{8,16},{12,20},{16,8},{20,12},{24,0},{28,4},{1,25},{... | collective-permute-start | bytes 98312 | tf_op jit(solution)/shard_map/ppermute | solution.py:582
  51.0 0.6 collective-permute-start.4
  51.6 3.8 %copy.12.coupling_ref = bf16[108,64,64]{2,1,0:T(8,128)(2,1)S(1)} copy(bf16[108,64,64]{0,2,1:T(8,128)(2,1)} %param.19) | data formatting | bytes 1769472 | tf_op args[8]
  55.5 0.8 widen.1.weight_ref
  56.4 7.3 %tree.1.down_ref = f32[128,1024]{1,0:T(8,128)S(1)} custom-call(s32[1]{0:T(128)} %bitcast.place_ref, bf16[128,128]{1,0:T(8,128)(2,1)S(1)} %copy-done.16, bf16[128,128]{1,0:T(8,128)(2,1)S(1)} %copy-done.17, bf16[512,128]{1,0:T(8,128)(2,1)S(1)} %collective-permute-done.got_left_ref.left_ref, ...), custom_call_target="tpu_custom_call" | custom-call | tf_op jit(solution)/shard_map/tree/pallas_call | solution.py:705
  63.7 14.1 %leaf.1 = (bf16[128,1024]{1,0:T(8,128)(2,1)S(1)}, bf16[64,1024]{1,0:T(8,128)(2,1)S(1)}) custom-call(s32[1]{0:T(128)} %bitcast.place_ref, s32[108,1024]{1,0:T(8,128)S(1)} %bitcast.6, bf16[8,128,128]{2,1,0:T(8,128)(2,1)S(1)} %copy-done.8, bf16[9,128,128]{2,1,0:T(8,128)(2,1)S(1)} %copy-done.7, bf16[512,128]{1,0:T(8,128)(2,1)S(1)} %collective-permute-done.got_left_ref.left_ref, ...), custom_call_target="tpu_custom_call" | custom-call | tf_op jit(solution)/shard_map/leaf/pallas_call | solution.py:748
  77.9 1.3 %collective-permute-done.7 = bf16[64,1024]{1,0:T(8,128)(2,1)S(1)} collective-permute-done((bf16[64,1024]{1,0:T(8,128)(2,1)S(1)}, bf16[64,1024]{1,0:T(8,128)(2,1)S(1)}, u32[]{:S(2)}, u32[]{:S(2)}) %collective-permute-start.7) | collective-permute-done | bytes 131104 | tf_op jit(solution)/shard_map/ppermute | solution.py:582
  79.3 0.6 collective-permute-start.8
  79.9 5.0 %collective-permute-done.8.other_total_ref = bf16[64,1024]{1,0:T(8,128)(2,1)S(1)} collective-permute-done((bf16[64,1024]{1,0:T(8,128)(2,1)S(1)}, bf16[64,1024]{1,0:T(8,128)(2,1)S(1)}, u32[]{:S(2)}, u32[]{:S(2)}) %collective-permute-start.8) | collective-permute-done | bytes 131104 | tf_op jit(solution)/shard_map/ppermute | solution.py:582
  84.9 3.1 %final.1 = f32[2,1024,256]{2,1,0:T(8,128)} custom-call(f32[2,1024,256]{2,1,0:T(8,128)S(1)} %copy-done, f32[8,256,256]{2,1,0:T(8,128)S(1)} %copy-done.4, bf16[8,256,128]{2,1,0:T(8,128)(2,1)S(1)} %add.6.sum_ref, bf16[8,256,128]{2,1,0:T(8,128)(2,1)S(1)} %collective-permute-done.3.other_sum_ref, bf16[128,1024]{1,0:T(8,128)(2,1)S(1)} %get-tuple-element.31.coeffs_ref, ...), custom_call_target="tpu_custom_call" | custom-call | tf_op jit(solution)/shard_map/final/pallas_call | solution.py:795
  (44 shorter events, 0.4 us)
Async XLA Ops:
  0.0 16.9 %copy-start.10 = (s32[1024,27]{0,1:T(8,128)S(1)}, s32[1024,27]{0,1:T(8,128)}, u32[]{:S(2)}) copy-start(s32[1024,27]{0,1:T(8,128)} %param.12) | copy-start | bytes 331780
  4.9 8.0 %collective-permute-start = (bf16[512,128]{1,0:T(8,128)(2,1)}, bf16[512,128]{1,0:T(8,128)(2,1)S(1)}, u32[]{:S(2)}, u32[]{:S(2)}) collective-permute-start(bf16[512,128]{1,0:T(8,128)(2,1)} %get-tuple-element.22), channel_id=1, source_target_pairs={{0,4},{4,8},{8,12},{12,16},{16,20},{20,24},{24,28},{1,5},{5,9},{9,... | collective-permute-start | bytes 393224 | tf_op jit(solution)/shard_map/ppermute | solution.py:587
  9.9 7.1 %collective-permute-start.1 = (bf16[512,128]{1,0:T(8,128)(2,1)}, bf16[512,128]{1,0:T(8,128)(2,1)S(1)}, u32[]{:S(2)}, u32[]{:S(2)}) collective-permute-start(bf16[512,128]{1,0:T(8,128)(2,1)} %get-tuple-element.23), channel_id=1, source_target_pairs={{4,0},{8,4},{12,8},{16,12},{20,16},{24,20},{28,24},{5,1},{9,5},{13... | collective-permute-start | bytes 393224 | tf_op jit(solution)/shard_map/ppermute | solution.py:587
  16.9 1.2 %copy-start.1 = (bf16[512,896]{1,0:T(8,128)(2,1)S(1)}, bf16[512,896]{1,0:T(8,128)(2,1)}, u32[]{:S(2)}) copy-start(bf16[512,896]{1,0:T(8,128)(2,1)} %get-tuple-element.19.early_ref.late_ref) | copy-start | bytes 2752516
  18.1 2.0 %copy-start.2 = (bf16[27,256,256]{2,1,0:T(8,128)(2,1)S(1)}, bf16[27,256,256]{2,1,0:T(8,128)(2,1)}, u32[]{:S(2)}) copy-start(bf16[27,256,256]{2,1,0:T(8,128)(2,1)} %table_hbm.1) | copy-start | bytes 10616836
  20.1 0.9 %copy-start.11 = (bf16[512,128]{1,0:T(8,128)(2,1)S(1)}, bf16[512,128]{1,0:T(8,128)(2,1)}, u32[]{:S(2)}) copy-start(bf16[512,128]{1,0:T(8,128)(2,1)} %get-tuple-element.20.first_ref) | copy-start | bytes 393220
  21.0 0.9 %copy-start.12 = (bf16[512,128]{1,0:T(8,128)(2,1)S(1)}, bf16[512,128]{1,0:T(8,128)(2,1)}, u32[]{:S(2)}) copy-start(bf16[512,128]{1,0:T(8,128)(2,1)} %get-tuple-element.21.last_ref) | copy-start | bytes 393220
  21.9 24.7 %copy-start.18 = (bf16[128,128]{1,0:T(8,128)(2,1)S(1)}, bf16[128,128]{1,0:T(8,128)(2,1)}, u32[]{:S(2)}) copy-start(bf16[128,128]{1,0:T(8,128)(2,1)} %get-tuple-element.30.cube_ref) | copy-start | bytes 98308
  41.7 1.3 %copy-start.3 = (f32[8,256,256]{2,1,0:T(8,128)}, f32[8,256,256]{2,1,0:T(8,128)S(1)}, u32[]{:S(2)}) copy-start(f32[8,256,256]{2,1,0:T(8,128)S(1)} %get-tuple-element.24.near_ref) | copy-start | bytes 6291460
  43.0 1.9 %collective-permute-start.2 = (bf16[8,256,128]{2,1,0:T(8,128)(2,1)S(1)}, bf16[8,256,128]{2,1,0:T(8,128)(2,1)S(1)}, u32[]{:S(2)}, u32[]{:S(2)}) collective-permute-start(bf16[8,256,128]{2,1,0:T(8,128)(2,1)S(1)} %get-tuple-element.25), channel_id=1, source_target_pairs={{0,1},{1,0},{2,3},{3,2},{4,5},{5,4},{6,7},{7,6},{8,9},{9,8},{10,11... | collective-permute-start | bytes 1572872 | tf_op jit(solution)/shard_map/ppermute | solution.py:582
  45.0 39.8 %collective-permute-start.3 = (bf16[8,256,128]{2,1,0:T(8,128)(2,1)S(1)}, bf16[8,256,128]{2,1,0:T(8,128)(2,1)S(1)}, u32[]{:S(2)}, u32[]{:S(2)}) collective-permute-start(bf16[8,256,128]{2,1,0:T(8,128)(2,1)S(1)} %add.6.sum_ref), channel_id=1, source_target_pairs={{0,2},{1,3},{2,0},{3,1},{4,6},{5,7},{6,4},{7,5},{8,10},{9,11},{10,... | collective-permute-start | bytes 1572872 | tf_op jit(solution)/shard_map/ppermute | solution.py:582
  46.8 9.5 %collective-permute-start.6 = (bf16[128,128]{1,0:T(8,128)(2,1)S(1)}, bf16[128,128]{1,0:T(8,128)(2,1)S(1)}, u32[]{:S(2)}, u32[]{:S(2)}) collective-permute-start(bf16[128,128]{1,0:T(8,128)(2,1)S(1)} %join.1.cube_ref), channel_id=1, source_target_pairs={{0,24},{4,28},{8,16},{12,20},{16,8},{20,12},{24,0},{28,4},{1,25},{... | collective-permute-start | bytes 98312 | tf_op jit(solution)/shard_map/ppermute | solution.py:582
  51.0 5.3 %collective-permute-start.5 = (bf16[128,128]{1,0:T(8,128)(2,1)S(1)}, bf16[128,128]{1,0:T(8,128)(2,1)S(1)}, u32[]{:S(2)}, u32[]{:S(2)}) collective-permute-start(bf16[128,128]{1,0:T(8,128)(2,1)S(1)} %join.1.cube_ref), channel_id=1, source_target_pairs={{0,16},{4,20},{8,24},{12,28},{16,0},{20,4},{24,8},{28,12},{1,17},{... | collective-permute-start | bytes 98312 | tf_op jit(solution)/shard_map/ppermute | solution.py:582
  51.0 5.3 %collective-permute-start.4 = (bf16[128,128]{1,0:T(8,128)(2,1)S(1)}, bf16[128,128]{1,0:T(8,128)(2,1)S(1)}, u32[]{:S(2)}, u32[]{:S(2)}) collective-permute-start(bf16[128,128]{1,0:T(8,128)(2,1)S(1)} %join.1.cube_ref), channel_id=1, source_target_pairs={{0,8},{4,12},{8,0},{12,4},{16,24},{20,28},{24,16},{28,20},{1,9},{5... | collective-permute-start | bytes 98312 | tf_op jit(solution)/shard_map/ppermute | solution.py:582
  55.4 0.9 %copy-start.5 = (bf16[8,64,64]{2,1,0:T(8,128)(2,1)S(1)}, bf16[8,64,64]{2,1,0:T(8,128)(2,1)}, u32[]{:S(2)}) copy-start(bf16[8,64,64]{2,1,0:T(8,128)(2,1)} %transfer_ref.1) | copy-start | bytes 196612
  55.4 0.9 %copy-start.13 = (bf16[4,64,64]{2,1,0:T(8,128)(2,1)S(1)}, bf16[4,64,64]{2,1,0:T(8,128)(2,1)}, u32[]{:S(2)}) copy-start(bf16[4,64,64]{2,1,0:T(8,128)(2,1)} %coarse_ref.1) | copy-start | bytes 98308
  56.3 7.3 %copy-start.6 = (s32[1024,108]{0,1:T(8,128)S(1)}, s32[1024,108]{0,1:T(8,128)}, u32[]{:S(2)}) copy-start(s32[1024,108]{0,1:T(8,128)} %param.13) | copy-start | bytes 1327108
  56.3 7.3 %copy-start.7 = (bf16[9,128,128]{2,1,0:T(8,128)(2,1)S(1)}, bf16[9,128,128]{2,1,0:T(8,128)(2,1)}, u32[]{:S(2)}) copy-start(bf16[9,128,128]{2,1,0:T(8,128)(2,1)} %get-tuple-element.27.odd_ref) | copy-start | bytes 884740
  56.3 7.3 %copy-start.8 = (bf16[8,128,128]{2,1,0:T(8,128)(2,1)S(1)}, bf16[8,128,128]{2,1,0:T(8,128)(2,1)}, u32[]{:S(2)}) copy-start(bf16[8,128,128]{2,1,0:T(8,128)(2,1)} %get-tuple-element.26.whole_ref) | copy-start | bytes 786436
  63.7 21.2 %copy-start = (f32[2,1024,256]{2,1,0:T(8,128)S(1)}, f32[2,1024,256]{2,1,0:T(8,128)}, u32[]{:S(2)}) copy-start(f32[2,1024,256]{2,1,0:T(8,128)} %orbitals_ref.1) | copy-start | bytes 6291460
  63.7 21.2 %copy-start.4 = (f32[8,256,256]{2,1,0:T(8,128)S(1)}, f32[8,256,256]{2,1,0:T(8,128)}, u32[]{:S(2)}) copy-start(f32[8,256,256]{2,1,0:T(8,128)} %copy-done.3) | copy-start | bytes 6291460
  63.7 21.2 %copy-start.9 = (bf16[64,256]{1,0:T(8,128)(2,1)S(1)}, bf16[64,256]{1,0:T(8,128)(2,1)}, u32[]{:S(2)}) copy-start(bf16[64,256]{1,0:T(8,128)(2,1)} %basis_ref.1) | copy-start | bytes 98308
  77.8 1.4 %collective-permute-start.7 = (bf16[64,1024]{1,0:T(8,128)(2,1)S(1)}, bf16[64,1024]{1,0:T(8,128)(2,1)S(1)}, u32[]{:S(2)}, u32[]{:S(2)}) collective-permute-start(bf16[64,1024]{1,0:T(8,128)(2,1)S(1)} %get-tuple-element.32), channel_id=1, source_target_pairs={{0,1},{1,0},{2,3},{3,2},{4,5},{5,4},{6,7},{7,6},{8,9},{9,8},{10,11... | collective-permute-start | bytes 393224 | tf_op jit(solution)/shard_map/ppermute | solution.py:582
  79.3 5.6 %collective-permute-start.8 = (bf16[64,1024]{1,0:T(8,128)(2,1)S(1)}, bf16[64,1024]{1,0:T(8,128)(2,1)S(1)}, u32[]{:S(2)}, u32[]{:S(2)}) collective-permute-start(bf16[64,1024]{1,0:T(8,128)(2,1)S(1)} %add.7.total_ref), channel_id=1, source_target_pairs={{0,2},{1,3},{2,0},{3,1},{4,6},{5,7},{6,4},{7,5},{8,10},{9,11},{10,... | collective-permute-start | bytes 393224 | tf_op jit(solution)/shard_map/ppermute | solution.py:582
  (5 other events, 4.4 us)

commit v5 on v4

--- a/solution.py
+++ b/solution.py
@@ -14,6 +14,7 @@
 BF = jnp.bfloat16
 F32 = jnp.float32
 relax_step = 0.1
+SELF = 13
 MID_RIM = 3 * (SIDE // 2) ** 2
 TOP_RIM = 3 * (SIDE // 4) ** 2
 MID_AT = LAYER
@@ -234,8 +235,17 @@
     turn_ref[:slots, :] = (source_ref[...] - start).astype(F32)
     orbits = side_ref.shape[0] // points
     group = 2
-    for begin in range(0, slots, group):
-        chunk = range(begin, min(begin + group, slots))
+    low = iota((points, PAIR), 1) < LAYER
+    for o in range(orbits):
+        rows = slice(o * points, (o + 1) * points)
+        before = side_ref[rows, :PAIR].astype(F32)
+        after = side_ref[rows, PAIR:].astype(F32)
+        picked_ref[SELF * points : (SELF + 1) * points, o * PAIR : (o + 1) * PAIR] = rolled(
+            jnp.where(low, after, before), LAYER
+        ).astype(BF)
+    entries = [k for k in range(slots) if k != SELF]
+    for begin in range(0, len(entries), group):
+        chunk = entries[begin : begin + group]
         columns = [index_columns(turn_ref[k : k + 1, :], 2 * PAIR) for k in chunk]
         columns = jnp.concatenate(columns, axis=1)
         for o in range(orbits):
@@ -463,9 +473,12 @@
             picked_ref[row : row + height, :128] = mid_picked[:, n * 128 : (n + 1) * 128]
 
     depth = half_slots * height
-    far = dot(weight_ref[:height], picked_ref[:depth]) + dot(weight_ref[height:], picked_ref[depth:])
-    top = (0.25 * far[:, 128:] + down_level(cube_own, 128, SIDE // 4, transfer, rank)).astype(BF)
-    mid = (0.5 * far[:, :128] + down_level(top, 128, SIDE // 2, transfer, rank)).astype(BF)
+    scale = jnp.where(iota((1, 256), 1) < 128, 0.5, 0.25)
+    far = scale * dot(weight_ref[:height], picked_ref[:depth]) + scale * dot(
+        weight_ref[height:], picked_ref[depth:]
+    )
+    top = (far[:, 128:] + down_level(cube_own, 128, SIDE // 4, transfer, rank)).astype(BF)
+    mid = (far[:, :128] + down_level(top, 128, SIDE // 2, transfer, rank)).astype(BF)
     out_ref[...] = down_level(mid, leaves, SIDE, transfer, rank)
 
 
@@ -559,22 +572,25 @@
     sum_ref[...] = total.astype(BF)
 
 
-def final_kernel(
-    orbitals_ref, near_ref, sum_ref, other_sum_ref, coeffs_ref, total_ref, other_total_ref, basis_ref, out_ref
-):
-    orbits = orbitals_ref.shape[0]
+def gap_kernel(near_ref, sum_ref, other_sum_ref, coeffs_ref, basis_ref, out_ref):
+    orbits, leaves, _ = out_ref.shape
     rank = basis_ref.shape[0]
-    batch = orbitals_ref.shape[1] // PAIR
+    batch = leaves // PAIR
     for n in range(batch):
         lanes = slice(n * PAIR, (n + 1) * PAIR)
         pair = pl.program_id(0) * batch + n
         hartree = sum_ref[n].astype(F32) + other_sum_ref[pair].astype(F32)
-        total = total_ref[:, lanes].astype(F32) + other_total_ref[:, lanes].astype(F32)
         for o in range(orbits):
-            rest = (total - coeffs_ref[o * rank : (o + 1) * rank, lanes].astype(F32)).astype(BF)
-            gap = hartree - near_ref[pair, :, o * PAIR : (o + 1) * PAIR] + dot_tn(basis_ref[...], rest)
-            value = orbitals_ref[o, lanes]
-            out_ref[o, lanes] = value - relax_step * turned(gap) * value
+            own = dot_tn(basis_ref[...], coeffs_ref[o * rank : (o + 1) * rank, lanes])
+            out_ref[o, lanes] = turned(hartree - near_ref[pair, :, o * PAIR : (o + 1) * PAIR] - own)
+
+
+def final_kernel(orbitals_ref, gap_ref, total_ref, other_total_ref, basis_ref, out_ref):
+    total = (total_ref[...].astype(F32) + other_total_ref[...].astype(F32)).astype(BF)
+    shared = dot_tn(total, basis_ref[...])
+    for o in range(orbitals_ref.shape[0]):
+        value = orbitals_ref[o]
+        out_ref[o] = value - relax_step * (gap_ref[o] + shared) * value
 
 
 def swap(values, axis, bit):
@@ -792,24 +808,30 @@
     per_pair = pl.BlockSpec((batch, points, PAIR), lambda i: (i, 0, 0))
     per_rank = pl.BlockSpec((rank, batch * PAIR), lambda i: (0, i))
     per_leaf = pl.BlockSpec((orbits, batch * PAIR, points), lambda i: (0, i, 0))
-    return pl.pallas_call(
-        final_kernel,
+    gap = pl.pallas_call(
+        gap_kernel,
         grid=(pairs // batch,),
         in_specs=[
-            per_leaf,
             in_vmem,
             per_pair,
             in_vmem,
             pl.BlockSpec((height, batch * PAIR), lambda i: (0, i)),
-            per_rank,
-            per_rank,
             full(leaf_basis.shape),
         ],
         out_specs=per_leaf,
         out_shape=jax.ShapeDtypeStruct(orbitals.shape, F32),
         compiler_params=WIDE_MEMORY,
+        name="gap",
+    )(near, near_chip, near_other, coeffs, leaf_basis)
+    return pl.pallas_call(
+        final_kernel,
+        grid=(pairs // batch,),
+        in_specs=[per_leaf, per_leaf, per_rank, per_rank, full(leaf_basis.shape)],
+        out_specs=per_leaf,
+        out_shape=jax.ShapeDtypeStruct(orbitals.shape, F32),
+        compiler_params=WIDE_MEMORY,
         name="final",
-    )(orbitals, near, near_chip, near_other, coeffs, coeff_chip, coeff_other, leaf_basis)
+    )(orbitals, gap, coeff_chip, coeff_other, leaf_basis)
 
 
 def solution(mesh):

time: 88.3 us -> 86.5 us (0.980)
  waiting for transfers between devices: 14 us -> 12.1 us
    ppermute x7, waiting for transfers between devices: 8.27 us -> 6.36 us  [swap(): return lax.ppermute(values, axis, [(i, i ^ bit) for i in range(count)])]
    pallas_call x0 -> x1, Pallas kernels: none -> 1.82 us  [shards(): pl.pallas_call(gap_kernel, grid=(pairs // batch,), in_specs=[in_vmem, per...]
  transfers between devices with their start and end apart: 9 -> 9, of which waited for: 5 -> 5; matrix products, arithmetic and copies ran while one was open for 4% -> 4% of each run, Pallas kernels for 25% -> 27%
where the time goes in v5:
time: 86.5 us; the launch traced here: 86.2 us
  Pallas kernels  50.1 us (58%)
  starting transfers between devices  13.3 us (15%)
  waiting for transfers between devices  12.1 us (14%)
  local copies, waits for them, and re-layouts  10.2 us (12%)
    pallas_call x1, Pallas kernels, shards(): pl.pallas_call(near_kernel, grid=(pairs,), in_specs=[smem, pl.BlockSpec((...  19.2 us
    pallas_call x1, Pallas kernels, shards(): pl.pallas_call(functools.partial(leaf_kernel, pairs), grid=(pairs // 2,),...  14.1 us
    unnamed x41, local copies, waits for them, and re-layouts  10.2 us
    ppermute x7, starting transfers between devices, swap(): return lax.ppermute(values, axis, [(i, i ^ bit) for i in range(count)])  7.13 us
    pallas_call x1, Pallas kernels, shards(): pl.pallas_call(functools.partial(tree_kernel, count, leaves, rank), grid=...  6.49 us
    ppermute x7, waiting for transfers between devices, swap(): return lax.ppermute(values, axis, [(i, i ^ bit) for i in range(count)])  6.36 us
    ppermute x2, starting transfers between devices, step_along(): return lax.ppermute(values, 'space', pairs)  6.2 us
    ppermute x2, waiting for transfers between devices, step_along(): return lax.ppermute(values, 'space', pairs)  5.77 us
  transfers between devices with their start and end apart: 9, of which 5 were waited for; matrix products, arithmetic and copies ran while one was open for 4% of the time, Pallas kernels for 27%

profile of v5, /device:TPU:0, one launch (start us, length us, event | category | flops | bytes accessed | tf_op | source)
XLA Modules:
  0.0 86.2 jit_solution(18002524335385959951)
XLA Ops:
  0.0 4.9 %moments.1 = (bf16[512,896]{1,0:T(8,128)(2,1)}, bf16[512,128]{1,0:T(8,128)(2,1)}, bf16[512,128]{1,0:T(8,128)(2,1)}, bf16[8,128,128]{2,1,0:T(8,128)(2,1)}, bf16[9...) custom-call(f32[2,1024,256]{2,1,0:T(8,128)} %orbitals_ref.1, ...), custom_call_target="tpu_custom_call" | custom-call | tf_op jit(solution)/shard_map/moments/pallas_call | solution.py:638
  4.9 4.9 %collective-permute-start = (bf16[512,128]{1,0:T(8,128)(2,1)}, bf16[512,128]{1,0:T(8,128)(2,1)S(1)}, u32[]{:S(2)}, u32[]{:S(2)}) collective-permute-start(bf16[512,128]{1,0:T(8,128)(2,1)} %get-tuple-element.22), channel_id=1, source_target_pairs={{0,4},{4,8},{8,12},{12,16},{16,20},{20,24},{24,28},{1,5},{5,9},{9,... | collective-permute-start | bytes 393224 | tf_op jit(solution)/shard_map/ppermute | solution.py:603
  9.9 1.3 %collective-permute-start.1 = (bf16[512,128]{1,0:T(8,128)(2,1)}, bf16[512,128]{1,0:T(8,128)(2,1)S(1)}, u32[]{:S(2)}, u32[]{:S(2)}) collective-permute-start(bf16[512,128]{1,0:T(8,128)(2,1)} %get-tuple-element.23), channel_id=1, source_target_pairs={{4,0},{8,4},{12,8},{16,12},{20,16},{24,20},{28,24},{5,1},{9,5},{13... | collective-permute-start | bytes 393224 | tf_op jit(solution)/shard_map/ppermute | solution.py:603
  11.2 1.7 %collective-permute-done.got_left_ref.left_ref = bf16[512,128]{1,0:T(8,128)(2,1)S(1)} collective-permute-done((bf16[512,128]{1,0:T(8,128)(2,1)}, bf16[512,128]{1,0:T(8,128)(2,1)S(1)}, u32[]{:S(2)}, u32[]{:S(2)}) %collective-permute-start) | collective-permute-done | bytes 131104 | tf_op jit(solution)/shard_map/ppermute | solution.py:603
  12.9 4.0 %collective-permute-done.1.got_right_ref.right_ref = bf16[512,128]{1,0:T(8,128)(2,1)S(1)} collective-permute-done((bf16[512,128]{1,0:T(8,128)(2,1)}, bf16[512,128]{1,0:T(8,128)(2,1)S(1)}, u32[]{:S(2)}, u32[]{:S(2)}) %collective-permute-start.1) | collective-permute-done | bytes 131104 | tf_op jit(solution)/shard_map/ppermute | solution.py:603
  16.9 1.2 %copy-done.1 = bf16[512,896]{1,0:T(8,128)(2,1)S(1)} copy-done((bf16[512,896]{1,0:T(8,128)(2,1)S(1)}, bf16[512,896]{1,0:T(8,128)(2,1)}, u32[]{:S(2)}) %copy-start.1) | copy-done | bytes 917528
  18.1 2.0 %copy-done.2 = bf16[27,256,256]{2,1,0:T(8,128)(2,1)S(1)} copy-done((bf16[27,256,256]{2,1,0:T(8,128)(2,1)S(1)}, bf16[27,256,256]{2,1,0:T(8,128)(2,1)}, u32[]{:S(2)}) %copy-start.2) | copy-done | bytes 3538968
  20.1 0.9 %copy-done.11 = bf16[512,128]{1,0:T(8,128)(2,1)S(1)} copy-done((bf16[512,128]{1,0:T(8,128)(2,1)S(1)}, bf16[512,128]{1,0:T(8,128)(2,1)}, u32[]{:S(2)}) %copy-start.11) | copy-done | bytes 131096
  21.0 0.9 %copy-done.12 = bf16[512,128]{1,0:T(8,128)(2,1)S(1)} copy-done((bf16[512,128]{1,0:T(8,128)(2,1)S(1)}, bf16[512,128]{1,0:T(8,128)(2,1)}, u32[]{:S(2)}) %copy-start.12) | copy-done | bytes 131096
  21.9 19.2 %near.1 = (f32[8,256,256]{2,1,0:T(8,128)S(1)}, bf16[8,256,128]{2,1,0:T(8,128)(2,1)S(1)}) custom-call(s32[1]{0:T(128)} %bitcast.place_ref, s32[27,1024]{1,0:T(8,128)S(1)} %bitcast.7, bf16[512,896]{1,0:T(8,128)(2,1)S(1)} %copy-done.1, bf16[512,896]{1,0:T(8,128)(2,1)S(1)} %copy-done.1, bf16[512,128]{1,0:T(8,128)(2,1)S(1)} %copy-done.11, ...), custom_call_target="tpu_custom_call" | custom-call | tf_op jit(solution)/shard_map/near/pallas_call | solution.py:692
  41.1 1.3 %copy-done.3 = f32[8,256,256]{2,1,0:T(8,128)} copy-done((f32[8,256,256]{2,1,0:T(8,128)}, f32[8,256,256]{2,1,0:T(8,128)S(1)}, u32[]{:S(2)}) %copy-start.3) | copy-done | bytes 2097176
  42.4 1.9 %collective-permute-done.2 = bf16[8,256,128]{2,1,0:T(8,128)(2,1)S(1)} collective-permute-done((bf16[8,256,128]{2,1,0:T(8,128)(2,1)S(1)}, bf16[8,256,128]{2,1,0:T(8,128)(2,1)S(1)}, u32[]{:S(2)}, u32[]{:S(2)}) %collective-permute-start.2) | collective-permute-done | bytes 524320 | tf_op jit(solution)/shard_map/ppermute | solution.py:598
  44.5 1.6 %collective-permute-start.3 = (bf16[8,256,128]{2,1,0:T(8,128)(2,1)S(1)}, bf16[8,256,128]{2,1,0:T(8,128)(2,1)S(1)}, u32[]{:S(2)}, u32[]{:S(2)}) collective-permute-start(bf16[8,256,128]{2,1,0:T(8,128)(2,1)S(1)} %add.6.sum_ref), channel_id=1, source_target_pairs={{0,2},{1,3},{2,0},{3,1},{4,6},{5,7},{6,4},{7,5},{8,10},{9,11},{10,... | collective-permute-start | bytes 1572872 | tf_op jit(solution)/shard_map/ppermute | solution.py:598
  46.2 4.2 %collective-permute-start.6 = (bf16[128,128]{1,0:T(8,128)(2,1)S(1)}, bf16[128,128]{1,0:T(8,128)(2,1)S(1)}, u32[]{:S(2)}, u32[]{:S(2)}) collective-permute-start(bf16[128,128]{1,0:T(8,128)(2,1)S(1)} %join.1.cube_ref), channel_id=1, source_target_pairs={{0,24},{4,28},{8,16},{12,20},{16,8},{20,12},{24,0},{28,4},{1,25},{... | collective-permute-start | bytes 98312 | tf_op jit(solution)/shard_map/ppermute | solution.py:598
  50.4 0.6 collective-permute-start.4
  51.1 3.8 %copy.12.coupling_ref = bf16[108,64,64]{2,1,0:T(8,128)(2,1)S(1)} copy(bf16[108,64,64]{0,2,1:T(8,128)(2,1)} %param.19) | data formatting | bytes 1769472 | tf_op args[8]
  54.9 0.8 widen.1.weight_ref
  55.8 6.5 %tree.1.down_ref = f32[128,1024]{1,0:T(8,128)S(1)} custom-call(s32[1]{0:T(128)} %bitcast.place_ref, bf16[128,128]{1,0:T(8,128)(2,1)S(1)} %copy-done.16, bf16[128,128]{1,0:T(8,128)(2,1)S(1)} %copy-done.17, bf16[512,128]{1,0:T(8,128)(2,1)S(1)} %collective-permute-done.got_left_ref.left_ref, ...), custom_call_target="tpu_custom_call" | custom-call | tf_op jit(solution)/shard_map/tree/pallas_call | solution.py:721
  62.4 14.1 %leaf.1 = (bf16[128,1024]{1,0:T(8,128)(2,1)S(1)}, bf16[64,1024]{1,0:T(8,128)(2,1)S(1)}) custom-call(s32[1]{0:T(128)} %bitcast.place_ref, s32[108,1024]{1,0:T(8,128)S(1)} %bitcast.6, bf16[8,128,128]{2,1,0:T(8,128)(2,1)S(1)} %copy-done.9, bf16[9,128,128]{2,1,0:T(8,128)(2,1)S(1)} %copy-done.8, bf16[512,128]{1,0:T(8,128)(2,1)S(1)} %collective-permute-done.got_left_ref.left_ref, ...), custom_call_target="tpu_custom_call" | custom-call | tf_op jit(solution)/shard_map/leaf/pallas_call | solution.py:764
  76.5 1.3 %collective-permute-done.7 = bf16[64,1024]{1,0:T(8,128)(2,1)S(1)} collective-permute-done((bf16[64,1024]{1,0:T(8,128)(2,1)S(1)}, bf16[64,1024]{1,0:T(8,128)(2,1)S(1)}, u32[]{:S(2)}, u32[]{:S(2)}) %collective-permute-start.7) | collective-permute-done | bytes 131104 | tf_op jit(solution)/shard_map/ppermute | solution.py:598
  77.9 0.7 collective-permute-start.8
  78.6 1.8 %gap.1.gap_ref = f32[2,1024,256]{2,1,0:T(8,128)S(1)} custom-call(f32[8,256,256]{2,1,0:T(8,128)S(1)} %copy-done.4, bf16[8,256,128]{2,1,0:T(8,128)(2,1)S(1)} %add.6.sum_ref, bf16[8,256,128]{2,1,0:T(8,128)(2,1)S(1)} %collective-permute-done.3.other_sum_ref, bf16[128,1024]{1,0:T(8,128)(2,1)S(1)} %get-tuple-element.31.coeffs_ref, bf16[64,256]{1,0:T(8,128)(2,1)S(1)} %copy-done.7), custom_call_target="tpu_custom_call" | custom-call | tf_op jit(solution)/shard_map/gap/pallas_call | solution.py:811
  80.4 3.1 %collective-permute-done.8.other_total_ref = bf16[64,1024]{1,0:T(8,128)(2,1)S(1)} collective-permute-done((bf16[64,1024]{1,0:T(8,128)(2,1)S(1)}, bf16[64,1024]{1,0:T(8,128)(2,1)S(1)}, u32[]{:S(2)}, u32[]{:S(2)}) %collective-permute-start.8) | collective-permute-done | bytes 131104 | tf_op jit(solution)/shard_map/ppermute | solution.py:598
  83.5 2.6 %final.1 = f32[2,1024,256]{2,1,0:T(8,128)} custom-call(f32[2,1024,256]{2,1,0:T(8,128)S(1)} %copy-done, f32[2,1024,256]{2,1,0:T(8,128)S(1)} %gap.1.gap_ref, bf16[64,1024]{1,0:T(8,128)(2,1)S(1)} %add.7.total_ref, bf16[64,1024]{1,0:T(8,128)(2,1)S(1)} %collective-permute-done.8.other_total_ref, bf16[64,256]{1,0:T(8,128)(2,1)S(1)} %copy-done.7), custom_call_target="tpu_custom_call" | custom-call | tf_op jit(solution)/shard_map/final/pallas_call | solution.py:826
  (45 shorter events, 0.5 us)
Async XLA Ops:
  0.0 16.9 %copy-start.10 = (s32[1024,27]{0,1:T(8,128)S(1)}, s32[1024,27]{0,1:T(8,128)}, u32[]{:S(2)}) copy-start(s32[1024,27]{0,1:T(8,128)} %param.12) | copy-start | bytes 331780
  4.9 8.0 %collective-permute-start = (bf16[512,128]{1,0:T(8,128)(2,1)}, bf16[512,128]{1,0:T(8,128)(2,1)S(1)}, u32[]{:S(2)}, u32[]{:S(2)}) collective-permute-start(bf16[512,128]{1,0:T(8,128)(2,1)} %get-tuple-element.22), channel_id=1, source_target_pairs={{0,4},{4,8},{8,12},{12,16},{16,20},{20,24},{24,28},{1,5},{5,9},{9,... | collective-permute-start | bytes 393224 | tf_op jit(solution)/shard_map/ppermute | solution.py:603
  9.9 7.1 %collective-permute-start.1 = (bf16[512,128]{1,0:T(8,128)(2,1)}, bf16[512,128]{1,0:T(8,128)(2,1)S(1)}, u32[]{:S(2)}, u32[]{:S(2)}) collective-permute-start(bf16[512,128]{1,0:T(8,128)(2,1)} %get-tuple-element.23), channel_id=1, source_target_pairs={{4,0},{8,4},{12,8},{16,12},{20,16},{24,20},{28,24},{5,1},{9,5},{13... | collective-permute-start | bytes 393224 | tf_op jit(solution)/shard_map/ppermute | solution.py:603
  16.9 1.2 %copy-start.1 = (bf16[512,896]{1,0:T(8,128)(2,1)S(1)}, bf16[512,896]{1,0:T(8,128)(2,1)}, u32[]{:S(2)}) copy-start(bf16[512,896]{1,0:T(8,128)(2,1)} %get-tuple-element.19.early_ref.late_ref) | copy-start | bytes 2752516
  18.1 2.0 %copy-start.2 = (bf16[27,256,256]{2,1,0:T(8,128)(2,1)S(1)}, bf16[27,256,256]{2,1,0:T(8,128)(2,1)}, u32[]{:S(2)}) copy-start(bf16[27,256,256]{2,1,0:T(8,128)(2,1)} %table_hbm.1) | copy-start | bytes 10616836
  20.1 0.9 %copy-start.11 = (bf16[512,128]{1,0:T(8,128)(2,1)S(1)}, bf16[512,128]{1,0:T(8,128)(2,1)}, u32[]{:S(2)}) copy-start(bf16[512,128]{1,0:T(8,128)(2,1)} %get-tuple-element.20.first_ref) | copy-start | bytes 393220
  21.0 0.9 %copy-start.12 = (bf16[512,128]{1,0:T(8,128)(2,1)S(1)}, bf16[512,128]{1,0:T(8,128)(2,1)}, u32[]{:S(2)}) copy-start(bf16[512,128]{1,0:T(8,128)(2,1)} %get-tuple-element.21.last_ref) | copy-start | bytes 393220
  21.9 24.1 %copy-start.18 = (bf16[128,128]{1,0:T(8,128)(2,1)S(1)}, bf16[128,128]{1,0:T(8,128)(2,1)}, u32[]{:S(2)}) copy-start(bf16[128,128]{1,0:T(8,128)(2,1)} %get-tuple-element.30.cube_ref) | copy-start | bytes 98308
  41.1 1.3 %copy-start.3 = (f32[8,256,256]{2,1,0:T(8,128)}, f32[8,256,256]{2,1,0:T(8,128)S(1)}, u32[]{:S(2)}) copy-start(f32[8,256,256]{2,1,0:T(8,128)S(1)} %get-tuple-element.24.near_ref) | copy-start | bytes 6291460
  42.4 1.9 %collective-permute-start.2 = (bf16[8,256,128]{2,1,0:T(8,128)(2,1)S(1)}, bf16[8,256,128]{2,1,0:T(8,128)(2,1)S(1)}, u32[]{:S(2)}, u32[]{:S(2)}) collective-permute-start(bf16[8,256,128]{2,1,0:T(8,128)(2,1)S(1)} %get-tuple-element.25), channel_id=1, source_target_pairs={{0,1},{1,0},{2,3},{3,2},{4,5},{5,4},{6,7},{7,6},{8,9},{9,8},{10,11... | collective-permute-start | bytes 1572872 | tf_op jit(solution)/shard_map/ppermute | solution.py:598
  44.5 34.1 %collective-permute-start.3 = (bf16[8,256,128]{2,1,0:T(8,128)(2,1)S(1)}, bf16[8,256,128]{2,1,0:T(8,128)(2,1)S(1)}, u32[]{:S(2)}, u32[]{:S(2)}) collective-permute-start(bf16[8,256,128]{2,1,0:T(8,128)(2,1)S(1)} %add.6.sum_ref), channel_id=1, source_target_pairs={{0,2},{1,3},{2,0},{3,1},{4,6},{5,7},{6,4},{7,5},{8,10},{9,11},{10,... | collective-permute-start | bytes 1572872 | tf_op jit(solution)/shard_map/ppermute | solution.py:598
  46.2 9.5 %collective-permute-start.6 = (bf16[128,128]{1,0:T(8,128)(2,1)S(1)}, bf16[128,128]{1,0:T(8,128)(2,1)S(1)}, u32[]{:S(2)}, u32[]{:S(2)}) collective-permute-start(bf16[128,128]{1,0:T(8,128)(2,1)S(1)} %join.1.cube_ref), channel_id=1, source_target_pairs={{0,24},{4,28},{8,16},{12,20},{16,8},{20,12},{24,0},{28,4},{1,25},{... | collective-permute-start | bytes 98312 | tf_op jit(solution)/shard_map/ppermute | solution.py:598
  50.4 5.3 %collective-permute-start.5 = (bf16[128,128]{1,0:T(8,128)(2,1)S(1)}, bf16[128,128]{1,0:T(8,128)(2,1)S(1)}, u32[]{:S(2)}, u32[]{:S(2)}) collective-permute-start(bf16[128,128]{1,0:T(8,128)(2,1)S(1)} %join.1.cube_ref), channel_id=1, source_target_pairs={{0,16},{4,20},{8,24},{12,28},{16,0},{20,4},{24,8},{28,12},{1,17},{... | collective-permute-start | bytes 98312 | tf_op jit(solution)/shard_map/ppermute | solution.py:598
  50.4 5.3 %collective-permute-start.4 = (bf16[128,128]{1,0:T(8,128)(2,1)S(1)}, bf16[128,128]{1,0:T(8,128)(2,1)S(1)}, u32[]{:S(2)}, u32[]{:S(2)}) collective-permute-start(bf16[128,128]{1,0:T(8,128)(2,1)S(1)} %join.1.cube_ref), channel_id=1, source_target_pairs={{0,8},{4,12},{8,0},{12,4},{16,24},{20,28},{24,16},{28,20},{1,9},{5... | collective-permute-start | bytes 98312 | tf_op jit(solution)/shard_map/ppermute | solution.py:598
  54.8 0.9 %copy-start.5 = (bf16[8,64,64]{2,1,0:T(8,128)(2,1)S(1)}, bf16[8,64,64]{2,1,0:T(8,128)(2,1)}, u32[]{:S(2)}) copy-start(bf16[8,64,64]{2,1,0:T(8,128)(2,1)} %transfer_ref.1) | copy-start | bytes 196612
  54.8 0.9 %copy-start.13 = (bf16[4,64,64]{2,1,0:T(8,128)(2,1)S(1)}, bf16[4,64,64]{2,1,0:T(8,128)(2,1)}, u32[]{:S(2)}) copy-start(bf16[4,64,64]{2,1,0:T(8,128)(2,1)} %coarse_ref.1) | copy-start | bytes 98308
  55.8 6.5 %copy-start.6 = (s32[1024,108]{0,1:T(8,128)S(1)}, s32[1024,108]{0,1:T(8,128)}, u32[]{:S(2)}) copy-start(s32[1024,108]{0,1:T(8,128)} %param.13) | copy-start | bytes 1327108
  55.8 6.5 %copy-start.8 = (bf16[9,128,128]{2,1,0:T(8,128)(2,1)S(1)}, bf16[9,128,128]{2,1,0:T(8,128)(2,1)}, u32[]{:S(2)}) copy-start(bf16[9,128,128]{2,1,0:T(8,128)(2,1)} %get-tuple-element.27.odd_ref) | copy-start | bytes 884740
  55.8 6.5 %copy-start.9 = (bf16[8,128,128]{2,1,0:T(8,128)(2,1)S(1)}, bf16[8,128,128]{2,1,0:T(8,128)(2,1)}, u32[]{:S(2)}) copy-start(bf16[8,128,128]{2,1,0:T(8,128)(2,1)} %get-tuple-element.26.whole_ref) | copy-start | bytes 786436
  62.3 16.2 %copy-start.4 = (f32[8,256,256]{2,1,0:T(8,128)S(1)}, f32[8,256,256]{2,1,0:T(8,128)}, u32[]{:S(2)}) copy-start(f32[8,256,256]{2,1,0:T(8,128)} %copy-done.3) | copy-start | bytes 6291460
  62.4 16.2 %copy-start.7 = (bf16[64,256]{1,0:T(8,128)(2,1)S(1)}, bf16[64,256]{1,0:T(8,128)(2,1)}, u32[]{:S(2)}) copy-start(bf16[64,256]{1,0:T(8,128)(2,1)} %basis_ref.3) | copy-start | bytes 98308
  76.5 1.4 %collective-permute-start.7 = (bf16[64,1024]{1,0:T(8,128)(2,1)S(1)}, bf16[64,1024]{1,0:T(8,128)(2,1)S(1)}, u32[]{:S(2)}, u32[]{:S(2)}) collective-permute-start(bf16[64,1024]{1,0:T(8,128)(2,1)S(1)} %get-tuple-element.32), channel_id=1, source_target_pairs={{0,1},{1,0},{2,3},{3,2},{4,5},{5,4},{6,7},{7,6},{8,9},{9,8},{10,11... | collective-permute-start | bytes 393224 | tf_op jit(solution)/shard_map/ppermute | solution.py:598
  77.9 5.6 %collective-permute-start.8 = (bf16[64,1024]{1,0:T(8,128)(2,1)S(1)}, bf16[64,1024]{1,0:T(8,128)(2,1)S(1)}, u32[]{:S(2)}, u32[]{:S(2)}) collective-permute-start(bf16[64,1024]{1,0:T(8,128)(2,1)S(1)} %add.7.total_ref), channel_id=1, source_target_pairs={{0,2},{1,3},{2,0},{3,1},{4,6},{5,7},{6,4},{7,5},{8,10},{9,11},{10,... | collective-permute-start | bytes 393224 | tf_op jit(solution)/shard_map/ppermute | solution.py:598
  78.6 5.0 %copy-start = (f32[2,1024,256]{2,1,0:T(8,128)S(1)}, f32[2,1024,256]{2,1,0:T(8,128)}, u32[]{:S(2)}) copy-start(f32[2,1024,256]{2,1,0:T(8,128)} %orbitals_ref.1) | copy-start | bytes 6291460
  (5 other events, 4.4 us)

commit v6 on v5

--- a/solution.py
+++ b/solution.py
@@ -573,24 +573,27 @@
 
 
 def gap_kernel(near_ref, sum_ref, other_sum_ref, coeffs_ref, basis_ref, out_ref):
-    orbits, leaves, _ = out_ref.shape
+    orbits = out_ref.shape[0]
     rank = basis_ref.shape[0]
-    batch = leaves // PAIR
+    batch = sum_ref.shape[0]
     for n in range(batch):
         lanes = slice(n * PAIR, (n + 1) * PAIR)
         pair = pl.program_id(0) * batch + n
+        rows = pl.ds(pl.multiple_of(pair * PAIR, PAIR), PAIR)
         hartree = sum_ref[n].astype(F32) + other_sum_ref[pair].astype(F32)
         for o in range(orbits):
             own = dot_tn(basis_ref[...], coeffs_ref[o * rank : (o + 1) * rank, lanes])
-            out_ref[o, lanes] = turned(hartree - near_ref[pair, :, o * PAIR : (o + 1) * PAIR] - own)
+            out_ref[o, rows] = turned(hartree - near_ref[pair, :, o * PAIR : (o + 1) * PAIR] - own)
 
 
 def final_kernel(orbitals_ref, gap_ref, total_ref, other_total_ref, basis_ref, out_ref):
     total = (total_ref[...].astype(F32) + other_total_ref[...].astype(F32)).astype(BF)
     shared = dot_tn(total, basis_ref[...])
-    for o in range(orbitals_ref.shape[0]):
-        value = orbitals_ref[o]
-        out_ref[o] = value - relax_step * (gap_ref[o] + shared) * value
+    count = out_ref.shape[1]
+    rows = pl.ds(pl.multiple_of(pl.program_id(0) * count, count), count)
+    for o in range(out_ref.shape[0]):
+        value = orbitals_ref[o, rows]
+        out_ref[o] = value - relax_step * (gap_ref[o, rows] + shared) * value
 
 
 def swap(values, axis, bit):
@@ -723,19 +726,13 @@
         grid=(1,),
         in_specs=[
             smem,
-            full((height, 128)),
-            full((height, 128)),
+            in_vmem,
+            in_vmem,
             mixed,
             mixed,
-            *[full((height, 128))] * 4,
-            full(weight.shape),
-            full(transfer.shape),
-            full(pair_transfer.shape),
-            full(coarse_coupling.shape),
-            full(far_mid.T.shape),
-            full(far_top.shape),
+            *[in_vmem] * 10,
         ],
-        out_specs=full((height, leaves)),
+        out_specs=in_vmem,
         out_shape=jax.ShapeDtypeStruct((height, leaves), F32),
         scratch_shapes=[
             pltpu.VMEM((128, 128), F32),
@@ -760,18 +757,17 @@
     )
     near_other = swap(near_chip, "orb", 2)
 
-    edge = lambda: full(from_left.shape)
     coeffs, coeff_sum = pl.pallas_call(
         functools.partial(leaf_kernel, pairs),
         grid=(pairs // 2,),
         in_specs=[
             smem,
             pl.BlockSpec((slots, 2 * PAIR), lambda i: (0, i)),
-            full(whole.shape),
-            full(odd.shape),
-            edge(),
-            edge(),
-            full(weight.shape),
+            in_vmem,
+            in_vmem,
+            in_vmem,
+            in_vmem,
+            in_vmem,
             pl.BlockSpec((height, 2 * PAIR), lambda i: (0, i)),
         ],
         out_specs=(
@@ -818,7 +814,7 @@
             pl.BlockSpec((height, batch * PAIR), lambda i: (0, i)),
             full(leaf_basis.shape),
         ],
-        out_specs=per_leaf,
+        out_specs=in_vmem,
         out_shape=jax.ShapeDtypeStruct(orbitals.shape, F32),
         compiler_params=WIDE_MEMORY,
         name="gap",
@@ -826,7 +822,7 @@
     return pl.pallas_call(
         final_kernel,
         grid=(pairs // batch,),
-        in_specs=[per_leaf, per_leaf, per_rank, per_rank, full(leaf_basis.shape)],
+        in_specs=[in_vmem, in_vmem, per_rank, per_rank, full(leaf_basis.shape)],
         out_specs=per_leaf,
         out_shape=jax.ShapeDtypeStruct(orbitals.shape, F32),
         compiler_params=WIDE_MEMORY,

time: 86.5 us -> 86.3 us (level)
  no operation moved by 1% of the time
where the time goes in v6:
time: 86.3 us; the launch traced here: 85.9 us
  Pallas kernels  49.8 us (58%)
  starting transfers between devices  13.3 us (15%)
  waiting for transfers between devices  12.2 us (14%)
  local copies, waits for them, and re-layouts  10.2 us (12%)
    pallas_call x1, Pallas kernels, shards(): pl.pallas_call(near_kernel, grid=(pairs,), in_specs=[smem, pl.BlockSpec((...  19.2 us
    pallas_call x1, Pallas kernels, shards(): pl.pallas_call(functools.partial(leaf_kernel, pairs), grid=(pairs // 2,),...  14.1 us
    unnamed x41, local copies, waits for them, and re-layouts  10.2 us
    ppermute x7, starting transfers between devices, swap(): return lax.ppermute(values, axis, [(i, i ^ bit) for i in range(count)])  7.13 us
    pallas_call x1, Pallas kernels, shards(): pl.pallas_call(functools.partial(tree_kernel, count, leaves, rank), grid=...  6.49 us
    ppermute x7, waiting for transfers between devices, swap(): return lax.ppermute(values, axis, [(i, i ^ bit) for i in range(count)])  6.45 us
    ppermute x2, starting transfers between devices, step_along(): return lax.ppermute(values, 'space', pairs)  6.2 us
    ppermute x2, waiting for transfers between devices, step_along(): return lax.ppermute(values, 'space', pairs)  5.77 us
  transfers between devices with their start and end apart: 9, of which 5 were waited for; matrix products, arithmetic and copies ran while one was open for 4% of the time, Pallas kernels for 27%

profile of v6, /device:TPU:0, one launch (start us, length us, event | category | flops | bytes accessed | tf_op | source)
XLA Modules:
  0.0 85.9 jit_solution(8319531286319553191)
XLA Ops:
  0.0 4.9 %moments.1 = (bf16[512,896]{1,0:T(8,128)(2,1)}, bf16[512,128]{1,0:T(8,128)(2,1)}, bf16[512,128]{1,0:T(8,128)(2,1)}, bf16[8,128,128]{2,1,0:T(8,128)(2,1)}, bf16[9...) custom-call(f32[2,1024,256]{2,1,0:T(8,128)} %orbitals_ref.1, ...), custom_call_target="tpu_custom_call" | custom-call | tf_op jit(solution)/shard_map/moments/pallas_call | solution.py:641
  4.9 4.9 %collective-permute-start = (bf16[512,128]{1,0:T(8,128)(2,1)}, bf16[512,128]{1,0:T(8,128)(2,1)S(1)}, u32[]{:S(2)}, u32[]{:S(2)}) collective-permute-start(bf16[512,128]{1,0:T(8,128)(2,1)} %get-tuple-element.22), channel_id=1, source_target_pairs={{0,4},{4,8},{8,12},{12,16},{16,20},{20,24},{24,28},{1,5},{5,9},{9,... | collective-permute-start | bytes 393224 | tf_op jit(solution)/shard_map/ppermute | solution.py:606
  9.9 1.3 %collective-permute-start.1 = (bf16[512,128]{1,0:T(8,128)(2,1)}, bf16[512,128]{1,0:T(8,128)(2,1)S(1)}, u32[]{:S(2)}, u32[]{:S(2)}) collective-permute-start(bf16[512,128]{1,0:T(8,128)(2,1)} %get-tuple-element.23), channel_id=1, source_target_pairs={{4,0},{8,4},{12,8},{16,12},{20,16},{24,20},{28,24},{5,1},{9,5},{13... | collective-permute-start | bytes 393224 | tf_op jit(solution)/shard_map/ppermute | solution.py:606
  11.2 1.7 %collective-permute-done.got_left_ref.left_ref = bf16[512,128]{1,0:T(8,128)(2,1)S(1)} collective-permute-done((bf16[512,128]{1,0:T(8,128)(2,1)}, bf16[512,128]{1,0:T(8,128)(2,1)S(1)}, u32[]{:S(2)}, u32[]{:S(2)}) %collective-permute-start) | collective-permute-done | bytes 131104 | tf_op jit(solution)/shard_map/ppermute | solution.py:606
  12.9 4.0 %collective-permute-done.1.got_right_ref.right_ref = bf16[512,128]{1,0:T(8,128)(2,1)S(1)} collective-permute-done((bf16[512,128]{1,0:T(8,128)(2,1)}, bf16[512,128]{1,0:T(8,128)(2,1)S(1)}, u32[]{:S(2)}, u32[]{:S(2)}) %collective-permute-start.1) | collective-permute-done | bytes 131104 | tf_op jit(solution)/shard_map/ppermute | solution.py:606
  16.9 1.2 %copy-done.1 = bf16[512,896]{1,0:T(8,128)(2,1)S(1)} copy-done((bf16[512,896]{1,0:T(8,128)(2,1)S(1)}, bf16[512,896]{1,0:T(8,128)(2,1)}, u32[]{:S(2)}) %copy-start.1) | copy-done | bytes 917528
  18.1 2.0 %copy-done.2 = bf16[27,256,256]{2,1,0:T(8,128)(2,1)S(1)} copy-done((bf16[27,256,256]{2,1,0:T(8,128)(2,1)S(1)}, bf16[27,256,256]{2,1,0:T(8,128)(2,1)}, u32[]{:S(2)}) %copy-start.2) | copy-done | bytes 3538968
  20.1 0.9 %copy-done.11 = bf16[512,128]{1,0:T(8,128)(2,1)S(1)} copy-done((bf16[512,128]{1,0:T(8,128)(2,1)S(1)}, bf16[512,128]{1,0:T(8,128)(2,1)}, u32[]{:S(2)}) %copy-start.11) | copy-done | bytes 131096
  21.0 0.9 %copy-done.12 = bf16[512,128]{1,0:T(8,128)(2,1)S(1)} copy-done((bf16[512,128]{1,0:T(8,128)(2,1)S(1)}, bf16[512,128]{1,0:T(8,128)(2,1)}, u32[]{:S(2)}) %copy-start.12) | copy-done | bytes 131096
  21.9 19.2 %near.1 = (f32[8,256,256]{2,1,0:T(8,128)S(1)}, bf16[8,256,128]{2,1,0:T(8,128)(2,1)S(1)}) custom-call(s32[1]{0:T(128)} %bitcast.place_ref, s32[27,1024]{1,0:T(8,128)S(1)} %bitcast.7, bf16[512,896]{1,0:T(8,128)(2,1)S(1)} %copy-done.1, bf16[512,896]{1,0:T(8,128)(2,1)S(1)} %copy-done.1, bf16[512,128]{1,0:T(8,128)(2,1)S(1)} %copy-done.11, ...), custom_call_target="tpu_custom_call" | custom-call | tf_op jit(solution)/shard_map/near/pallas_call | solution.py:695
  41.1 1.3 %copy-done.3 = f32[8,256,256]{2,1,0:T(8,128)} copy-done((f32[8,256,256]{2,1,0:T(8,128)}, f32[8,256,256]{2,1,0:T(8,128)S(1)}, u32[]{:S(2)}) %copy-start.3) | copy-done | bytes 2097176
  42.4 1.9 %collective-permute-done.2 = bf16[8,256,128]{2,1,0:T(8,128)(2,1)S(1)} collective-permute-done((bf16[8,256,128]{2,1,0:T(8,128)(2,1)S(1)}, bf16[8,256,128]{2,1,0:T(8,128)(2,1)S(1)}, u32[]{:S(2)}, u32[]{:S(2)}) %collective-permute-start.2) | collective-permute-done | bytes 524320 | tf_op jit(solution)/shard_map/ppermute | solution.py:601
  44.5 1.6 %collective-permute-start.3 = (bf16[8,256,128]{2,1,0:T(8,128)(2,1)S(1)}, bf16[8,256,128]{2,1,0:T(8,128)(2,1)S(1)}, u32[]{:S(2)}, u32[]{:S(2)}) collective-permute-start(bf16[8,256,128]{2,1,0:T(8,128)(2,1)S(1)} %add.6.sum_ref), channel_id=1, source_target_pairs={{0,2},{1,3},{2,0},{3,1},{4,6},{5,7},{6,4},{7,5},{8,10},{9,11},{10,... | collective-permute-start | bytes 1572872 | tf_op jit(solution)/shard_map/ppermute | solution.py:601
  46.2 4.2 %collective-permute-start.6 = (bf16[128,128]{1,0:T(8,128)(2,1)S(1)}, bf16[128,128]{1,0:T(8,128)(2,1)S(1)}, u32[]{:S(2)}, u32[]{:S(2)}) collective-permute-start(bf16[128,128]{1,0:T(8,128)(2,1)S(1)} %join.1.cube_ref), channel_id=1, source_target_pairs={{0,24},{4,28},{8,16},{12,20},{16,8},{20,12},{24,0},{28,4},{1,25},{... | collective-permute-start | bytes 98312 | tf_op jit(solution)/shard_map/ppermute | solution.py:601
  50.4 0.6 collective-permute-start.4
  51.1 3.8 %copy.12.coupling_ref = bf16[108,64,64]{2,1,0:T(8,128)(2,1)S(1)} copy(bf16[108,64,64]{0,2,1:T(8,128)(2,1)} %param.19) | data formatting | bytes 1769472 | tf_op args[8]
  54.9 0.8 widen.1.weight_ref
  55.8 6.5 %tree.1.down_ref = f32[128,1024]{1,0:T(8,128)S(1)} custom-call(s32[1]{0:T(128)} %bitcast.place_ref, bf16[128,128]{1,0:T(8,128)(2,1)S(1)} %copy-done.16, bf16[128,128]{1,0:T(8,128)(2,1)S(1)} %copy-done.17, bf16[512,128]{1,0:T(8,128)(2,1)S(1)} %collective-permute-done.got_left_ref.left_ref, ...), custom_call_target="tpu_custom_call" | custom-call | tf_op jit(solution)/shard_map/tree/pallas_call | solution.py:724
  62.4 14.1 %leaf.1 = (bf16[128,1024]{1,0:T(8,128)(2,1)S(1)}, bf16[64,1024]{1,0:T(8,128)(2,1)S(1)}) custom-call(s32[1]{0:T(128)} %bitcast.place_ref, s32[108,1024]{1,0:T(8,128)S(1)} %bitcast.6, bf16[8,128,128]{2,1,0:T(8,128)(2,1)S(1)} %copy-done.9, bf16[9,128,128]{2,1,0:T(8,128)(2,1)S(1)} %copy-done.8, bf16[512,128]{1,0:T(8,128)(2,1)S(1)} %collective-permute-done.got_left_ref.left_ref, ...), custom_call_target="tpu_custom_call" | custom-call | tf_op jit(solution)/shard_map/leaf/pallas_call | solution.py:760
  76.5 1.3 %collective-permute-done.7 = bf16[64,1024]{1,0:T(8,128)(2,1)S(1)} collective-permute-done((bf16[64,1024]{1,0:T(8,128)(2,1)S(1)}, bf16[64,1024]{1,0:T(8,128)(2,1)S(1)}, u32[]{:S(2)}, u32[]{:S(2)}) %collective-permute-start.7) | collective-permute-done | bytes 131104 | tf_op jit(solution)/shard_map/ppermute | solution.py:601
  77.9 0.7 collective-permute-start.8
  78.6 1.7 %gap.1.gap_ref = f32[2,1024,256]{2,1,0:T(8,128)S(1)} custom-call(f32[8,256,256]{2,1,0:T(8,128)S(1)} %copy-done.4, bf16[8,256,128]{2,1,0:T(8,128)(2,1)S(1)} %add.6.sum_ref, bf16[8,256,128]{2,1,0:T(8,128)(2,1)S(1)} %collective-permute-done.3.other_sum_ref, bf16[128,1024]{1,0:T(8,128)(2,1)S(1)} %get-tuple-element.31.coeffs_ref, bf16[64,256]{1,0:T(8,128)(2,1)S(1)} %copy-done.7), custom_call_target="tpu_custom_call" | custom-call | tf_op jit(solution)/shard_map/gap/pallas_call | solution.py:807
  80.3 3.2 %collective-permute-done.8.other_total_ref = bf16[64,1024]{1,0:T(8,128)(2,1)S(1)} collective-permute-done((bf16[64,1024]{1,0:T(8,128)(2,1)S(1)}, bf16[64,1024]{1,0:T(8,128)(2,1)S(1)}, u32[]{:S(2)}, u32[]{:S(2)}) %collective-permute-start.8) | collective-permute-done | bytes 131104 | tf_op jit(solution)/shard_map/ppermute | solution.py:601
  83.5 2.4 %final.1 = f32[2,1024,256]{2,1,0:T(8,128)} custom-call(f32[2,1024,256]{2,1,0:T(8,128)S(1)} %copy-done, f32[2,1024,256]{2,1,0:T(8,128)S(1)} %gap.1.gap_ref, bf16[64,1024]{1,0:T(8,128)(2,1)S(1)} %add.7.total_ref, bf16[64,1024]{1,0:T(8,128)(2,1)S(1)} %collective-permute-done.8.other_total_ref, bf16[64,256]{1,0:T(8,128)(2,1)S(1)} %copy-done.7), custom_call_target="tpu_custom_call" | custom-call | tf_op jit(solution)/shard_map/final/pallas_call | solution.py:822
  (45 shorter events, 0.5 us)
Async XLA Ops:
  0.0 16.9 %copy-start.10 = (s32[1024,27]{0,1:T(8,128)S(1)}, s32[1024,27]{0,1:T(8,128)}, u32[]{:S(2)}) copy-start(s32[1024,27]{0,1:T(8,128)} %param.12) | copy-start | bytes 331780
  4.9 8.0 %collective-permute-start = (bf16[512,128]{1,0:T(8,128)(2,1)}, bf16[512,128]{1,0:T(8,128)(2,1)S(1)}, u32[]{:S(2)}, u32[]{:S(2)}) collective-permute-start(bf16[512,128]{1,0:T(8,128)(2,1)} %get-tuple-element.22), channel_id=1, source_target_pairs={{0,4},{4,8},{8,12},{12,16},{16,20},{20,24},{24,28},{1,5},{5,9},{9,... | collective-permute-start | bytes 393224 | tf_op jit(solution)/shard_map/ppermute | solution.py:606
  9.9 7.1 %collective-permute-start.1 = (bf16[512,128]{1,0:T(8,128)(2,1)}, bf16[512,128]{1,0:T(8,128)(2,1)S(1)}, u32[]{:S(2)}, u32[]{:S(2)}) collective-permute-start(bf16[512,128]{1,0:T(8,128)(2,1)} %get-tuple-element.23), channel_id=1, source_target_pairs={{4,0},{8,4},{12,8},{16,12},{20,16},{24,20},{28,24},{5,1},{9,5},{13... | collective-permute-start | bytes 393224 | tf_op jit(solution)/shard_map/ppermute | solution.py:606
  16.9 1.2 %copy-start.1 = (bf16[512,896]{1,0:T(8,128)(2,1)S(1)}, bf16[512,896]{1,0:T(8,128)(2,1)}, u32[]{:S(2)}) copy-start(bf16[512,896]{1,0:T(8,128)(2,1)} %get-tuple-element.19.early_ref.late_ref) | copy-start | bytes 2752516
  18.1 2.0 %copy-start.2 = (bf16[27,256,256]{2,1,0:T(8,128)(2,1)S(1)}, bf16[27,256,256]{2,1,0:T(8,128)(2,1)}, u32[]{:S(2)}) copy-start(bf16[27,256,256]{2,1,0:T(8,128)(2,1)} %table_hbm.1) | copy-start | bytes 10616836
  20.1 0.9 %copy-start.11 = (bf16[512,128]{1,0:T(8,128)(2,1)S(1)}, bf16[512,128]{1,0:T(8,128)(2,1)}, u32[]{:S(2)}) copy-start(bf16[512,128]{1,0:T(8,128)(2,1)} %get-tuple-element.20.first_ref) | copy-start | bytes 393220
  21.0 0.9 %copy-start.12 = (bf16[512,128]{1,0:T(8,128)(2,1)S(1)}, bf16[512,128]{1,0:T(8,128)(2,1)}, u32[]{:S(2)}) copy-start(bf16[512,128]{1,0:T(8,128)(2,1)} %get-tuple-element.21.last_ref) | copy-start | bytes 393220
  21.9 24.1 %copy-start.18 = (bf16[128,128]{1,0:T(8,128)(2,1)S(1)}, bf16[128,128]{1,0:T(8,128)(2,1)}, u32[]{:S(2)}) copy-start(bf16[128,128]{1,0:T(8,128)(2,1)} %get-tuple-element.30.cube_ref) | copy-start | bytes 98308
  41.1 1.3 %copy-start.3 = (f32[8,256,256]{2,1,0:T(8,128)}, f32[8,256,256]{2,1,0:T(8,128)S(1)}, u32[]{:S(2)}) copy-start(f32[8,256,256]{2,1,0:T(8,128)S(1)} %get-tuple-element.24.near_ref) | copy-start | bytes 6291460
  42.4 1.9 %collective-permute-start.2 = (bf16[8,256,128]{2,1,0:T(8,128)(2,1)S(1)}, bf16[8,256,128]{2,1,0:T(8,128)(2,1)S(1)}, u32[]{:S(2)}, u32[]{:S(2)}) collective-permute-start(bf16[8,256,128]{2,1,0:T(8,128)(2,1)S(1)} %get-tuple-element.25), channel_id=1, source_target_pairs={{0,1},{1,0},{2,3},{3,2},{4,5},{5,4},{6,7},{7,6},{8,9},{9,8},{10,11... | collective-permute-start | bytes 1572872 | tf_op jit(solution)/shard_map/ppermute | solution.py:601
  44.5 34.1 %collective-permute-start.3 = (bf16[8,256,128]{2,1,0:T(8,128)(2,1)S(1)}, bf16[8,256,128]{2,1,0:T(8,128)(2,1)S(1)}, u32[]{:S(2)}, u32[]{:S(2)}) collective-permute-start(bf16[8,256,128]{2,1,0:T(8,128)(2,1)S(1)} %add.6.sum_ref), channel_id=1, source_target_pairs={{0,2},{1,3},{2,0},{3,1},{4,6},{5,7},{6,4},{7,5},{8,10},{9,11},{10,... | collective-permute-start | bytes 1572872 | tf_op jit(solution)/shard_map/ppermute | solution.py:601
  46.2 9.5 %collective-permute-start.6 = (bf16[128,128]{1,0:T(8,128)(2,1)S(1)}, bf16[128,128]{1,0:T(8,128)(2,1)S(1)}, u32[]{:S(2)}, u32[]{:S(2)}) collective-permute-start(bf16[128,128]{1,0:T(8,128)(2,1)S(1)} %join.1.cube_ref), channel_id=1, source_target_pairs={{0,24},{4,28},{8,16},{12,20},{16,8},{20,12},{24,0},{28,4},{1,25},{... | collective-permute-start | bytes 98312 | tf_op jit(solution)/shard_map/ppermute | solution.py:601
  50.4 5.3 %collective-permute-start.5 = (bf16[128,128]{1,0:T(8,128)(2,1)S(1)}, bf16[128,128]{1,0:T(8,128)(2,1)S(1)}, u32[]{:S(2)}, u32[]{:S(2)}) collective-permute-start(bf16[128,128]{1,0:T(8,128)(2,1)S(1)} %join.1.cube_ref), channel_id=1, source_target_pairs={{0,16},{4,20},{8,24},{12,28},{16,0},{20,4},{24,8},{28,12},{1,17},{... | collective-permute-start | bytes 98312 | tf_op jit(solution)/shard_map/ppermute | solution.py:601
  50.4 5.3 %collective-permute-start.4 = (bf16[128,128]{1,0:T(8,128)(2,1)S(1)}, bf16[128,128]{1,0:T(8,128)(2,1)S(1)}, u32[]{:S(2)}, u32[]{:S(2)}) collective-permute-start(bf16[128,128]{1,0:T(8,128)(2,1)S(1)} %join.1.cube_ref), channel_id=1, source_target_pairs={{0,8},{4,12},{8,0},{12,4},{16,24},{20,28},{24,16},{28,20},{1,9},{5... | collective-permute-start | bytes 98312 | tf_op jit(solution)/shard_map/ppermute | solution.py:601
  54.8 0.9 %copy-start.5 = (bf16[8,64,64]{2,1,0:T(8,128)(2,1)S(1)}, bf16[8,64,64]{2,1,0:T(8,128)(2,1)}, u32[]{:S(2)}) copy-start(bf16[8,64,64]{2,1,0:T(8,128)(2,1)} %transfer_ref.1) | copy-start | bytes 196612
  54.8 0.9 %copy-start.13 = (bf16[4,64,64]{2,1,0:T(8,128)(2,1)S(1)}, bf16[4,64,64]{2,1,0:T(8,128)(2,1)}, u32[]{:S(2)}) copy-start(bf16[4,64,64]{2,1,0:T(8,128)(2,1)} %coarse_ref.1) | copy-start | bytes 98308
  55.8 6.5 %copy-start.6 = (s32[1024,108]{0,1:T(8,128)S(1)}, s32[1024,108]{0,1:T(8,128)}, u32[]{:S(2)}) copy-start(s32[1024,108]{0,1:T(8,128)} %param.13) | copy-start | bytes 1327108
  55.8 6.5 %copy-start.8 = (bf16[9,128,128]{2,1,0:T(8,128)(2,1)S(1)}, bf16[9,128,128]{2,1,0:T(8,128)(2,1)}, u32[]{:S(2)}) copy-start(bf16[9,128,128]{2,1,0:T(8,128)(2,1)} %get-tuple-element.27.odd_ref) | copy-start | bytes 884740
  55.8 6.5 %copy-start.9 = (bf16[8,128,128]{2,1,0:T(8,128)(2,1)S(1)}, bf16[8,128,128]{2,1,0:T(8,128)(2,1)}, u32[]{:S(2)}) copy-start(bf16[8,128,128]{2,1,0:T(8,128)(2,1)} %get-tuple-element.26.whole_ref) | copy-start | bytes 786436
  62.3 16.2 %copy-start.4 = (f32[8,256,256]{2,1,0:T(8,128)S(1)}, f32[8,256,256]{2,1,0:T(8,128)}, u32[]{:S(2)}) copy-start(f32[8,256,256]{2,1,0:T(8,128)} %copy-done.3) | copy-start | bytes 6291460
  62.4 16.2 %copy-start.7 = (bf16[64,256]{1,0:T(8,128)(2,1)S(1)}, bf16[64,256]{1,0:T(8,128)(2,1)}, u32[]{:S(2)}) copy-start(bf16[64,256]{1,0:T(8,128)(2,1)} %basis_ref.3) | copy-start | bytes 98308
  76.5 1.4 %collective-permute-start.7 = (bf16[64,1024]{1,0:T(8,128)(2,1)S(1)}, bf16[64,1024]{1,0:T(8,128)(2,1)S(1)}, u32[]{:S(2)}, u32[]{:S(2)}) collective-permute-start(bf16[64,1024]{1,0:T(8,128)(2,1)S(1)} %get-tuple-element.32), channel_id=1, source_target_pairs={{0,1},{1,0},{2,3},{3,2},{4,5},{5,4},{6,7},{7,6},{8,9},{9,8},{10,11... | collective-permute-start | bytes 393224 | tf_op jit(solution)/shard_map/ppermute | solution.py:601
  77.9 5.6 %collective-permute-start.8 = (bf16[64,1024]{1,0:T(8,128)(2,1)S(1)}, bf16[64,1024]{1,0:T(8,128)(2,1)S(1)}, u32[]{:S(2)}, u32[]{:S(2)}) collective-permute-start(bf16[64,1024]{1,0:T(8,128)(2,1)S(1)} %add.7.total_ref), channel_id=1, source_target_pairs={{0,2},{1,3},{2,0},{3,1},{4,6},{5,7},{6,4},{7,5},{8,10},{9,11},{10,... | collective-permute-start | bytes 393224 | tf_op jit(solution)/shard_map/ppermute | solution.py:601
  78.6 5.0 %copy-start = (f32[2,1024,256]{2,1,0:T(8,128)S(1)}, f32[2,1024,256]{2,1,0:T(8,128)}, u32[]{:S(2)}) copy-start(f32[2,1024,256]{2,1,0:T(8,128)} %orbitals_ref.1) | copy-start | bytes 6291460
  (5 other events, 4.4 us)
